TPU v7x, 32 devices: a whole 2x2x4 slice. The times are simulated.
32 devices in a mesh: parts: 2 (over x), xline: 16 (over z, y, core).
Axes of the slice: x: 2, y: 2, z: 4, core: 2. Of those that a mesh axis runs over, the one named last changes fastest.
Arguments:
- gathers: bfloat16 [4, 96, 96, 256], P('parts', 'xline'), parts along dimension 0, may hold values from -6 to 6
- time_steps: float32 [2], replicated, may hold values from 0.3 to 0.8
- radon_op: bfloat16 [32, 2, 96, 96], P('xline'), may hold values from -0.4375 to 0.4375
Outputs:
- conditioned: bfloat16 [4, 96, 96, 256], P('parts', 'xline'), parts along dimension 0
There are 2 independent parts, one for each index of `parts`. A program takes and returns all parts, laid end to end along the dimension named above; an argument that names none is the same for every part. Nothing has to cross between parts.
All inputs are finite; a program needn't handle non-finite values.
Results may differ from a plain program's by a relative error of at most 0.0072.
Values may be sent and summed in bfloat16 or wider, within the bound.
No kernel may reach another device: no remote copies, remote signals or barrier semaphores. Data moves between devices by JAX's collectives and lax.ppermute only.
A program may use at most 128 MiB of HBM per device.

v0:
```python
import math

import jax
import jax.numpy as jnp
from jax import lax
from jax.sharding import PartitionSpec as P


def diff_depth(field):
    padded = jnp.pad(field, ((0, 0), (0, 0), (0, 0), (1, 1)))
    return 0.5 * (padded[..., 2:] - padded[..., :-2])


def box_depth(field):
    padded = jnp.pad(field, ((0, 0), (0, 0), (0, 0), (1, 1)))
    return (padded[..., :-2] + padded[..., 1:-1] + padded[..., 2:]) / 3.0


def diff_cross(field):
    return 0.5 * (field[:, 2:] - field[:, :-2])


def box_cross(field):
    return (field[:, :-2] + field[:, 1:-1] + field[:, 2:]) / 3.0


def diffuse(extended, tau_value, columns, total):
    inside = ((columns >= 0) & (columns < total)).astype(jnp.float32)[None, :, None, None]
    grad_cross = diff_cross(extended) * inside[:, 1:-1]
    grad_depth = diff_depth(extended[:, 1:-1]) * inside[:, 1:-1]
    tensor_xx = box_cross(box_depth(grad_cross * grad_cross)) * inside[:, 2:-2]
    tensor_xz = box_cross(box_depth(grad_cross * grad_depth)) * inside[:, 2:-2]
    tensor_zz = box_cross(box_depth(grad_depth * grad_depth)) * inside[:, 2:-2]
    norm_term = 1.0 + tensor_xx + tensor_zz
    inner_x = grad_cross[:, 1:-1]
    inner_z = grad_depth[:, 1:-1]
    flux_cross = inner_x - (tensor_xx * inner_x + tensor_xz * inner_z) / norm_term
    flux_depth = inner_z - (tensor_xz * inner_x + tensor_zz * inner_z) / norm_term
    change = diff_cross(flux_cross) + diff_depth(flux_depth[:, 1:-1])
    return (extended[:, 3:-3] + tau_value * change) * inside[:, 3:-3]


def forward_table(depth, bins):
    zeds = jnp.arange(depth, dtype=jnp.int32)[:, None]
    freqs = jnp.arange(bins, dtype=jnp.int32)[None, :]
    phase = (zeds * freqs % depth).astype(jnp.float32) * (2.0 * math.pi / depth)
    return jnp.concatenate([jnp.cos(phase), -jnp.sin(phase)], axis=1).astype(jnp.bfloat16)


def inverse_table(depth, bins):
    freqs = jnp.arange(bins, dtype=jnp.int32)[:, None]
    zeds = jnp.arange(depth, dtype=jnp.int32)[None, :]
    phase = (zeds * freqs % depth).astype(jnp.float32) * (2.0 * math.pi / depth)
    weight = jnp.where(freqs == 0, 1.0, 2.0).astype(jnp.float32) / depth
    return jnp.concatenate([weight * jnp.cos(phase), -weight * jnp.sin(phase)], axis=0).astype(
        jnp.bfloat16
    )


def complex_mats(operators):
    real_row = jnp.stack([operators[:, 0], -operators[:, 1]], axis=1)
    imag_row = jnp.stack([operators[:, 1], operators[:, 0]], axis=1)
    return jnp.stack([real_row, imag_row], axis=1)


def per_device(gathers, time_steps, radon_op):
    inlines, lines, offsets, depth = gathers.shape
    devices = lax.axis_size("xline")
    total = lines * devices
    bins = radon_op.shape[0] * devices
    steps_count = time_steps.shape[0]
    traces = jnp.transpose(gathers, (0, 2, 1, 3)).reshape(inlines * offsets, lines, depth)
    local_rows = lax.all_to_all(traces, "xline", split_axis=0, concat_axis=1, tiled=True)
    pair_rows = local_rows.shape[0]
    field = local_rows.astype(jnp.float32).reshape(pair_rows, total, 1, depth)
    columns = jnp.arange(-3, total + 3, dtype=jnp.int32)
    for number in range(steps_count):
        extended = jnp.pad(field, ((0, 0), (3, 3), (0, 0), (0, 0)))
        field = diffuse(extended, time_steps[number], columns, total)
    smooth = field.astype(jnp.bfloat16)
    spectrum = jnp.dot(
        smooth.reshape(-1, depth), forward_table(depth, bins), preferred_element_type=jnp.float32
    )
    spectrum = spectrum.astype(jnp.bfloat16).reshape(pair_rows, total, 2, bins)
    by_bins = lax.all_to_all(spectrum, "xline", split_axis=3, concat_axis=0, tiled=True)
    by_bins = by_bins.reshape(inlines, offsets, total, 2, radon_op.shape[0])
    mats = complex_mats(radon_op)
    done = jnp.einsum("ioxrf,fqrpo->ipxqf", by_bins, mats, preferred_element_type=jnp.float32)
    done = done.astype(jnp.bfloat16)
    back = lax.all_to_all(done, "xline", split_axis=2, concat_axis=4, tiled=True)
    filtered = jnp.transpose(back, (0, 2, 1, 3, 4))
    result = jnp.dot(
        filtered.reshape(-1, 2 * bins),
        inverse_table(depth, bins),
        preferred_element_type=jnp.float32,
    )
    return result.astype(jnp.bfloat16).reshape(inlines, lines, offsets, depth)


def solution(mesh):
    return jax.shard_map(
        per_device,
        mesh=mesh,
        in_specs=(P("parts", "xline", None, None), P(), P("xline", None, None, None)),
        out_specs=P("parts", "xline", None, None),
        check_vma=False,
    )
```

profile of v0, /device:TPU:0, one launch (start us, length us, event | category | flops | bytes accessed | tf_op | source)
XLA Modules:
  0.0 80.3 jit_solution(15486866586063491887)
XLA Ops:
  0.0 1.1 %copy.34 = bf16[2,6,96,256]{3,2,0,1:T(8,128)(2,1)S(1)} copy(bf16[2,6,96,256]{3,2,1,0:T(8,128)(2,1)} %param.3) | data formatting | bytes 1179648 | tf_op args[0]
  1.1 1.2 %copy.35 = bf16[192,6,256]{2,1,0:T(8,128)(2,1)} copy(bf16[192,6,256]{2,0,1:T(8,128)(2,1)S(1)} %bitcast.56) | data formatting | bytes 1179648 | tf_op jit(solution)/shard_map/reshape | solution.py:72
  2.3 7.4 %all-to-all-start = ((bf16[192,6,256]{2,1,0:T(8,128)(2,1)}), bf16[192,6,256]{2,1,0:T(8,128)(2,1)S(1)}, u32[]{:S(2)}, u32[]{:S(2)}) async-start(bf16[192,6,256]{2,1,0:T(8,128)(2,1)} %copy.35), calls=%async_computation | async-start | bytes 1572864 | tf_op jit(solution)/shard_map/all_to_all | solution.py:73
  12.0 16.4 %all-to-all-done = bf16[192,6,256]{2,1,0:T(8,128)(2,1)S(1)} async-done(((bf16[192,6,256]{2,1,0:T(8,128)(2,1)}), bf16[192,6,256]{2,1,0:T(8,128)(2,1)S(1)}, u32[]{:S(2)}, u32[]{:S(2)}) %all-to-all-start) | async-done | bytes 589856 | tf_op jit(solution)/shard_map/all_to_all | solution.py:73
  29.7 0.8 fusion.79
  30.8 0.7 fusion.10
  31.6 1.4 %fusion.2 = (f32[12,100,1,256]{3,1,0,2:T(8,128)S(1)}, f32[12,100,1,256]{3,1,0,2:T(8,128)S(1)}) fusion(f32[12,100,1,256]{3,1,0,2:T(8,128)S(1)} %mul.293, f32[12,100,1,256]{3,1,0,2:T(8,128)S(1)} %get-tuple-element.16), kind=kLoop, calls=%fused_computation.24 | loop fusion | flops 1843200 | bytes 4915200 | tf_op jit(solution)/shard_map/div | solution.py:16
  33.0 2.9 %divide_subtract_fusion.1 = (f32[12,98,1,256]{3,1,0,2:T(8,128)S(1)}, f32[12,98,1,256]{3,1,0,2:T(8,128)}, f32[12,98,1,256]{3,1,0,2:T(8,128)S(1)}, f32[12,98,1,256...) fusion(f32[12,100,1,256]{3,1,0,2:T(8,128)S(1)} %get-tuple-element.18, ...), kind=kLoop, calls=%fused_computation.65 | loop fusion | flops 4816896 | bytes 20472200 | tf_op jit(solution)/shard_map/sub | solution.py:37
  36.0 1.1 %copy-done.2 = f32[12,98,1,256]{3,1,0,2:T(8,128)S(1)} copy-done((f32[12,98,1,256]{3,1,0,2:T(8,128)S(1)}, f32[12,98,1,256]{3,1,0,2:T(8,128)}, u32[]{:S(2)}) %copy-start.2) | copy-done | bytes 1204248
  37.9 0.7 fusion.41
  38.6 0.7 fusion.32
  39.5 0.8 fusion.74
  40.4 0.7 fusion.13
  41.3 0.7 fusion.21
  42.8 3.0 %divide_subtract_fusion = (f32[12,98,1,256]{3,1,0,2:T(8,128)S(1)}, f32[12,98,1,256]{3,1,0,2:T(8,128)S(1)}, f32[12,98,1,256]{3,1,0,2:T(8,128)S(1)}, f32[12,98,1,2...) fusion(f32[12,100,1,256]{3,1,0,2:T(8,128)S(1)} %get-tuple-element.11, ...), kind=kLoop, calls=%fused_computation.62 | loop fusion | flops 4816896 | bytes 20472200 | tf_op jit(solution)/shard_map/sub | solution.py:37
  46.0 1.1 %copy-done = f32[12,98,1,256]{3,1,0,2:T(8,128)S(1)} copy-done((f32[12,98,1,256]{3,1,0,2:T(8,128)S(1)}, f32[12,98,1,256]{3,1,0,2:T(8,128)}, u32[]{:S(2)}) %copy-start) | copy-done | bytes 1204248
  47.5 0.7 fusion.39
  49.6 0.9 %copy.38 = bf16[12,96,2,32]{1,2,0,3:T(2,128)(2,1)} copy(bf16[12,96,2,32]{1,0,3,2:T(8,128)(2,1)S(1)} %reshape.81) | data formatting | bytes 294912 | tf_op jit(solution)/shard_map/reshape | solution.py:84
  50.5 5.4 %all-to-all-start.1 = ((bf16[12,96,2,32]{1,2,0,3:T(2,128)(2,1)}), bf16[12,96,2,32]{1,2,0,3:T(2,128)(2,1)S(1)}, u32[]{:S(2)}, u32[]{:S(2)}) async-start(bf16[12,96,2,32]{1,2,0,3:T(2,128)(2,1)} %copy.38), calls=%async_computation.1 | async-start | bytes 393216 | tf_op jit(solution)/shard_map/all_to_all | solution.py:85
  56.0 8.9 %all-to-all-done.1 = bf16[12,96,2,32]{1,2,0,3:T(2,128)(2,1)S(1)} async-done(((bf16[12,96,2,32]{1,2,0,3:T(2,128)(2,1)}), bf16[12,96,2,32]{1,2,0,3:T(2,128)(2,1)S(1)}, u32[]{:S(2)}, u32[]{:S(2)}) %all-to-all-start.1) | async-done | bytes 147488 | tf_op jit(solution)/shard_map/all_to_all | solution.py:85
  65.3 0.8 %copy.41 = bf16[2,96,96,2,2]{1,0,3,4,2:T(2,128)(2,1)} copy(bf16[2,96,96,2,2]{2,1,0,3,4:T(8,128)(2,1)S(1)} %fusion.44) | data formatting | bytes 294912 | tf_op jit(solution)/shard_map/convert_element_type | solution.py:89
  66.2 3.5 %all-to-all-start.2 = ((bf16[2,96,96,2,2]{1,0,3,4,2:T(2,128)(2,1)}), bf16[2,96,96,2,2]{1,0,3,4,2:T(2,128)(2,1)S(1)}, u32[]{:S(2)}, u32[]{:S(2)}) async-start(bf16[2,96,96,2,2]{1,0,3,4,2:T(2,128)(2,1)} %copy.41), calls=%async_computation.2 | async-start | bytes 393216 | tf_op jit(solution)/shard_map/all_to_all | solution.py:90
  69.9 8.8 %all-to-all-done.2 = bf16[2,96,96,2,2]{1,0,3,4,2:T(2,128)(2,1)S(1)} async-done(((bf16[2,96,96,2,2]{1,0,3,4,2:T(2,128)(2,1)}), bf16[2,96,96,2,2]{1,0,3,4,2:T(2,128)(2,1)S(1)}, u32[]{:S(2)}, u32[]{:S(2)}) %all-to-all-start.2) | async-done | bytes 147488 | tf_op jit(solution)/shard_map/all_to_all | solution.py:90
  79.2 1.2 %convolution_convert_fusion = bf16[1152,256]{1,0:T(8,128)(2,1)} fusion(bf16[1152,64]{0,1:T(8,128)(2,1)S(1)} %reshape.83, bf16[32,256]{1,0:T(8,128)(2,1)S(1)} %get-tuple-element.34, bf16[32,256]{1,0:T(8,128)(2,1)S(1)} %get-tuple-element.35), kind=kOutput, calls=%fused_computation | convolution fusion | flops 38109184 | bytes 770048 | tf_op jit(solution)/shard_map/dot_general | solution.py:92
  (44 shorter events, 7.7 us)
Async XLA Ops:
  1.1 8.7 %copy-start.6 = (f32[2]{0:T(128)S(1)}, f32[2]{0:T(128)}, u32[]{:S(2)}) copy-start(f32[2]{0:T(128)} %param.4) | copy-start | bytes 28
  2.3 26.1 %all-to-all-start = ((bf16[192,6,256]{2,1,0:T(8,128)(2,1)}), bf16[192,6,256]{2,1,0:T(8,128)(2,1)S(1)}, u32[]{:S(2)}, u32[]{:S(2)}) async-start(bf16[192,6,256]{2,1,0:T(8,128)(2,1)} %copy.35), calls=%async_computation | async-start | bytes 1572864 | tf_op jit(solution)/shard_map/all_to_all | solution.py:73
  35.8 1.3 %copy-start.2 = (f32[12,98,1,256]{3,1,0,2:T(8,128)S(1)}, f32[12,98,1,256]{3,1,0,2:T(8,128)}, u32[]{:S(2)}) copy-start(f32[12,98,1,256]{3,1,0,2:T(8,128)} %get-tuple-element.13) | copy-start | bytes 3612676
  35.8 1.7 %copy-start.3 = (f32[12,98,1,256]{3,1,0,2:T(8,128)S(1)}, f32[12,98,1,256]{3,1,0,2:T(8,128)}, u32[]{:S(2)}) copy-start(f32[12,98,1,256]{3,1,0,2:T(8,128)} %get-tuple-element.21) | copy-start | bytes 3612676
  35.8 2.1 %copy-start.4 = (f32[12,98,1,256]{3,1,0,2:T(8,128)S(1)}, f32[12,98,1,256]{3,1,0,2:T(8,128)}, u32[]{:S(2)}) copy-start(f32[12,98,1,256]{3,1,0,2:T(8,128)} %get-tuple-element.22) | copy-start | bytes 3612676
  45.8 1.3 %copy-start = (f32[12,98,1,256]{3,1,0,2:T(8,128)S(1)}, f32[12,98,1,256]{3,1,0,2:T(8,128)}, u32[]{:S(2)}) copy-start(f32[12,98,1,256]{3,1,0,2:T(8,128)} %get-tuple-element.19) | copy-start | bytes 3612676
  45.8 1.7 %copy-start.1 = (f32[12,98,1,256]{3,1,0,2:T(8,128)S(1)}, f32[12,98,1,256]{3,1,0,2:T(8,128)}, u32[]{:S(2)}) copy-start(f32[12,98,1,256]{3,1,0,2:T(8,128)} %get-tuple-element.20) | copy-start | bytes 3612676
  49.0 6.9 %copy-start.5 = (bf16[2,2,96,96]{3,2,1,0:T(8,128)(2,1)S(1)}, bf16[2,2,96,96]{3,2,1,0:T(8,128)(2,1)}, u32[]{:S(2)}) copy-start(bf16[2,2,96,96]{3,2,1,0:T(8,128)(2,1)} %param.5) | copy-start | bytes 221188
  50.5 14.3 %all-to-all-start.1 = ((bf16[12,96,2,32]{1,2,0,3:T(2,128)(2,1)}), bf16[12,96,2,32]{1,2,0,3:T(2,128)(2,1)S(1)}, u32[]{:S(2)}, u32[]{:S(2)}) async-start(bf16[12,96,2,32]{1,2,0,3:T(2,128)(2,1)} %copy.38), calls=%async_computation.1 | async-start | bytes 393216 | tf_op jit(solution)/shard_map/all_to_all | solution.py:85
  66.2 12.5 %all-to-all-start.2 = ((bf16[2,96,96,2,2]{1,0,3,4,2:T(2,128)(2,1)}), bf16[2,96,96,2,2]{1,0,3,4,2:T(2,128)(2,1)S(1)}, u32[]{:S(2)}, u32[]{:S(2)}) async-start(bf16[2,96,96,2,2]{1,0,3,4,2:T(2,128)(2,1)} %copy.41), calls=%async_computation.2 | async-start | bytes 393216 | tf_op jit(solution)/shard_map/all_to_all | solution.py:90
where the time goes:
time: 80.8 us; the launch traced here: 80.3 us
  waiting for transfers between devices  34 us (42%)
  starting transfers between devices  16.3 us (20%)
  other arithmetic  16.3 us (20%)
  local copies, waits for them, and re-layouts  10.4 us (13%)
  matrix products  1.73 us (2%)
  between operations  1.56 us (2%)
    all_to_all x1, waiting for transfers between devices, per_device(): lax.all_to_all(traces, 'xline', split_axis=0, concat_axis=1, tiled=True)  16.4 us
    all_to_all x1, waiting for transfers between devices, per_device(): lax.all_to_all(spectrum, 'xline', split_axis=3, concat_axis=0, tiled=True)  8.87 us
    all_to_all x1, waiting for transfers between devices, per_device(): lax.all_to_all(done, 'xline', split_axis=2, concat_axis=4, tiled=True)  8.76 us
    all_to_all x1, starting transfers between devices, per_device(): lax.all_to_all(traces, 'xline', split_axis=0, concat_axis=1, tiled=True)  7.41 us
    sub x2, other arithmetic, diffuse(): inner_x - (tensor_xx * inner_x + tensor_xz * inner_z) / norm_term  5.89 us
    all_to_all x1, starting transfers between devices, per_device(): lax.all_to_all(spectrum, 'xline', split_axis=3, concat_axis=0, tiled=True)  5.38 us
    unnamed x15, local copies, waits for them, and re-layouts  4.54 us
    div x5, other arithmetic, box_depth(): return (padded[..., :-2] + padded[..., 1:-1] + padded[..., 2:]) / 3.0  4.28 us
  transfers between devices with their start and end apart: 3, of which 3 were waited for; matrix products, arithmetic and copies ran while one was open for 1% of the time, Pallas kernels for 0%

commit v1 on v0

v1 whole, which is shorter than its diff:
```python
import functools
import math

import jax
import jax.numpy as jnp
import numpy as np
from jax import lax
from jax.experimental import pallas as pl
from jax.experimental.pallas import tpu as pltpu
from jax.sharding import PartitionSpec as P

F32 = jnp.float32
BF16 = jnp.bfloat16
ROWS = 16


def forward_table(depth, bins):
    phase = (np.arange(depth)[:, None] * np.arange(bins)[None, :] % depth).astype(np.float32)
    phase = phase * np.float32(2.0 * math.pi / depth)
    return np.concatenate([np.cos(phase), -np.sin(phase)], axis=1).astype(BF16)


def inverse_table(depth, bins):
    phase = (np.arange(bins)[:, None] * np.arange(depth)[None, :] % depth).astype(np.float32)
    phase = phase * np.float32(2.0 * math.pi / depth)
    weight = np.where(np.arange(bins)[:, None] == 0, 1.0, 2.0).astype(np.float32) / np.float32(depth)
    return np.concatenate([weight * np.cos(phase), -weight * np.sin(phase)], axis=0).astype(BF16)


def split_matrix(depth):
    half = depth // 2
    source = np.concatenate([2 * np.arange(half), 2 * np.arange(half) + 1])
    return (np.arange(depth)[:, None] == source[None, :]).astype(BF16)


def shifts(half):
    lane = lax.broadcasted_iota(jnp.int32, (ROWS, half), 1)
    first, last = lane == 0, lane == half - 1

    def before(odd):
        return jnp.where(first, 0.0, pltpu.roll(odd, 1, 1))

    def after(even):
        return jnp.where(last, 0.0, pltpu.roll(even, half - 1, 1))

    return before, after


def step_lines(load, store, low, high, quarter, gate, before, after):
    lines = {}

    def line(u):
        if u not in lines:
            lines[u] = load(u)
        return lines[u]

    grads, prods, fluxes, slopes = {}, {}, {}, {}
    for u in range(low - 2, high + 2):
        (ae, ao), (be, bo), (ce, co) = line(u - 1), line(u), line(u + 1)
        gxe, gxo = ce - ae, co - ao
        if u == -1 and gate is not None:
            gxe, gxo = gxe * gate, gxo * gate
        gze, gzo = bo - before(bo), after(be) - be
        grads[u] = gxe, gxo, gze, gzo
        prods[u] = (gxe * gxe, gxo * gxo, gxe * gze, gxo * gzo, gze * gze, gzo * gzo)
        v = u - 1
        if v - 1 in prods:
            sums = [a + b + c for a, b, c in zip(prods[v - 1], prods[v], prods[v + 1])]
            boxes = []
            for even, odd in zip(sums[0::2], sums[1::2]):
                both = even + odd
                boxes.append((both + before(odd), both + after(even)))
            gxe, gxo, gze, gzo = grads[v]
            flux = []
            for part, (gx, gz) in enumerate(((gxe, gze), (gxo, gzo))):
                sxx, sxz, szz = (box[part] for box in boxes)
                top = szz + 36.0
                inverse = 1.0 / (top + sxx)
                flux.append(((top * gx - sxz * gz) * inverse, ((sxx + 36.0) * gz - sxz * gx) * inverse))
            (fxe, fze), (fxo, fzo) = flux
            fluxes[v] = fxe, fxo
            slopes[v] = fzo - before(fzo), after(fze) - fze
        w = v - 1
        if low <= w < high:
            (fe, fo), (le, lo), (re, ro), (se, so) = line(w), fluxes[w - 1], fluxes[w + 1], slopes[w]
            fe = fe + quarter * ((re - le) + se)
            fo = fo + quarter * ((ro - lo) + so)
            if w == -1:
                fe, fo = fe * gate, fo * gate
            store(w, fe, fo)


def place_of(flip, lines):
    def place(u):
        if u < 0:
            return 0, jnp.where(flip, -1 - u, lines + u)
        if u < lines:
            return 1, jnp.where(flip, lines - 1 - u, u)
        return 2, jnp.where(flip, 2 * lines - 1 - u, u - lines)

    return place


def strips(offsets, body):
    def run(s, carry):
        body(pl.ds(pl.multiple_of(s * ROWS, ROWS), ROWS))
        return carry

    lax.fori_loop(0, offsets // ROWS, run, 0)


def split_block(block, split):
    lines, offsets, depth = block.shape
    plain = jnp.dot(block.reshape(lines * offsets, depth), split, preferred_element_type=F32)
    return plain.reshape(lines, offsets, depth)


def early_kernel(tau_ref, own_ref, mate_ref, split_ref, out_ref, field_ref):
    _, lines, offsets, depth = own_ref.shape
    share = out_ref.shape[0]
    half = depth // 2
    parity = lax.axis_index("xline") % 2
    place = place_of(parity == 1, lines)
    places = {u: place(u) for u in range(2 * lines)}
    for i in range(share):
        at = parity * share + i
        field_ref[0] = split_block(own_ref[at], split_ref[...])
        field_ref[1] = split_block(mate_ref[at], split_ref[...])

        def strip(rows, i=i):
            before, after = shifts(half)

            def load(u):
                b, spot = places[u]
                return field_ref[b - 1, spot, rows, :half], field_ref[b - 1, spot, rows, half:]

            def store(u, even, odd):
                out_ref[i, u - 3, rows, :half] = even
                out_ref[i, u - 3, rows, half:] = odd

            step_lines(load, store, 3, lines + 3, tau_ref[0] * 0.25, None, before, after)

        strips(offsets, strip)


def late_kernel(inline, start, tau_ref, halo_hbm, own_hbm, first_hbm, other_hbm, split_ref, table_ref, out_ref, halo_ref, own_ref, first_ref, field_ref, mid_ref, smooth_ref, sems):
    lines, offsets, depth = own_ref.shape
    half = depth // 2
    share = first_hbm.shape[0]
    me = lax.axis_index("xline")
    last = lax.axis_size("xline") - 1
    parity = me % 2
    gate = jnp.where((me == 0) | (me == last), 0.0, 1.0)
    mine = parity == inline // share
    place = place_of(parity == 1, lines)
    places = {u: place(u) for u in range(-lines, lines)}
    some = pl.ds(start, offsets)
    halo_copy = pltpu.make_async_copy(halo_hbm.at[0, :, some], halo_ref, sems.at[0])
    own_copy = pltpu.make_async_copy(own_hbm.at[inline, :, some], own_ref, sems.at[1])
    first_copy = pltpu.make_async_copy(first_hbm.at[inline % share, :, some], first_ref, sems.at[2])
    other_copy = pltpu.make_async_copy(other_hbm.at[inline % share, :, some], first_ref, sems.at[2])
    own_copy.start()
    halo_copy.start()
    pl.when(mine)(lambda: first_copy.start())
    pl.when(jnp.logical_not(mine))(lambda: other_copy.start())
    own_copy.wait()
    field_ref[1] = split_block(own_ref[...], split_ref[...])
    halo_copy.wait()
    field_ref[0] = split_block(halo_ref[...], split_ref[...])
    first_copy.wait()

    def strip(rows):
        before, after = shifts(half)

        def load(u):
            b, spot = places[u]
            return field_ref[b, spot, rows, :half], field_ref[b, spot, rows, half:]

        def keep(u, even, odd):
            mid_ref[u + 3, :, :half] = even
            mid_ref[u + 3, :, half:] = odd

        def fetch(u):
            if u < 3:
                return mid_ref[u + 3, :, :half], mid_ref[u + 3, :, half:]
            spot = jnp.where(mine, u - 3, lines + 2 - u)
            return first_ref[spot, rows, :half], first_ref[spot, rows, half:]

        def store(u, even, odd):
            spot = places[u][1]
            smooth_ref[spot, rows, :half] = even
            smooth_ref[spot, rows, half:] = odd

        step_lines(load, keep, -3, 3, tau_ref[0] * 0.25, gate, before, after)
        step_lines(fetch, store, 0, lines, tau_ref[1] * 0.25, gate, before, after)

    strips(offsets, strip)
    for x in range(lines):
        smooth = smooth_ref[x].astype(BF16)
        spectrum = lax.dot_general(table_ref[...], smooth, (((1,), (1,)), ((), ())), preferred_element_type=F32)
        out_ref[x] = spectrum.astype(BF16)


def radon_kernel(near, apart, *refs):
    *spec_refs, mine_ref, theirs_ref, mine_mate_ref, theirs_mate_ref, inverse_ref, out_ref, bins_ref, done_ref = refs
    lines, twice, _ = spec_refs[0].shape
    bins = twice // 2
    rows = bins_ref.shape[0] // twice
    me = lax.axis_index("xline")
    for i, spec_ref in enumerate(spec_refs):
        for x in range(lines):
            at = (i * lines + x) * twice
            bins_ref[at : at + twice, :] = spec_ref[x].astype(F32)
    held = mine_ref.shape[1]
    for ref, extra in ((mine_ref, 0), (mine_mate_ref, 1), (theirs_ref, apart), (theirs_mate_ref, 1 ^ apart)):
        for j, offset in enumerate(near):
            owner = me ^ (offset ^ extra)
            for b in range(held):
                k = owner * held + b
                real = bins_ref[pl.ds(k, rows, stride=twice), :]
                imag = bins_ref[pl.ds(bins + k, rows, stride=twice), :]
                both = jnp.concatenate([real, imag], axis=0).astype(BF16)
                by_real = lax.dot_general(both, ref[j, b, 0], (((1,), (1,)), ((), ())), preferred_element_type=F32)
                by_imag = lax.dot_general(both, ref[j, b, 1], (((1,), (1,)), ((), ())), preferred_element_type=F32)
                done_ref[pl.ds(k, rows, stride=twice), :] = by_real[:rows] - by_imag[rows:]
                done_ref[pl.ds(bins + k, rows, stride=twice), :] = by_imag[:rows] + by_real[rows:]
    for i in range(len(spec_refs)):
        for x in range(lines):
            at = (i * lines + x) * twice
            filtered = done_ref[at : at + twice, :].astype(BF16)
            result = lax.dot_general(filtered, inverse_ref[...], (((0,), (0,)), ((), ())), preferred_element_type=F32)
            out_ref[i, x] = result.astype(BF16)


def swapped(gathers, time_steps, radon_op):
    inlines, lines, offsets, depth = gathers.shape
    devices = lax.axis_size("xline")
    held = radon_op.shape[0]
    bins = held * devices
    apart = 4
    near = tuple(o for o in range(0, devices, 2) if not o & apart)

    def swap(value, mask):
        return lax.ppermute(value, "xline", [(i, i ^ mask) for i in range(devices)])

    cross = [(i, i + 1) for i in range(1, devices - 1, 2)] + [(i + 1, i) for i in range(1, devices - 1, 2)]
    pieces = [radon_op]
    for o in reversed(near[1:]):
        pieces.append(swap(radon_op, o))
    pieces = [pieces[0]] + pieces[:0:-1]
    mate = swap(gathers, 1)
    halos = []
    for i in range(inlines):
        halos.append(lax.ppermute(gathers[i : i + 1], "xline", cross))
    mine = jnp.stack(pieces)
    theirs = swap(mine, apart)
    mine_mate = swap(mine, 1)
    theirs_mate = swap(theirs, 1)

    vmem = pl.BlockSpec(memory_space=pltpu.VMEM)
    smem = pl.BlockSpec(memory_space=pltpu.SMEM)
    table = forward_table(depth, bins)
    table = np.concatenate([table[0::2], table[1::2]], axis=0).T
    split = jnp.asarray(split_matrix(depth))
    any_space = pl.BlockSpec(memory_space=pltpu.HBM)
    share = inlines // 2
    first = pl.pallas_call(
        early_kernel,
        out_shape=jax.ShapeDtypeStruct((share, lines, offsets, depth), F32),
        in_specs=[smem] + [vmem] * 3,
        out_specs=vmem,
        scratch_shapes=[pltpu.VMEM((2, lines, offsets, depth), F32)],
        cost_estimate=pl.CostEstimate(flops=3_000_000_000, bytes_accessed=0, transcendentals=0),
        name="early",
    )(time_steps, gathers, mate, split)
    other = swap(first, 1)
    spectra = []
    half = offsets
    starts = (0,)
    for i in range(inlines):
        for start in starts:
            spectra.append(
                pl.pallas_call(
                    functools.partial(late_kernel, i, start),
                    out_shape=jax.ShapeDtypeStruct((lines, 2 * bins, half), BF16),
                    in_specs=[smem] + [any_space] * 4 + [vmem] * 2,
                    out_specs=vmem,
                    scratch_shapes=[
                        pltpu.VMEM((lines, half, depth), BF16),
                        pltpu.VMEM((lines, half, depth), BF16),
                        pltpu.VMEM((lines, half, depth), F32),
                        pltpu.VMEM((2, lines, half, depth), F32),
                        pltpu.VMEM((6, ROWS, depth), F32),
                        pltpu.VMEM((lines, half, depth), F32),
                        pltpu.SemaphoreType.DMA((3,)),
                    ],
                    cost_estimate=pl.CostEstimate(flops=3_000_000_000, bytes_accessed=0, transcendentals=0),
                )(time_steps, halos[i], gathers, first, other, split, jnp.asarray(table))
            )
    rows = -(-inlines * lines // 16) * 16
    return pl.pallas_call(
        functools.partial(radon_kernel, near, apart),
        out_shape=jax.ShapeDtypeStruct((inlines, lines, offsets, depth), BF16),
        in_specs=[vmem] * (len(spectra) + 5),
        out_specs=vmem,
        scratch_shapes=[
            pltpu.VMEM((rows * 2 * bins, offsets), F32),
            pltpu.VMEM((rows * 2 * bins, offsets), F32),
        ],
        cost_estimate=pl.CostEstimate(flops=int(4e-6 * 1.0e15), bytes_accessed=0, transcendentals=0),
        name="radon",
    )(*spectra, mine, theirs, mine_mate, theirs_mate, jnp.asarray(inverse_table(depth, bins)))


def solution(mesh):
    return jax.shard_map(
        swapped,
        mesh=mesh,
        in_specs=(P("parts", "xline", None, None), P(), P("xline", None, None, None)),
        out_specs=P("parts", "xline", None, None),
        check_vma=False,
    )
```

time: 80.8 us -> 52.9 us (0.65)
  the two profiles are of different devices: /device:TPU:0 before, /device:TPU:17 now
where the time goes in v1:
time: 52.9 us; the launch traced here: 52.7 us
  Pallas kernels  23.2 us (44%)
  starting transfers between devices  18.3 us (35%)
  waiting for transfers between devices  6.38 us (12%)
  local copies, waits for them, and re-layouts  4.59 us (9%)
    pallas_call x2, Pallas kernels, swapped(): pl.pallas_call(functools.partial(late_kernel, i, start), out_shape=jax.Sh...  15.2 us
    ppermute x8, starting transfers between devices, swap(): return lax.ppermute(value, 'xline', [(i, i ^ mask) for i in range(devices)])  12.6 us
    ppermute x2, starting transfers between devices, swapped(): halos.append(lax.ppermute(gathers[i:i + 1], 'xline', cross))  5.69 us
    unnamed x20, local copies, waits for them, and re-layouts  4.55 us
    ppermute x2, waiting for transfers between devices, swapped(): halos.append(lax.ppermute(gathers[i:i + 1], 'xline', cross))  4.42 us
    pallas_call x1, Pallas kernels, swapped(): pl.pallas_call(early_kernel, out_shape=jax.ShapeDtypeStruct((share, lines...  4.24 us
    pallas_call x1, Pallas kernels, swapped(): pl.pallas_call(functools.partial(radon_kernel, near, apart), out_shape=ja...  3.75 us
    ppermute x8, waiting for transfers between devices, swap(): return lax.ppermute(value, 'xline', [(i, i ^ mask) for i in range(devices)])  1.95 us
  transfers between devices with their start and end apart: 10, of which 3 were waited for; matrix products, arithmetic and copies ran while one was open for 0% of the time, Pallas kernels for 37%

profile of v1, /device:TPU:17, one launch (start us, length us, event | category | flops | bytes accessed | tf_op | source)
XLA Modules:
  0.0 52.7 jit_solution(17272951461848058884)
XLA Ops:
  0.0 0.7 %collective-permute-start.1 = (bf16[2,6,96,256]{3,2,1,0:T(8,128)(2,1)}, bf16[2,6,96,256]{3,2,1,0:T(8,128)(2,1)S(1)}, u32[]{:S(2)}, u32[]{:S(2)}) collective-permute-start(bf16[2,6,96,256]{3,2,1,0:T(8,128)(2,1)} %own_hbm.3), channel_id=1, source_target_pairs={{0,1},{1,0},{2,3},{3,2},{4,5},{5,4},{6,7},{7,6},{8,9},{9,8},{10,11... | collective-permute-start | bytes 1769480 | tf_op jit(solution)/shard_map/ppermute | solution.py:244
  0.7 1.2 %collective-permute-start.4 = (bf16[2,2,96,96]{3,2,1,0:T(8,128)(2,1)}, bf16[2,2,96,96]{3,2,1,0:T(8,128)(2,1)S(1)}, u32[]{:S(2)}, u32[]{:S(2)}) collective-permute-start(bf16[2,2,96,96]{3,2,1,0:T(8,128)(2,1)} %param.8), channel_id=1, source_target_pairs={{0,2},{1,3},{2,0},{3,1},{4,6},{5,7},{6,4},{7,5},{8,10},{9,11},{10,... | collective-permute-start | bytes 221192 | tf_op jit(solution)/shard_map/ppermute | solution.py:244
  1.9 0.1 collective-permute-start.5
  2.0 2.3 %collective-permute-start.6 = (bf16[2,2,96,96]{3,2,1,0:T(8,128)(2,1)}, bf16[2,2,96,96]{3,2,1,0:T(8,128)(2,1)S(1)}, u32[]{:S(2)}, u32[]{:S(2)}) collective-permute-start(bf16[2,2,96,96]{3,2,1,0:T(8,128)(2,1)} %param.8), channel_id=1, source_target_pairs={{0,10},{1,11},{2,8},{3,9},{4,14},{5,15},{6,12},{7,13},{8,2},{9,3},... | collective-permute-start | bytes 221192 | tf_op jit(solution)/shard_map/ppermute | solution.py:244
  4.2 0.8 %copy-done.4 = bf16[2,6,96,256]{3,2,1,0:T(8,128)(2,1)} copy-done((bf16[2,6,96,256]{3,2,1,0:T(8,128)(2,1)}, bf16[2,6,96,256]{3,2,1,0:T(8,128)(2,1)S(1)}, u32[]{:S(2)}) %copy-start.4) | copy-done | bytes 589848
  5.0 4.2 %early.1.first_hbm = f32[1,6,96,256]{3,2,1,0:T(8,128)} custom-call(f32[2]{0:T(128)} %tau_ref.5, bf16[2,6,96,256]{3,2,1,0:T(8,128)(2,1)} %own_hbm.3, bf16[2,6,96,256]{3,2,1,0:T(8,128)(2,1)} %copy-done.4, bf16[256,256]{1,0:T(8,128)(2,1)} %constant.6.clone.split_ref), custom_call_target="tpu_custom_call" | custom-call | flops 3000000000 | tf_op jit(solution)/shard_map/early/pallas_call | solution.py:267
  9.3 0.9 %collective-permute-start.2 = (f32[1,6,96,256]{3,2,1,0:T(8,128)}, f32[1,6,96,256]{3,2,1,0:T(8,128)S(1)}, u32[]{:S(2)}, u32[]{:S(2)}) collective-permute-start(f32[1,6,96,256]{3,2,1,0:T(8,128)} %early.1.first_hbm), channel_id=1, source_target_pairs={{0,1},{1,0},{2,3},{3,2},{4,5},{5,4},{6,7},{7,6},{8,9},{9,8},{10,11... | collective-permute-start | bytes 1769480 | tf_op jit(solution)/shard_map/ppermute | solution.py:244
  10.3 0.2 collective-permute-done.6
  10.5 0.1 pad_maximum_fusion.refs_2_
  10.6 4.8 %collective-permute-start.7 = (bf16[4,2,2,96,96]{4,3,2,1,0:T(8,128)(2,1)S(1)}, bf16[4,2,2,96,96]{4,3,2,1,0:T(8,128)(2,1)S(1)}, u32[]{:S(2)}, u32[]{:S(2)}) collective-permute-start(bf16[4,2,2,96,96]{4,3,2,1,0:T(8,128)(2,1)S(1)} %pad_maximum_fusion.refs_2_), channel_id=1, source_target_pairs={{0,4},{1,5},{2,6},{3,7},{4,0},{5,1},{6,2},{7,3},{8,12},{9,13},{10,... | collective-permute-start | bytes 884744 | tf_op jit(solution)/shard_map/ppermute | solution.py:244
  15.4 3.8 %collective-permute-start.3 = (bf16[1,6,96,256]{3,2,1,0:T(8,128)(2,1)S(1)}, bf16[1,6,96,256]{3,2,1,0:T(8,128)(2,1)S(1)}, u32[]{:S(2)}, u32[]{:S(2)}) collective-permute-start(bf16[1,6,96,256]{3,2,1,0:T(8,128)(2,1)S(1)} %get-tuple-element.5), channel_id=1, source_target_pairs={{1,2},{3,4},{5,6},{7,8},{9,10},{11,12},{13,14},{2,1},{4,3},{6,5},{... | collective-permute-start | bytes 884744 | tf_op jit(solution)/shard_map/ppermute | solution.py:254
  19.2 1.9 %collective-permute-start = (bf16[1,6,96,256]{3,2,1,0:T(8,128)(2,1)S(1)}, bf16[1,6,96,256]{3,2,1,0:T(8,128)(2,1)S(1)}, u32[]{:S(2)}, u32[]{:S(2)}) collective-permute-start(bf16[1,6,96,256]{3,2,1,0:T(8,128)(2,1)S(1)} %get-tuple-element.6), channel_id=1, source_target_pairs={{1,2},{3,4},{5,6},{7,8},{9,10},{11,12},{13,14},{2,1},{4,3},{6,5},{... | collective-permute-start | bytes 884744 | tf_op jit(solution)/shard_map/ppermute | solution.py:254
  21.1 1.6 %collective-permute-start.8 = (bf16[4,2,2,96,96]{4,3,2,1,0:T(8,128)(2,1)S(1)}, bf16[4,2,2,96,96]{4,3,2,1,0:T(8,128)(2,1)S(1)}, u32[]{:S(2)}, u32[]{:S(2)}) collective-permute-start(bf16[4,2,2,96,96]{4,3,2,1,0:T(8,128)(2,1)S(1)} %pad_maximum_fusion.refs_2_), channel_id=1, source_target_pairs={{0,1},{1,0},{2,3},{3,2},{4,5},{5,4},{6,7},{7,6},{8,9},{9,8},{10,11... | collective-permute-start | bytes 884744 | tf_op jit(solution)/shard_map/ppermute | solution.py:244
  22.7 1.7 %collective-permute-done.7.refs_3_ = bf16[4,2,2,96,96]{4,3,2,1,0:T(8,128)(2,1)S(1)} collective-permute-done((bf16[4,2,2,96,96]{4,3,2,1,0:T(8,128)(2,1)S(1)}, bf16[4,2,2,96,96]{4,3,2,1,0:T(8,128)(2,1)S(1)}, u32[]{:S(2)}, u32[]{:S(2)}) %collective-permute-start.7) | collective-permute-done | bytes 294944 | tf_op jit(solution)/shard_map/ppermute | solution.py:244
  24.4 1.0 %collective-permute-start.9 = (bf16[4,2,2,96,96]{4,3,2,1,0:T(8,128)(2,1)S(1)}, bf16[4,2,2,96,96]{4,3,2,1,0:T(8,128)(2,1)S(1)}, u32[]{:S(2)}, u32[]{:S(2)}) collective-permute-start(bf16[4,2,2,96,96]{4,3,2,1,0:T(8,128)(2,1)S(1)} %collective-permute-done.7.refs_3_), channel_id=1, source_target_pairs={{0,1},{1,0},{2,3},{3,2},{4,5},{5,4},{6,7},{7,6},{8,9},{9,8},{10,11... | collective-permute-start | bytes 884744 | tf_op jit(solution)/shard_map/ppermute | solution.py:244
  25.5 4.4 %collective-permute-done.3.halo_hbm = bf16[1,6,96,256]{3,2,1,0:T(8,128)(2,1)S(1)} collective-permute-done((bf16[1,6,96,256]{3,2,1,0:T(8,128)(2,1)S(1)}, bf16[1,6,96,256]{3,2,1,0:T(8,128)(2,1)S(1)}, u32[]{:S(2)}, u32[]{:S(2)}) %collective-permute-start.3) | collective-permute-done | bytes 294944 | tf_op jit(solution)/shard_map/ppermute | solution.py:254
  29.9 0.7 %copy-done.9 = bf16[1,6,96,256]{3,2,1,0:T(8,128)(2,1)} copy-done((bf16[1,6,96,256]{3,2,1,0:T(8,128)(2,1)}, bf16[1,6,96,256]{3,2,1,0:T(8,128)(2,1)S(1)}, u32[]{:S(2)}) %copy-start.9) | copy-done | bytes 294936
  30.6 0.8 %copy-done.3 = f32[1,6,96,256]{3,2,1,0:T(8,128)} copy-done((f32[1,6,96,256]{3,2,1,0:T(8,128)}, f32[1,6,96,256]{3,2,1,0:T(8,128)S(1)}, u32[]{:S(2)}) %copy-start.3) | copy-done | bytes 589848
  31.4 7.6 %shard_map.65.refs_1_ = bf16[6,64,96]{2,1,0:T(8,128)(2,1)} custom-call(f32[2]{0:T(128)} %tau_ref.5, bf16[1,6,96,256]{3,2,1,0:T(8,128)(2,1)} %copy-done.9, bf16[2,6,96,256]{3,2,1,0:T(8,128)(2,1)} %own_hbm.3, f32[1,6,96,256]{3,2,1,0:T(8,128)} %early.1.first_hbm, f32[1,6,96,256]{3,2,1,0:T(8,128)} %copy-done.3, bf16[256,256]{1,0:T(8,128)(2,1)} %constant.6.clone.split_ref, ...), custom_call_target="tpu_custom_call" | custom-call | flops 3000000000 | tf_op jit(solution)/shard_map/pallas_call | solution.py:283
  39.1 0.7 %copy-done.8 = bf16[1,6,96,256]{3,2,1,0:T(8,128)(2,1)} copy-done((bf16[1,6,96,256]{3,2,1,0:T(8,128)(2,1)}, bf16[1,6,96,256]{3,2,1,0:T(8,128)(2,1)S(1)}, u32[]{:S(2)}) %copy-start.8) | copy-done | bytes 294936
  39.8 7.6 %shard_map.64.refs_0_ = bf16[6,64,96]{2,1,0:T(8,128)(2,1)} custom-call(f32[2]{0:T(128)} %tau_ref.5, bf16[1,6,96,256]{3,2,1,0:T(8,128)(2,1)} %copy-done.8, bf16[2,6,96,256]{3,2,1,0:T(8,128)(2,1)} %own_hbm.3, f32[1,6,96,256]{3,2,1,0:T(8,128)} %early.1.first_hbm, f32[1,6,96,256]{3,2,1,0:T(8,128)} %copy-done.3, bf16[256,256]{1,0:T(8,128)(2,1)} %constant.6.clone.split_ref, ...), custom_call_target="tpu_custom_call" | custom-call | flops 3000000000 | tf_op jit(solution)/shard_map/pallas_call | solution.py:283
  47.4 0.7 %copy-done.6 = bf16[4,2,2,96,96]{4,3,2,1,0:T(8,128)(2,1)} copy-done((bf16[4,2,2,96,96]{4,3,2,1,0:T(8,128)(2,1)}, bf16[4,2,2,96,96]{4,3,2,1,0:T(8,128)(2,1)S(1)}, u32[]{:S(2)}) %copy-start.6) | copy-done | bytes 294936
  48.2 0.7 %copy-done.7 = bf16[4,2,2,96,96]{4,3,2,1,0:T(8,128)(2,1)} copy-done((bf16[4,2,2,96,96]{4,3,2,1,0:T(8,128)(2,1)}, bf16[4,2,2,96,96]{4,3,2,1,0:T(8,128)(2,1)S(1)}, u32[]{:S(2)}) %copy-start.7) | copy-done | bytes 294936
  48.9 3.8 %radon.1 = bf16[2,6,96,256]{3,2,1,0:T(8,128)(2,1)} custom-call(bf16[6,64,96]{2,1,0:T(8,128)(2,1)} %shard_map.64.refs_0_, bf16[6,64,96]{2,1,0:T(8,128)(2,1)} %shard_map.65.refs_1_, bf16[4,2,2,96,96]{4,3,2,1,0:T(8,128)(2,1)} %copy-done.1, bf16[4,2,2,96,96]{4,3,2,1,0:T(8,128)(2,1)} %copy-done.5, bf16[4,2,2,96,96]{4,3,2,1,0:T(8,128)(2,1)} %copy-done.6, ...), custom_call_target="tpu_custom_call" | custom-call | flops 4000000000 | tf_op jit(solution)/shard_map/radon/pallas_call | solution.py:301
  (22 shorter events, 0.1 us)
Async XLA Ops:
  0.0 10.2 %copy-start = (bf16[2,6,96,256]{3,2,1,0:T(8,128)(2,1)S(1)}, bf16[2,6,96,256]{3,2,1,0:T(8,128)(2,1)}, u32[]{:S(2)}) copy-start(bf16[2,6,96,256]{3,2,1,0:T(8,128)(2,1)} %own_hbm.3) | copy-start | bytes 1769476
  0.0 4.2 %collective-permute-start.1 = (bf16[2,6,96,256]{3,2,1,0:T(8,128)(2,1)}, bf16[2,6,96,256]{3,2,1,0:T(8,128)(2,1)S(1)}, u32[]{:S(2)}, u32[]{:S(2)}) collective-permute-start(bf16[2,6,96,256]{3,2,1,0:T(8,128)(2,1)} %own_hbm.3), channel_id=1, source_target_pairs={{0,1},{1,0},{2,3},{3,2},{4,5},{5,4},{6,7},{7,6},{8,9},{9,8},{10,11... | collective-permute-start | bytes 1769480 | tf_op jit(solution)/shard_map/ppermute | solution.py:244
  0.7 9.6 %collective-permute-start.4 = (bf16[2,2,96,96]{3,2,1,0:T(8,128)(2,1)}, bf16[2,2,96,96]{3,2,1,0:T(8,128)(2,1)S(1)}, u32[]{:S(2)}, u32[]{:S(2)}) collective-permute-start(bf16[2,2,96,96]{3,2,1,0:T(8,128)(2,1)} %param.8), channel_id=1, source_target_pairs={{0,2},{1,3},{2,0},{3,1},{4,6},{5,7},{6,4},{7,5},{8,10},{9,11},{10,... | collective-permute-start | bytes 221192 | tf_op jit(solution)/shard_map/ppermute | solution.py:244
  1.9 8.3 %collective-permute-start.5 = (bf16[2,2,96,96]{3,2,1,0:T(8,128)(2,1)}, bf16[2,2,96,96]{3,2,1,0:T(8,128)(2,1)S(1)}, u32[]{:S(2)}, u32[]{:S(2)}) collective-permute-start(bf16[2,2,96,96]{3,2,1,0:T(8,128)(2,1)} %param.8), channel_id=1, source_target_pairs={{0,8},{1,9},{2,10},{3,11},{4,12},{5,13},{6,14},{7,15},{8,0},{9,1},... | collective-permute-start | bytes 221192 | tf_op jit(solution)/shard_map/ppermute | solution.py:244
  2.0 8.5 %collective-permute-start.6 = (bf16[2,2,96,96]{3,2,1,0:T(8,128)(2,1)}, bf16[2,2,96,96]{3,2,1,0:T(8,128)(2,1)S(1)}, u32[]{:S(2)}, u32[]{:S(2)}) collective-permute-start(bf16[2,2,96,96]{3,2,1,0:T(8,128)(2,1)} %param.8), channel_id=1, source_target_pairs={{0,10},{1,11},{2,8},{3,9},{4,14},{5,15},{6,12},{7,13},{8,2},{9,3},... | collective-permute-start | bytes 221192 | tf_op jit(solution)/shard_map/ppermute | solution.py:244
  4.2 0.8 %copy-start.4 = (bf16[2,6,96,256]{3,2,1,0:T(8,128)(2,1)}, bf16[2,6,96,256]{3,2,1,0:T(8,128)(2,1)S(1)}, u32[]{:S(2)}) copy-start(bf16[2,6,96,256]{3,2,1,0:T(8,128)(2,1)S(1)} %collective-permute-done.1.mate_ref) | copy-start | bytes 1769476
  9.3 1.2 %copy-start.2 = (bf16[2,2,96,96]{3,2,1,0:T(8,128)(2,1)S(1)}, bf16[2,2,96,96]{3,2,1,0:T(8,128)(2,1)}, u32[]{:S(2)}) copy-start(bf16[2,2,96,96]{3,2,1,0:T(8,128)(2,1)} %param.8) | copy-start | bytes 221188
  9.3 20.6 %collective-permute-start.2 = (f32[1,6,96,256]{3,2,1,0:T(8,128)}, f32[1,6,96,256]{3,2,1,0:T(8,128)S(1)}, u32[]{:S(2)}, u32[]{:S(2)}) collective-permute-start(f32[1,6,96,256]{3,2,1,0:T(8,128)} %early.1.first_hbm), channel_id=1, source_target_pairs={{0,1},{1,0},{2,3},{3,2},{4,5},{5,4},{6,7},{7,6},{8,9},{9,8},{10,11... | collective-permute-start | bytes 1769480 | tf_op jit(solution)/shard_map/ppermute | solution.py:244
  10.6 28.5 %copy-start.1 = (bf16[4,2,2,96,96]{4,3,2,1,0:T(8,128)(2,1)}, bf16[4,2,2,96,96]{4,3,2,1,0:T(8,128)(2,1)S(1)}, u32[]{:S(2)}) copy-start(bf16[4,2,2,96,96]{4,3,2,1,0:T(8,128)(2,1)S(1)} %pad_maximum_fusion.refs_2_) | copy-start | bytes 884740
  10.6 13.8 %collective-permute-start.7 = (bf16[4,2,2,96,96]{4,3,2,1,0:T(8,128)(2,1)S(1)}, bf16[4,2,2,96,96]{4,3,2,1,0:T(8,128)(2,1)S(1)}, u32[]{:S(2)}, u32[]{:S(2)}) collective-permute-start(bf16[4,2,2,96,96]{4,3,2,1,0:T(8,128)(2,1)S(1)} %pad_maximum_fusion.refs_2_), channel_id=1, source_target_pairs={{0,4},{1,5},{2,6},{3,7},{4,0},{5,1},{6,2},{7,3},{8,12},{9,13},{10,... | collective-permute-start | bytes 884744 | tf_op jit(solution)/shard_map/ppermute | solution.py:244
  15.4 14.5 %collective-permute-start.3 = (bf16[1,6,96,256]{3,2,1,0:T(8,128)(2,1)S(1)}, bf16[1,6,96,256]{3,2,1,0:T(8,128)(2,1)S(1)}, u32[]{:S(2)}, u32[]{:S(2)}) collective-permute-start(bf16[1,6,96,256]{3,2,1,0:T(8,128)(2,1)S(1)} %get-tuple-element.5), channel_id=1, source_target_pairs={{1,2},{3,4},{5,6},{7,8},{9,10},{11,12},{13,14},{2,1},{4,3},{6,5},{... | collective-permute-start | bytes 884744 | tf_op jit(solution)/shard_map/ppermute | solution.py:254
  19.2 19.9 %collective-permute-start = (bf16[1,6,96,256]{3,2,1,0:T(8,128)(2,1)S(1)}, bf16[1,6,96,256]{3,2,1,0:T(8,128)(2,1)S(1)}, u32[]{:S(2)}, u32[]{:S(2)}) collective-permute-start(bf16[1,6,96,256]{3,2,1,0:T(8,128)(2,1)S(1)} %get-tuple-element.6), channel_id=1, source_target_pairs={{1,2},{3,4},{5,6},{7,8},{9,10},{11,12},{13,14},{2,1},{4,3},{6,5},{... | collective-permute-start | bytes 884744 | tf_op jit(solution)/shard_map/ppermute | solution.py:254
  21.1 26.3 %collective-permute-start.8 = (bf16[4,2,2,96,96]{4,3,2,1,0:T(8,128)(2,1)S(1)}, bf16[4,2,2,96,96]{4,3,2,1,0:T(8,128)(2,1)S(1)}, u32[]{:S(2)}, u32[]{:S(2)}) collective-permute-start(bf16[4,2,2,96,96]{4,3,2,1,0:T(8,128)(2,1)S(1)} %pad_maximum_fusion.refs_2_), channel_id=1, source_target_pairs={{0,1},{1,0},{2,3},{3,2},{4,5},{5,4},{6,7},{7,6},{8,9},{9,8},{10,11... | collective-permute-start | bytes 884744 | tf_op jit(solution)/shard_map/ppermute | solution.py:244
  24.4 14.6 %copy-start.5 = (bf16[4,2,2,96,96]{4,3,2,1,0:T(8,128)(2,1)}, bf16[4,2,2,96,96]{4,3,2,1,0:T(8,128)(2,1)S(1)}, u32[]{:S(2)}) copy-start(bf16[4,2,2,96,96]{4,3,2,1,0:T(8,128)(2,1)S(1)} %collective-permute-done.7.refs_3_) | copy-start | bytes 884740
  24.4 23.0 %collective-permute-start.9 = (bf16[4,2,2,96,96]{4,3,2,1,0:T(8,128)(2,1)S(1)}, bf16[4,2,2,96,96]{4,3,2,1,0:T(8,128)(2,1)S(1)}, u32[]{:S(2)}, u32[]{:S(2)}) collective-permute-start(bf16[4,2,2,96,96]{4,3,2,1,0:T(8,128)(2,1)S(1)} %collective-permute-done.7.refs_3_), channel_id=1, source_target_pairs={{0,1},{1,0},{2,3},{3,2},{4,5},{5,4},{6,7},{7,6},{8,9},{9,8},{10,11... | collective-permute-start | bytes 884744 | tf_op jit(solution)/shard_map/ppermute | solution.py:244
  29.9 0.7 %copy-start.9 = (bf16[1,6,96,256]{3,2,1,0:T(8,128)(2,1)}, bf16[1,6,96,256]{3,2,1,0:T(8,128)(2,1)S(1)}, u32[]{:S(2)}) copy-start(bf16[1,6,96,256]{3,2,1,0:T(8,128)(2,1)S(1)} %collective-permute-done.3.halo_hbm) | copy-start | bytes 884740
  30.6 0.8 %copy-start.3 = (f32[1,6,96,256]{3,2,1,0:T(8,128)}, f32[1,6,96,256]{3,2,1,0:T(8,128)S(1)}, u32[]{:S(2)}) copy-start(f32[1,6,96,256]{3,2,1,0:T(8,128)S(1)} %collective-permute-done.2.other_hbm) | copy-start | bytes 1769476
  39.1 0.7 %copy-start.8 = (bf16[1,6,96,256]{3,2,1,0:T(8,128)(2,1)}, bf16[1,6,96,256]{3,2,1,0:T(8,128)(2,1)S(1)}, u32[]{:S(2)}) copy-start(bf16[1,6,96,256]{3,2,1,0:T(8,128)(2,1)S(1)} %collective-permute-done.halo_hbm) | copy-start | bytes 884740
  47.4 0.8 %copy-start.6 = (bf16[4,2,2,96,96]{4,3,2,1,0:T(8,128)(2,1)}, bf16[4,2,2,96,96]{4,3,2,1,0:T(8,128)(2,1)S(1)}, u32[]{:S(2)}) copy-start(bf16[4,2,2,96,96]{4,3,2,1,0:T(8,128)(2,1)S(1)} %collective-permute-done.8.refs_4_) | copy-start | bytes 884740
  48.2 0.8 %copy-start.7 = (bf16[4,2,2,96,96]{4,3,2,1,0:T(8,128)(2,1)}, bf16[4,2,2,96,96]{4,3,2,1,0:T(8,128)(2,1)S(1)}, u32[]{:S(2)}) copy-start(bf16[4,2,2,96,96]{4,3,2,1,0:T(8,128)(2,1)S(1)} %collective-permute-done.9.refs_5_) | copy-start | bytes 884740

commit v2 on v1

--- a/solution.py
+++ b/solution.py
@@ -262,7 +262,7 @@
     table = forward_table(depth, bins)
     table = np.concatenate([table[0::2], table[1::2]], axis=0).T
     split = jnp.asarray(split_matrix(depth))
-    any_space = pl.BlockSpec(memory_space=pltpu.HBM)
+    any_space = pl.BlockSpec(memory_space=pl.ANY)
     share = inlines // 2
     first = pl.pallas_call(
         early_kernel,
@@ -271,6 +271,7 @@
         out_specs=vmem,
         scratch_shapes=[pltpu.VMEM((2, lines, offsets, depth), F32)],
         cost_estimate=pl.CostEstimate(flops=3_000_000_000, bytes_accessed=0, transcendentals=0),
+        compiler_params=pltpu.CompilerParams(vmem_limit_bytes=16 << 20),
         name="early",
     )(time_steps, gathers, mate, split)
     other = swap(first, 1)
@@ -295,6 +296,7 @@
                         pltpu.SemaphoreType.DMA((3,)),
                     ],
                     cost_estimate=pl.CostEstimate(flops=3_000_000_000, bytes_accessed=0, transcendentals=0),
+                    compiler_params=pltpu.CompilerParams(vmem_limit_bytes=16 << 20),
                 )(time_steps, halos[i], gathers, first, other, split, jnp.asarray(table))
             )
     rows = -(-inlines * lines // 16) * 16
@@ -308,6 +310,7 @@
             pltpu.VMEM((rows * 2 * bins, offsets), F32),
         ],
         cost_estimate=pl.CostEstimate(flops=int(4e-6 * 1.0e15), bytes_accessed=0, transcendentals=0),
+        compiler_params=pltpu.CompilerParams(vmem_limit_bytes=16 << 20),
         name="radon",
     )(*spectra, mine, theirs, mine_mate, theirs_mate, jnp.asarray(inverse_table(depth, bins)))
 

time: 52.9 us -> 44.3 us (0.84)
  the two profiles are of different devices: /device:TPU:17 before, /device:TPU:19 now
where the time goes in v2:
time: 44.3 us; the launch traced here: 44.1 us
  starting transfers between devices  18.1 us (41%)
  Pallas kernels  16.8 us (38%)
  waiting for transfers between devices  6.19 us (14%)
  local copies, waits for them, and re-layouts  2.68 us (6%)
    ppermute x8, starting transfers between devices, swap(): return lax.ppermute(value, 'xline', [(i, i ^ mask) for i in range(devices)])  12.5 us
    pallas_call x2, Pallas kernels, swapped(): pl.pallas_call(functools.partial(late_kernel, i, start), out_shape=jax.Sh...  11.8 us
    ppermute x2, starting transfers between devices, swapped(): halos.append(lax.ppermute(gathers[i:i + 1], 'xline', cross))  5.69 us
    ppermute x2, waiting for transfers between devices, swapped(): halos.append(lax.ppermute(gathers[i:i + 1], 'xline', cross))  4.42 us
    pallas_call x1, Pallas kernels, swapped(): pl.pallas_call(early_kernel, out_shape=jax.ShapeDtypeStruct((share, lines...  2.69 us
    unnamed x12, local copies, waits for them, and re-layouts  2.64 us
    pallas_call x1, Pallas kernels, swapped(): pl.pallas_call(functools.partial(radon_kernel, near, apart), out_shape=ja...  2.31 us
    ppermute x8, waiting for transfers between devices, swap(): return lax.ppermute(value, 'xline', [(i, i ^ mask) for i in range(devices)])  1.77 us
  transfers between devices with their start and end apart: 10, of which 2 were waited for; matrix products, arithmetic and copies ran while one was open for 0% of the time, Pallas kernels for 33%

profile of v2, /device:TPU:19, one launch (start us, length us, event | category | flops | bytes accessed | tf_op | source)
XLA Modules:
  0.0 44.1 jit_solution(4270753898067060574)
XLA Ops:
  0.0 0.7 %collective-permute-start.1 = (bf16[2,6,96,256]{3,2,1,0:T(8,128)(2,1)}, bf16[2,6,96,256]{3,2,1,0:T(8,128)(2,1)S(1)}, u32[]{:S(2)}, u32[]{:S(2)}) collective-permute-start(bf16[2,6,96,256]{3,2,1,0:T(8,128)(2,1)} %own_hbm.3), channel_id=1, source_target_pairs={{0,1},{1,0},{2,3},{3,2},{4,5},{5,4},{6,7},{7,6},{8,9},{9,8},{10,11... | collective-permute-start | bytes 1769480 | tf_op jit(solution)/shard_map/ppermute | solution.py:244
  0.7 1.2 %collective-permute-start.4 = (bf16[2,2,96,96]{3,2,1,0:T(8,128)(2,1)}, bf16[2,2,96,96]{3,2,1,0:T(8,128)(2,1)S(1)}, u32[]{:S(2)}, u32[]{:S(2)}) collective-permute-start(bf16[2,2,96,96]{3,2,1,0:T(8,128)(2,1)} %param.8), channel_id=1, source_target_pairs={{0,2},{1,3},{2,0},{3,1},{4,6},{5,7},{6,4},{7,5},{8,10},{9,11},{10,... | collective-permute-start | bytes 221192 | tf_op jit(solution)/shard_map/ppermute | solution.py:244
  1.9 0.1 collective-permute-start.5
  2.0 2.3 %collective-permute-start.6 = (bf16[2,2,96,96]{3,2,1,0:T(8,128)(2,1)}, bf16[2,2,96,96]{3,2,1,0:T(8,128)(2,1)S(1)}, u32[]{:S(2)}, u32[]{:S(2)}) collective-permute-start(bf16[2,2,96,96]{3,2,1,0:T(8,128)(2,1)} %param.8), channel_id=1, source_target_pairs={{0,10},{1,11},{2,8},{3,9},{4,14},{5,15},{6,12},{7,13},{8,2},{9,3},... | collective-permute-start | bytes 221192 | tf_op jit(solution)/shard_map/ppermute | solution.py:244
  4.2 1.1 %copy-done = bf16[2,6,96,256]{3,2,1,0:T(8,128)(2,1)S(1)} copy-done((bf16[2,6,96,256]{3,2,1,0:T(8,128)(2,1)S(1)}, bf16[2,6,96,256]{3,2,1,0:T(8,128)(2,1)}, u32[]{:S(2)}) %copy-start) | copy-done | bytes 589848
  5.3 0.7 %copy-done.1 = f32[2]{0:T(128)S(1)} copy-done((f32[2]{0:T(128)S(1)}, f32[2]{0:T(128)}, u32[]{:S(2)}) %copy-start.1) | copy-done | bytes 32
  6.0 0.9 %copy-done.2 = bf16[256,256]{1,0:T(8,128)(2,1)S(1)} copy-done((bf16[256,256]{1,0:T(8,128)(2,1)S(1)}, bf16[256,256]{1,0:T(8,128)(2,1)}, u32[]{:S(2)}) %copy-start.2) | copy-done | bytes 131096
  6.9 2.7 %early.1.first_hbm = f32[1,6,96,256]{3,2,1,0:T(8,128)S(1)} custom-call(f32[2]{0:T(128)S(1)} %copy-done.1, bf16[2,6,96,256]{3,2,1,0:T(8,128)(2,1)S(1)} %copy-done, bf16[2,6,96,256]{3,2,1,0:T(8,128)(2,1)S(1)} %collective-permute-done.1.mate_ref, bf16[256,256]{1,0:T(8,128)(2,1)S(1)} %copy-done.2), custom_call_target="tpu_custom_call" | custom-call | flops 3000000000 | tf_op jit(solution)/shard_map/early/pallas_call | solution.py:267
  9.6 0.0 copy-start.5
  9.6 0.9 %collective-permute-start.2 = (f32[1,6,96,256]{3,2,1,0:T(8,128)S(1)}, f32[1,6,96,256]{3,2,1,0:T(8,128)S(1)}, u32[]{:S(2)}, u32[]{:S(2)}) collective-permute-start(f32[1,6,96,256]{3,2,1,0:T(8,128)S(1)} %early.1.first_hbm), channel_id=1, source_target_pairs={{0,1},{1,0},{2,3},{3,2},{4,5},{5,4},{6,7},{7,6},{8,9},{9,8},{10,11... | collective-permute-start | bytes 1769480 | tf_op jit(solution)/shard_map/ppermute | solution.py:244
  10.5 0.0 collective-permute-done.4
  10.6 0.0 copy-start.4
  10.6 0.1 pad_maximum_fusion.refs_2_
  10.7 4.7 %collective-permute-start.7 = (bf16[4,2,2,96,96]{4,3,2,1,0:T(8,128)(2,1)S(1)}, bf16[4,2,2,96,96]{4,3,2,1,0:T(8,128)(2,1)S(1)}, u32[]{:S(2)}, u32[]{:S(2)}) collective-permute-start(bf16[4,2,2,96,96]{4,3,2,1,0:T(8,128)(2,1)S(1)} %pad_maximum_fusion.refs_2_), channel_id=1, source_target_pairs={{0,4},{1,5},{2,6},{3,7},{4,0},{5,1},{6,2},{7,3},{8,12},{9,13},{10,... | collective-permute-start | bytes 884744 | tf_op jit(solution)/shard_map/ppermute | solution.py:244
  15.4 3.8 %collective-permute-start.3 = (bf16[1,6,96,256]{3,2,1,0:T(8,128)(2,1)S(1)}, bf16[1,6,96,256]{3,2,1,0:T(8,128)(2,1)S(1)}, u32[]{:S(2)}, u32[]{:S(2)}) collective-permute-start(bf16[1,6,96,256]{3,2,1,0:T(8,128)(2,1)S(1)} %get-tuple-element.5), channel_id=1, source_target_pairs={{1,2},{3,4},{5,6},{7,8},{9,10},{11,12},{13,14},{2,1},{4,3},{6,5},{... | collective-permute-start | bytes 884744 | tf_op jit(solution)/shard_map/ppermute | solution.py:254
  19.2 1.9 %collective-permute-start = (bf16[1,6,96,256]{3,2,1,0:T(8,128)(2,1)S(1)}, bf16[1,6,96,256]{3,2,1,0:T(8,128)(2,1)S(1)}, u32[]{:S(2)}, u32[]{:S(2)}) collective-permute-start(bf16[1,6,96,256]{3,2,1,0:T(8,128)(2,1)S(1)} %get-tuple-element.6), channel_id=1, source_target_pairs={{1,2},{3,4},{5,6},{7,8},{9,10},{11,12},{13,14},{2,1},{4,3},{6,5},{... | collective-permute-start | bytes 884744 | tf_op jit(solution)/shard_map/ppermute | solution.py:254
  21.1 1.6 %collective-permute-start.8 = (bf16[4,2,2,96,96]{4,3,2,1,0:T(8,128)(2,1)S(1)}, bf16[4,2,2,96,96]{4,3,2,1,0:T(8,128)(2,1)S(1)}, u32[]{:S(2)}, u32[]{:S(2)}) collective-permute-start(bf16[4,2,2,96,96]{4,3,2,1,0:T(8,128)(2,1)S(1)} %pad_maximum_fusion.refs_2_), channel_id=1, source_target_pairs={{0,1},{1,0},{2,3},{3,2},{4,5},{5,4},{6,7},{7,6},{8,9},{9,8},{10,11... | collective-permute-start | bytes 884744 | tf_op jit(solution)/shard_map/ppermute | solution.py:244
  22.7 1.8 %collective-permute-done.7.refs_3_ = bf16[4,2,2,96,96]{4,3,2,1,0:T(8,128)(2,1)S(1)} collective-permute-done((bf16[4,2,2,96,96]{4,3,2,1,0:T(8,128)(2,1)S(1)}, bf16[4,2,2,96,96]{4,3,2,1,0:T(8,128)(2,1)S(1)}, u32[]{:S(2)}, u32[]{:S(2)}) %collective-permute-start.7) | collective-permute-done | bytes 294944 | tf_op jit(solution)/shard_map/ppermute | solution.py:244
  24.4 1.0 %collective-permute-start.9 = (bf16[4,2,2,96,96]{4,3,2,1,0:T(8,128)(2,1)S(1)}, bf16[4,2,2,96,96]{4,3,2,1,0:T(8,128)(2,1)S(1)}, u32[]{:S(2)}, u32[]{:S(2)}) collective-permute-start(bf16[4,2,2,96,96]{4,3,2,1,0:T(8,128)(2,1)S(1)} %collective-permute-done.7.refs_3_), channel_id=1, source_target_pairs={{0,1},{1,0},{2,3},{3,2},{4,5},{5,4},{6,7},{7,6},{8,9},{9,8},{10,11... | collective-permute-start | bytes 884744 | tf_op jit(solution)/shard_map/ppermute | solution.py:244
  25.5 4.4 %collective-permute-done.3.halo_hbm = bf16[1,6,96,256]{3,2,1,0:T(8,128)(2,1)S(1)} collective-permute-done((bf16[1,6,96,256]{3,2,1,0:T(8,128)(2,1)S(1)}, bf16[1,6,96,256]{3,2,1,0:T(8,128)(2,1)S(1)}, u32[]{:S(2)}, u32[]{:S(2)}) %collective-permute-start.3) | collective-permute-done | bytes 294944 | tf_op jit(solution)/shard_map/ppermute | solution.py:254
  29.9 5.9 %shard_map.65.refs_1_ = bf16[6,64,96]{2,1,0:T(8,128)(2,1)S(1)} custom-call(f32[2]{0:T(128)S(1)} %copy-done.1, bf16[1,6,96,256]{3,2,1,0:T(8,128)(2,1)S(1)} %collective-permute-done.3.halo_hbm, bf16[2,6,96,256]{3,2,1,0:T(8,128)(2,1)S(1)} %copy-done, f32[1,6,96,256]{3,2,1,0:T(8,128)S(1)} %early.1.first_hbm, ...), custom_call_target="tpu_custom_call" | custom-call | flops 3000000000 | tf_op jit(solution)/shard_map/pallas_call | solution.py:284
  35.8 0.0 copy-start.3
  35.8 5.9 %shard_map.64.refs_0_ = bf16[6,64,96]{2,1,0:T(8,128)(2,1)S(1)} custom-call(f32[2]{0:T(128)S(1)} %copy-done.1, bf16[1,6,96,256]{3,2,1,0:T(8,128)(2,1)S(1)} %collective-permute-done.halo_hbm, bf16[2,6,96,256]{3,2,1,0:T(8,128)(2,1)S(1)} %copy-done, f32[1,6,96,256]{3,2,1,0:T(8,128)S(1)} %early.1.first_hbm, ...), custom_call_target="tpu_custom_call" | custom-call | flops 3000000000 | tf_op jit(solution)/shard_map/pallas_call | solution.py:284
  41.8 2.3 %radon.1 = bf16[2,6,96,256]{3,2,1,0:T(8,128)(2,1)} custom-call(bf16[6,64,96]{2,1,0:T(8,128)(2,1)S(1)} %shard_map.64.refs_0_, bf16[6,64,96]{2,1,0:T(8,128)(2,1)S(1)} %shard_map.65.refs_1_, bf16[4,2,2,96,96]{4,3,2,1,0:T(8,128)(2,1)S(1)} %pad_maximum_fusion.refs_2_, bf16[4,2,2,96,96]{4,3,2,1,0:T(8,128)(2,1)S(1)} %collective-permute-done.7.refs_3_, ...), custom_call_target="tpu_custom_call" | custom-call | flops 4000000000 | tf_op jit(solution)/shard_map/radon/pallas_call | solution.py:303
  (14 shorter events, 0.1 us)
Async XLA Ops:
  0.0 4.2 %collective-permute-start.1 = (bf16[2,6,96,256]{3,2,1,0:T(8,128)(2,1)}, bf16[2,6,96,256]{3,2,1,0:T(8,128)(2,1)S(1)}, u32[]{:S(2)}, u32[]{:S(2)}) collective-permute-start(bf16[2,6,96,256]{3,2,1,0:T(8,128)(2,1)} %own_hbm.3), channel_id=1, source_target_pairs={{0,1},{1,0},{2,3},{3,2},{4,5},{5,4},{6,7},{7,6},{8,9},{9,8},{10,11... | collective-permute-start | bytes 1769480 | tf_op jit(solution)/shard_map/ppermute | solution.py:244
  0.7 9.8 %collective-permute-start.4 = (bf16[2,2,96,96]{3,2,1,0:T(8,128)(2,1)}, bf16[2,2,96,96]{3,2,1,0:T(8,128)(2,1)S(1)}, u32[]{:S(2)}, u32[]{:S(2)}) collective-permute-start(bf16[2,2,96,96]{3,2,1,0:T(8,128)(2,1)} %param.8), channel_id=1, source_target_pairs={{0,2},{1,3},{2,0},{3,1},{4,6},{5,7},{6,4},{7,5},{8,10},{9,11},{10,... | collective-permute-start | bytes 221192 | tf_op jit(solution)/shard_map/ppermute | solution.py:244
  1.9 8.6 %collective-permute-start.5 = (bf16[2,2,96,96]{3,2,1,0:T(8,128)(2,1)}, bf16[2,2,96,96]{3,2,1,0:T(8,128)(2,1)S(1)}, u32[]{:S(2)}, u32[]{:S(2)}) collective-permute-start(bf16[2,2,96,96]{3,2,1,0:T(8,128)(2,1)} %param.8), channel_id=1, source_target_pairs={{0,8},{1,9},{2,10},{3,11},{4,12},{5,13},{6,14},{7,15},{8,0},{9,1},... | collective-permute-start | bytes 221192 | tf_op jit(solution)/shard_map/ppermute | solution.py:244
  2.0 8.6 %collective-permute-start.6 = (bf16[2,2,96,96]{3,2,1,0:T(8,128)(2,1)}, bf16[2,2,96,96]{3,2,1,0:T(8,128)(2,1)S(1)}, u32[]{:S(2)}, u32[]{:S(2)}) collective-permute-start(bf16[2,2,96,96]{3,2,1,0:T(8,128)(2,1)} %param.8), channel_id=1, source_target_pairs={{0,10},{1,11},{2,8},{3,9},{4,14},{5,15},{6,12},{7,13},{8,2},{9,3},... | collective-permute-start | bytes 221192 | tf_op jit(solution)/shard_map/ppermute | solution.py:244
  4.2 1.1 %copy-start = (bf16[2,6,96,256]{3,2,1,0:T(8,128)(2,1)S(1)}, bf16[2,6,96,256]{3,2,1,0:T(8,128)(2,1)}, u32[]{:S(2)}) copy-start(bf16[2,6,96,256]{3,2,1,0:T(8,128)(2,1)} %own_hbm.3) | copy-start | bytes 1769476
  5.3 0.7 %copy-start.1 = (f32[2]{0:T(128)S(1)}, f32[2]{0:T(128)}, u32[]{:S(2)}) copy-start(f32[2]{0:T(128)} %tau_ref.5) | copy-start | bytes 28
  5.9 0.9 %copy-start.2 = (bf16[256,256]{1,0:T(8,128)(2,1)S(1)}, bf16[256,256]{1,0:T(8,128)(2,1)}, u32[]{:S(2)}) copy-start(bf16[256,256]{1,0:T(8,128)(2,1)} %constant.6.clone.split_ref) | copy-start | bytes 393220
  9.6 1.0 %copy-start.5 = (bf16[2,2,96,96]{3,2,1,0:T(8,128)(2,1)S(1)}, bf16[2,2,96,96]{3,2,1,0:T(8,128)(2,1)}, u32[]{:S(2)}) copy-start(bf16[2,2,96,96]{3,2,1,0:T(8,128)(2,1)} %param.8) | copy-start | bytes 221188
  9.6 20.3 %collective-permute-start.2 = (f32[1,6,96,256]{3,2,1,0:T(8,128)S(1)}, f32[1,6,96,256]{3,2,1,0:T(8,128)S(1)}, u32[]{:S(2)}, u32[]{:S(2)}) collective-permute-start(f32[1,6,96,256]{3,2,1,0:T(8,128)S(1)} %early.1.first_hbm), channel_id=1, source_target_pairs={{0,1},{1,0},{2,3},{3,2},{4,5},{5,4},{6,7},{7,6},{8,9},{9,8},{10,11... | collective-permute-start | bytes 1769480 | tf_op jit(solution)/shard_map/ppermute | solution.py:244
  10.6 19.3 %copy-start.4 = (bf16[64,256]{1,0:T(8,128)(2,1)S(1)}, bf16[64,256]{1,0:T(8,128)(2,1)}, u32[]{:S(2)}) copy-start(bf16[64,256]{1,0:T(8,128)(2,1)} %constant.7.clone.table_ref) | copy-start | bytes 98308
  10.7 13.7 %collective-permute-start.7 = (bf16[4,2,2,96,96]{4,3,2,1,0:T(8,128)(2,1)S(1)}, bf16[4,2,2,96,96]{4,3,2,1,0:T(8,128)(2,1)S(1)}, u32[]{:S(2)}, u32[]{:S(2)}) collective-permute-start(bf16[4,2,2,96,96]{4,3,2,1,0:T(8,128)(2,1)S(1)} %pad_maximum_fusion.refs_2_), channel_id=1, source_target_pairs={{0,4},{1,5},{2,6},{3,7},{4,0},{5,1},{6,2},{7,3},{8,12},{9,13},{10,... | collective-permute-start | bytes 884744 | tf_op jit(solution)/shard_map/ppermute | solution.py:244
  15.4 14.5 %collective-permute-start.3 = (bf16[1,6,96,256]{3,2,1,0:T(8,128)(2,1)S(1)}, bf16[1,6,96,256]{3,2,1,0:T(8,128)(2,1)S(1)}, u32[]{:S(2)}, u32[]{:S(2)}) collective-permute-start(bf16[1,6,96,256]{3,2,1,0:T(8,128)(2,1)S(1)} %get-tuple-element.5), channel_id=1, source_target_pairs={{1,2},{3,4},{5,6},{7,8},{9,10},{11,12},{13,14},{2,1},{4,3},{6,5},{... | collective-permute-start | bytes 884744 | tf_op jit(solution)/shard_map/ppermute | solution.py:254
  19.2 16.6 %collective-permute-start = (bf16[1,6,96,256]{3,2,1,0:T(8,128)(2,1)S(1)}, bf16[1,6,96,256]{3,2,1,0:T(8,128)(2,1)S(1)}, u32[]{:S(2)}, u32[]{:S(2)}) collective-permute-start(bf16[1,6,96,256]{3,2,1,0:T(8,128)(2,1)S(1)} %get-tuple-element.6), channel_id=1, source_target_pairs={{1,2},{3,4},{5,6},{7,8},{9,10},{11,12},{13,14},{2,1},{4,3},{6,5},{... | collective-permute-start | bytes 884744 | tf_op jit(solution)/shard_map/ppermute | solution.py:254
  21.1 20.6 %collective-permute-start.8 = (bf16[4,2,2,96,96]{4,3,2,1,0:T(8,128)(2,1)S(1)}, bf16[4,2,2,96,96]{4,3,2,1,0:T(8,128)(2,1)S(1)}, u32[]{:S(2)}, u32[]{:S(2)}) collective-permute-start(bf16[4,2,2,96,96]{4,3,2,1,0:T(8,128)(2,1)S(1)} %pad_maximum_fusion.refs_2_), channel_id=1, source_target_pairs={{0,1},{1,0},{2,3},{3,2},{4,5},{5,4},{6,7},{7,6},{8,9},{9,8},{10,11... | collective-permute-start | bytes 884744 | tf_op jit(solution)/shard_map/ppermute | solution.py:244
  24.4 17.3 %collective-permute-start.9 = (bf16[4,2,2,96,96]{4,3,2,1,0:T(8,128)(2,1)S(1)}, bf16[4,2,2,96,96]{4,3,2,1,0:T(8,128)(2,1)S(1)}, u32[]{:S(2)}, u32[]{:S(2)}) collective-permute-start(bf16[4,2,2,96,96]{4,3,2,1,0:T(8,128)(2,1)S(1)} %collective-permute-done.7.refs_3_), channel_id=1, source_target_pairs={{0,1},{1,0},{2,3},{3,2},{4,5},{5,4},{6,7},{7,6},{8,9},{9,8},{10,11... | collective-permute-start | bytes 884744 | tf_op jit(solution)/shard_map/ppermute | solution.py:244
  35.8 6.0 %copy-start.3 = (bf16[64,256]{1,0:T(8,128)(2,1)S(1)}, bf16[64,256]{1,0:T(8,128)(2,1)}, u32[]{:S(2)}) copy-start(bf16[64,256]{1,0:T(8,128)(2,1)} %constant.8.clone.refs_6_) | copy-start | bytes 98308

commit v3 on v2

--- a/solution.py
+++ b/solution.py
@@ -11,7 +11,7 @@
 
 F32 = jnp.float32
 BF16 = jnp.bfloat16
-ROWS = 16
+ROWS = 32
 
 
 def forward_table(depth, bins):
@@ -36,30 +36,31 @@
 def shifts(half):
     lane = lax.broadcasted_iota(jnp.int32, (ROWS, half), 1)
     first, last = lane == 0, lane == half - 1
+    zero = jnp.zeros((ROWS, half), BF16)
 
     def before(odd):
-        return jnp.where(first, 0.0, pltpu.roll(odd, 1, 1))
+        return jnp.where(first, zero, pltpu.roll(odd, 1, 1))
 
     def after(even):
-        return jnp.where(last, 0.0, pltpu.roll(even, half - 1, 1))
+        return jnp.where(last, zero, pltpu.roll(even, half - 1, 1))
 
     return before, after
 
 
 def step_lines(load, store, low, high, quarter, gate, before, after):
-    lines = {}
+    narrow = {}
 
     def line(u):
-        if u not in lines:
-            lines[u] = load(u)
-        return lines[u]
+        if u not in narrow:
+            narrow[u] = tuple(part.astype(BF16) for part in load(u))
+        return narrow[u]
 
     grads, prods, fluxes, slopes = {}, {}, {}, {}
     for u in range(low - 2, high + 2):
         (ae, ao), (be, bo), (ce, co) = line(u - 1), line(u), line(u + 1)
         gxe, gxo = ce - ae, co - ao
         if u == -1 and gate is not None:
-            gxe, gxo = gxe * gate, gxo * gate
+            gxe, gxo = gxe * gate.astype(BF16), gxo * gate.astype(BF16)
         gze, gzo = bo - before(bo), after(be) - be
         grads[u] = gxe, gxo, gze, gzo
         prods[u] = (gxe * gxe, gxo * gxo, gxe * gze, gxo * gzo, gze * gze, gzo * gzo)
@@ -74,18 +75,17 @@
             flux = []
             for part, (gx, gz) in enumerate(((gxe, gze), (gxo, gzo))):
                 sxx, sxz, szz = (box[part] for box in boxes)
-                top = szz + 36.0
-                inverse = 1.0 / (top + sxx)
-                flux.append(((top * gx - sxz * gz) * inverse, ((sxx + 36.0) * gz - sxz * gx) * inverse))
+                inverse = (1.0 / ((sxx + szz).astype(F32) + 36.0)).astype(BF16)
+                flux.append((gx - (sxx * gx + sxz * gz) * inverse, gz - (sxz * gx + szz * gz) * inverse))
             (fxe, fze), (fxo, fzo) = flux
-            fluxes[v] = fxe, fxo
-            slopes[v] = fzo - before(fzo), after(fze) - fze
+            fluxes[v] = fxe.astype(F32), fxo.astype(F32)
+            slopes[v] = fzo.astype(F32) - before(fzo).astype(F32), after(fze).astype(F32) - fze.astype(F32)
         w = v - 1
         if low <= w < high:
-            (fe, fo), (le, lo), (re, ro), (se, so) = line(w), fluxes[w - 1], fluxes[w + 1], slopes[w]
+            (fe, fo), (le, lo), (re, ro), (se, so) = load(w), fluxes[w - 1], fluxes[w + 1], slopes[w]
             fe = fe + quarter * ((re - le) + se)
             fo = fo + quarter * ((ro - lo) + so)
-            if w == -1:
+            if w == -1 and gate is not None:
                 fe, fo = fe * gate, fo * gate
             store(w, fe, fo)
 
@@ -113,6 +113,10 @@
     lines, offsets, depth = block.shape
     plain = jnp.dot(block.reshape(lines * offsets, depth), split, preferred_element_type=F32)
     return plain.reshape(lines, offsets, depth)
+
+
+def inline_at(parity, turn, share):
+    return jnp.where(parity == 1, (share + turn) % (2 * share), turn)
 
 
 def early_kernel(tau_ref, own_ref, mate_ref, split_ref, out_ref, field_ref):
@@ -143,7 +147,7 @@
         strips(offsets, strip)
 
 
-def late_kernel(inline, start, tau_ref, halo_hbm, own_hbm, first_hbm, other_hbm, split_ref, table_ref, out_ref, halo_ref, own_ref, first_ref, field_ref, mid_ref, smooth_ref, sems):
+def late_kernel(turn, tau_ref, halo_hbm, own_hbm, first_hbm, split_ref, table_ref, out_ref, halo_ref, own_ref, first_ref, field_ref, mid_ref, smooth_ref, sems):
     lines, offsets, depth = own_ref.shape
     half = depth // 2
     share = first_hbm.shape[0]
@@ -151,18 +155,16 @@
     last = lax.axis_size("xline") - 1
     parity = me % 2
     gate = jnp.where((me == 0) | (me == last), 0.0, 1.0)
-    mine = parity == inline // share
+    mine = turn < share
     place = place_of(parity == 1, lines)
     places = {u: place(u) for u in range(-lines, lines)}
-    some = pl.ds(start, offsets)
-    halo_copy = pltpu.make_async_copy(halo_hbm.at[0, :, some], halo_ref, sems.at[0])
-    own_copy = pltpu.make_async_copy(own_hbm.at[inline, :, some], own_ref, sems.at[1])
-    first_copy = pltpu.make_async_copy(first_hbm.at[inline % share, :, some], first_ref, sems.at[2])
-    other_copy = pltpu.make_async_copy(other_hbm.at[inline % share, :, some], first_ref, sems.at[2])
+    inline = inline_at(parity, turn, share)
+    halo_copy = pltpu.make_async_copy(halo_hbm.at[0], halo_ref, sems.at[0])
+    own_copy = pltpu.make_async_copy(own_hbm.at[inline], own_ref, sems.at[1])
+    first_copy = pltpu.make_async_copy(first_hbm.at[turn % share], first_ref, sems.at[2])
     own_copy.start()
     halo_copy.start()
-    pl.when(mine)(lambda: first_copy.start())
-    pl.when(jnp.logical_not(mine))(lambda: other_copy.start())
+    first_copy.start()
     own_copy.wait()
     field_ref[1] = split_block(own_ref[...], split_ref[...])
     halo_copy.wait()
@@ -183,7 +185,7 @@
         def fetch(u):
             if u < 3:
                 return mid_ref[u + 3, :, :half], mid_ref[u + 3, :, half:]
-            spot = jnp.where(mine, u - 3, lines + 2 - u)
+            spot = u - 3 if mine else lines + 2 - u
             return first_ref[spot, rows, :half], first_ref[spot, rows, half:]
 
         def store(u, even, odd):
@@ -225,11 +227,12 @@
                 done_ref[pl.ds(k, rows, stride=twice), :] = by_real[:rows] - by_imag[rows:]
                 done_ref[pl.ds(bins + k, rows, stride=twice), :] = by_imag[:rows] + by_real[rows:]
     for i in range(len(spec_refs)):
+        inline = inline_at(me % 2, i, len(spec_refs) // 2)
         for x in range(lines):
             at = (i * lines + x) * twice
             filtered = done_ref[at : at + twice, :].astype(BF16)
             result = lax.dot_general(filtered, inverse_ref[...], (((0,), (0,)), ((), ())), preferred_element_type=F32)
-            out_ref[i, x] = result.astype(BF16)
+            out_ref[inline, x] = result.astype(BF16)
 
 
 def swapped(gathers, time_steps, radon_op):
@@ -251,7 +254,9 @@
     mate = swap(gathers, 1)
     halos = []
     for i in range(inlines):
-        halos.append(lax.ppermute(gathers[i : i + 1], "xline", cross))
+        at = inline_at(1 - lax.axis_index("xline") % 2, i, inlines // 2)
+        sent = lax.dynamic_slice_in_dim(gathers, at, 1, axis=0)
+        halos.append(lax.ppermute(sent, "xline", cross))
     mine = jnp.stack(pieces)
     theirs = swap(mine, apart)
     mine_mate = swap(mine, 1)
@@ -276,29 +281,26 @@
     )(time_steps, gathers, mate, split)
     other = swap(first, 1)
     spectra = []
-    half = offsets
-    starts = (0,)
     for i in range(inlines):
-        for start in starts:
-            spectra.append(
-                pl.pallas_call(
-                    functools.partial(late_kernel, i, start),
-                    out_shape=jax.ShapeDtypeStruct((lines, 2 * bins, half), BF16),
-                    in_specs=[smem] + [any_space] * 4 + [vmem] * 2,
-                    out_specs=vmem,
-                    scratch_shapes=[
-                        pltpu.VMEM((lines, half, depth), BF16),
-                        pltpu.VMEM((lines, half, depth), BF16),
-                        pltpu.VMEM((lines, half, depth), F32),
-                        pltpu.VMEM((2, lines, half, depth), F32),
-                        pltpu.VMEM((6, ROWS, depth), F32),
-                        pltpu.VMEM((lines, half, depth), F32),
-                        pltpu.SemaphoreType.DMA((3,)),
-                    ],
-                    cost_estimate=pl.CostEstimate(flops=3_000_000_000, bytes_accessed=0, transcendentals=0),
-                    compiler_params=pltpu.CompilerParams(vmem_limit_bytes=16 << 20),
-                )(time_steps, halos[i], gathers, first, other, split, jnp.asarray(table))
-            )
+        spectra.append(
+            pl.pallas_call(
+                functools.partial(late_kernel, i),
+                out_shape=jax.ShapeDtypeStruct((lines, 2 * bins, offsets), BF16),
+                in_specs=[smem] + [any_space] * 3 + [vmem] * 2,
+                out_specs=vmem,
+                scratch_shapes=[
+                    pltpu.VMEM((lines, offsets, depth), BF16),
+                    pltpu.VMEM((lines, offsets, depth), BF16),
+                    pltpu.VMEM((lines, offsets, depth), F32),
+                    pltpu.VMEM((2, lines, offsets, depth), F32),
+                    pltpu.VMEM((6, ROWS, depth), F32),
+                    pltpu.VMEM((lines, offsets, depth), F32),
+                    pltpu.SemaphoreType.DMA((3,)),
+                ],
+                cost_estimate=pl.CostEstimate(flops=3_000_000_000, bytes_accessed=0, transcendentals=0),
+                compiler_params=pltpu.CompilerParams(vmem_limit_bytes=16 << 20),
+            )(time_steps, halos[i], gathers, first if i < share else other, split, jnp.asarray(table))
+        )
     rows = -(-inlines * lines // 16) * 16
     return pl.pallas_call(
         functools.partial(radon_kernel, near, apart),

time: 44.3 us -> 40.1 us (0.905)
  the two profiles are of different devices: /device:TPU:19 before, /device:TPU:17 now
where the time goes in v3:
time: 40.1 us; the launch traced here: 39.9 us
  starting transfers between devices  18.2 us (45%)
  Pallas kernels  11.7 us (29%)
  waiting for transfers between devices  8.46 us (21%)
  local copies, waits for them, and re-layouts  1.26 us (3%)
    ppermute x8, starting transfers between devices, swap(): return lax.ppermute(value, 'xline', [(i, i ^ mask) for i in range(devices)])  12.5 us
    pallas_call x2, Pallas kernels, swapped(): pl.pallas_call(functools.partial(late_kernel, i), out_shape=jax.ShapeDtyp...  7.6 us
    ppermute x2, starting transfers between devices, swapped(): halos.append(lax.ppermute(sent, 'xline', cross))  5.69 us
    ppermute x2, waiting for transfers between devices, swapped(): halos.append(lax.ppermute(sent, 'xline', cross))  4.42 us
    ppermute x8, waiting for transfers between devices, swap(): return lax.ppermute(value, 'xline', [(i, i ^ mask) for i in range(devices)])  4.04 us
    pallas_call x1, Pallas kernels, swapped(): pl.pallas_call(functools.partial(radon_kernel, near, apart), out_shape=ja...  2.32 us
    pallas_call x1, Pallas kernels, swapped(): pl.pallas_call(early_kernel, out_shape=jax.ShapeDtypeStruct((share, lines...  1.81 us
    dynamic_slice x1, local copies, waits for them, and re-layouts, swapped(): sent = lax.dynamic_slice_in_dim(gathers, at, 1, axis=0)  1.16 us
  transfers between devices with their start and end apart: 10, of which 3 were waited for; matrix products, arithmetic and copies ran while one was open for 3% of the time, Pallas kernels for 24%

profile of v3, /device:TPU:17, one launch (start us, length us, event | category | flops | bytes accessed | tf_op | source)
XLA Modules:
  0.0 39.9 jit_solution(15818489333284414445)
XLA Ops:
  0.0 0.7 %collective-permute-start.1 = (bf16[2,6,96,256]{3,2,1,0:T(8,128)(2,1)}, bf16[2,6,96,256]{3,2,1,0:T(8,128)(2,1)S(1)}, u32[]{:S(2)}, u32[]{:S(2)}) collective-permute-start(bf16[2,6,96,256]{3,2,1,0:T(8,128)(2,1)} %own_hbm.3), channel_id=1, source_target_pairs={{0,1},{1,0},{2,3},{3,2},{4,5},{5,4},{6,7},{7,6},{8,9},{9,8},{10,11... | collective-permute-start | bytes 1769480 | tf_op jit(solution)/shard_map/ppermute | solution.py:247
  0.7 1.2 %collective-permute-start.4 = (bf16[2,2,96,96]{3,2,1,0:T(8,128)(2,1)}, bf16[2,2,96,96]{3,2,1,0:T(8,128)(2,1)S(1)}, u32[]{:S(2)}, u32[]{:S(2)}) collective-permute-start(bf16[2,2,96,96]{3,2,1,0:T(8,128)(2,1)} %param.8), channel_id=1, source_target_pairs={{0,2},{1,3},{2,0},{3,1},{4,6},{5,7},{6,4},{7,5},{8,10},{9,11},{10,... | collective-permute-start | bytes 221192 | tf_op jit(solution)/shard_map/ppermute | solution.py:247
  1.9 0.1 collective-permute-start.5
  2.0 2.3 %collective-permute-start.6 = (bf16[2,2,96,96]{3,2,1,0:T(8,128)(2,1)}, bf16[2,2,96,96]{3,2,1,0:T(8,128)(2,1)S(1)}, u32[]{:S(2)}, u32[]{:S(2)}) collective-permute-start(bf16[2,2,96,96]{3,2,1,0:T(8,128)(2,1)} %param.8), channel_id=1, source_target_pairs={{0,10},{1,11},{2,8},{3,9},{4,14},{5,15},{6,12},{7,13},{8,2},{9,3},... | collective-permute-start | bytes 221192 | tf_op jit(solution)/shard_map/ppermute | solution.py:247
  4.2 1.2 %constant_dynamic-slice_fusion = (bf16[1,6,96,256]{3,2,1,0:T(8,128)(2,1)S(1)}, bf16[1,6,96,256]{3,2,1,0:T(8,128)(2,1)S(1)}) fusion(bf16[2,6,96,256]{3,2,1,0:T(8,128)(2,1)} %own_hbm.3, s32[]{:T(128)S(6)} %select_n.20, s32[]{:T(128)S(6)} %select_n.19), kind=kLoop, calls=%fused_computation.1 | loop fusion | bytes 1179656 | tf_op jit(solution)/shard_map/dynamic_slice | solution.py:258
  5.4 0.0 copy-start.5
  5.4 0.1 copy-done
  5.5 0.0 copy-done.2
  5.5 1.8 %early.1.first_hbm = f32[1,6,96,256]{3,2,1,0:T(8,128)S(1)} custom-call(f32[2]{0:T(128)S(1)} %copy-done.1, bf16[2,6,96,256]{3,2,1,0:T(8,128)(2,1)S(1)} %copy-done, bf16[2,6,96,256]{3,2,1,0:T(8,128)(2,1)S(1)} %collective-permute-done.1.mate_ref, bf16[256,256]{1,0:T(8,128)(2,1)S(1)} %copy-done.2), custom_call_target="tpu_custom_call" | custom-call | flops 3000000000 | tf_op jit(solution)/shard_map/early/pallas_call | solution.py:272
  7.3 0.9 %collective-permute-start.3 = (f32[1,6,96,256]{3,2,1,0:T(8,128)S(1)}, f32[1,6,96,256]{3,2,1,0:T(8,128)S(1)}, u32[]{:S(2)}, u32[]{:S(2)}) collective-permute-start(f32[1,6,96,256]{3,2,1,0:T(8,128)S(1)} %early.1.first_hbm), channel_id=1, source_target_pairs={{0,1},{1,0},{2,3},{3,2},{4,5},{5,4},{6,7},{7,6},{8,9},{9,8},{10,11... | collective-permute-start | bytes 1769480 | tf_op jit(solution)/shard_map/ppermute | solution.py:247
  8.2 2.3 %collective-permute-done.6 = bf16[2,2,96,96]{3,2,1,0:T(8,128)(2,1)S(1)} collective-permute-done((bf16[2,2,96,96]{3,2,1,0:T(8,128)(2,1)}, bf16[2,2,96,96]{3,2,1,0:T(8,128)(2,1)S(1)}, u32[]{:S(2)}, u32[]{:S(2)}) %collective-permute-start.6) | collective-permute-done | bytes 73760 | tf_op jit(solution)/shard_map/ppermute | solution.py:247
  10.5 0.1 pad_maximum_fusion.refs_2_
  10.6 4.8 %collective-permute-start.7 = (bf16[4,2,2,96,96]{4,3,2,1,0:T(8,128)(2,1)S(1)}, bf16[4,2,2,96,96]{4,3,2,1,0:T(8,128)(2,1)S(1)}, u32[]{:S(2)}, u32[]{:S(2)}) collective-permute-start(bf16[4,2,2,96,96]{4,3,2,1,0:T(8,128)(2,1)S(1)} %pad_maximum_fusion.refs_2_), channel_id=1, source_target_pairs={{0,4},{1,5},{2,6},{3,7},{4,0},{5,1},{6,2},{7,3},{8,12},{9,13},{10,... | collective-permute-start | bytes 884744 | tf_op jit(solution)/shard_map/ppermute | solution.py:247
  15.4 3.8 %collective-permute-start = (bf16[1,6,96,256]{3,2,1,0:T(8,128)(2,1)S(1)}, bf16[1,6,96,256]{3,2,1,0:T(8,128)(2,1)S(1)}, u32[]{:S(2)}, u32[]{:S(2)}) collective-permute-start(bf16[1,6,96,256]{3,2,1,0:T(8,128)(2,1)S(1)} %get-tuple-element.6), channel_id=1, source_target_pairs={{1,2},{3,4},{5,6},{7,8},{9,10},{11,12},{13,14},{2,1},{4,3},{6,5},{... | collective-permute-start | bytes 884744 | tf_op jit(solution)/shard_map/ppermute | solution.py:259
  19.2 1.9 %collective-permute-start.2 = (bf16[1,6,96,256]{3,2,1,0:T(8,128)(2,1)S(1)}, bf16[1,6,96,256]{3,2,1,0:T(8,128)(2,1)S(1)}, u32[]{:S(2)}, u32[]{:S(2)}) collective-permute-start(bf16[1,6,96,256]{3,2,1,0:T(8,128)(2,1)S(1)} %get-tuple-element.5), channel_id=1, source_target_pairs={{1,2},{3,4},{5,6},{7,8},{9,10},{11,12},{13,14},{2,1},{4,3},{6,5},{... | collective-permute-start | bytes 884744 | tf_op jit(solution)/shard_map/ppermute | solution.py:259
  21.1 1.6 %collective-permute-start.8 = (bf16[4,2,2,96,96]{4,3,2,1,0:T(8,128)(2,1)S(1)}, bf16[4,2,2,96,96]{4,3,2,1,0:T(8,128)(2,1)S(1)}, u32[]{:S(2)}, u32[]{:S(2)}) collective-permute-start(bf16[4,2,2,96,96]{4,3,2,1,0:T(8,128)(2,1)S(1)} %pad_maximum_fusion.refs_2_), channel_id=1, source_target_pairs={{0,1},{1,0},{2,3},{3,2},{4,5},{5,4},{6,7},{7,6},{8,9},{9,8},{10,11... | collective-permute-start | bytes 884744 | tf_op jit(solution)/shard_map/ppermute | solution.py:247
  22.7 1.8 %collective-permute-done.7.refs_3_ = bf16[4,2,2,96,96]{4,3,2,1,0:T(8,128)(2,1)S(1)} collective-permute-done((bf16[4,2,2,96,96]{4,3,2,1,0:T(8,128)(2,1)S(1)}, bf16[4,2,2,96,96]{4,3,2,1,0:T(8,128)(2,1)S(1)}, u32[]{:S(2)}, u32[]{:S(2)}) %collective-permute-start.7) | collective-permute-done | bytes 294944 | tf_op jit(solution)/shard_map/ppermute | solution.py:247
  24.4 1.0 %collective-permute-start.9 = (bf16[4,2,2,96,96]{4,3,2,1,0:T(8,128)(2,1)S(1)}, bf16[4,2,2,96,96]{4,3,2,1,0:T(8,128)(2,1)S(1)}, u32[]{:S(2)}, u32[]{:S(2)}) collective-permute-start(bf16[4,2,2,96,96]{4,3,2,1,0:T(8,128)(2,1)S(1)} %collective-permute-done.7.refs_3_), channel_id=1, source_target_pairs={{0,1},{1,0},{2,3},{3,2},{4,5},{5,4},{6,7},{7,6},{8,9},{9,8},{10,11... | collective-permute-start | bytes 884744 | tf_op jit(solution)/shard_map/ppermute | solution.py:247
  25.5 4.4 %collective-permute-done.halo_hbm = bf16[1,6,96,256]{3,2,1,0:T(8,128)(2,1)S(1)} collective-permute-done((bf16[1,6,96,256]{3,2,1,0:T(8,128)(2,1)S(1)}, bf16[1,6,96,256]{3,2,1,0:T(8,128)(2,1)S(1)}, u32[]{:S(2)}, u32[]{:S(2)}) %collective-permute-start) | collective-permute-done | bytes 294944 | tf_op jit(solution)/shard_map/ppermute | solution.py:259
  29.9 3.8 %shard_map.64.refs_0_ = bf16[6,64,96]{2,1,0:T(8,128)(2,1)S(1)} custom-call(f32[2]{0:T(128)S(1)} %copy-done.1, bf16[1,6,96,256]{3,2,1,0:T(8,128)(2,1)S(1)} %collective-permute-done.halo_hbm, bf16[2,6,96,256]{3,2,1,0:T(8,128)(2,1)S(1)} %copy-done, f32[1,6,96,256]{3,2,1,0:T(8,128)S(1)} %early.1.first_hbm, bf16[256,256]{1,0:T(8,128)(2,1)S(1)} %copy-done.2, ...), custom_call_target="tpu_custom_call" | custom-call | flops 3000000000 | tf_op jit(solution)/shard_map/pallas_call | solution.py:286
  33.7 0.0 copy-start.3
  33.7 0.0 collective-permute-done.3.first_hbm
  33.7 3.8 %shard_map.65.refs_1_ = bf16[6,64,96]{2,1,0:T(8,128)(2,1)S(1)} custom-call(f32[2]{0:T(128)S(1)} %copy-done.1, bf16[1,6,96,256]{3,2,1,0:T(8,128)(2,1)S(1)} %collective-permute-done.2.halo_hbm, bf16[2,6,96,256]{3,2,1,0:T(8,128)(2,1)S(1)} %copy-done, f32[1,6,96,256]{3,2,1,0:T(8,128)S(1)} %collective-permute-done.3.first_hbm, bf16[256,256]{1,0:T(8,128)(2,1)S(1)} %copy-done.2, ...), custom_call_target="tpu_custom_call" | custom-call | flops 3000000000 | tf_op jit(solution)/shard_map/pallas_call | solution.py:286
  37.6 2.3 %radon.1 = bf16[2,6,96,256]{3,2,1,0:T(8,128)(2,1)} custom-call(bf16[6,64,96]{2,1,0:T(8,128)(2,1)S(1)} %shard_map.64.refs_0_, bf16[6,64,96]{2,1,0:T(8,128)(2,1)S(1)} %shard_map.65.refs_1_, bf16[4,2,2,96,96]{4,3,2,1,0:T(8,128)(2,1)S(1)} %pad_maximum_fusion.refs_2_, bf16[4,2,2,96,96]{4,3,2,1,0:T(8,128)(2,1)S(1)} %collective-permute-done.7.refs_3_, ...), custom_call_target="tpu_custom_call" | custom-call | flops 4000000000 | tf_op jit(solution)/shard_map/radon/pallas_call | solution.py:305
  (14 shorter events, 0.0 us)
Async XLA Ops:
  0.0 5.4 %collective-permute-start.1 = (bf16[2,6,96,256]{3,2,1,0:T(8,128)(2,1)}, bf16[2,6,96,256]{3,2,1,0:T(8,128)(2,1)S(1)}, u32[]{:S(2)}, u32[]{:S(2)}) collective-permute-start(bf16[2,6,96,256]{3,2,1,0:T(8,128)(2,1)} %own_hbm.3), channel_id=1, source_target_pairs={{0,1},{1,0},{2,3},{3,2},{4,5},{5,4},{6,7},{7,6},{8,9},{9,8},{10,11... | collective-permute-start | bytes 1769480 | tf_op jit(solution)/shard_map/ppermute | solution.py:247
  0.7 7.6 %collective-permute-start.4 = (bf16[2,2,96,96]{3,2,1,0:T(8,128)(2,1)}, bf16[2,2,96,96]{3,2,1,0:T(8,128)(2,1)S(1)}, u32[]{:S(2)}, u32[]{:S(2)}) collective-permute-start(bf16[2,2,96,96]{3,2,1,0:T(8,128)(2,1)} %param.8), channel_id=1, source_target_pairs={{0,2},{1,3},{2,0},{3,1},{4,6},{5,7},{6,4},{7,5},{8,10},{9,11},{10,... | collective-permute-start | bytes 221192 | tf_op jit(solution)/shard_map/ppermute | solution.py:247
  1.9 6.3 %collective-permute-start.5 = (bf16[2,2,96,96]{3,2,1,0:T(8,128)(2,1)}, bf16[2,2,96,96]{3,2,1,0:T(8,128)(2,1)S(1)}, u32[]{:S(2)}, u32[]{:S(2)}) collective-permute-start(bf16[2,2,96,96]{3,2,1,0:T(8,128)(2,1)} %param.8), channel_id=1, source_target_pairs={{0,8},{1,9},{2,10},{3,11},{4,12},{5,13},{6,14},{7,15},{8,0},{9,1},... | collective-permute-start | bytes 221192 | tf_op jit(solution)/shard_map/ppermute | solution.py:247
  2.0 8.5 %collective-permute-start.6 = (bf16[2,2,96,96]{3,2,1,0:T(8,128)(2,1)}, bf16[2,2,96,96]{3,2,1,0:T(8,128)(2,1)S(1)}, u32[]{:S(2)}, u32[]{:S(2)}) collective-permute-start(bf16[2,2,96,96]{3,2,1,0:T(8,128)(2,1)} %param.8), channel_id=1, source_target_pairs={{0,10},{1,11},{2,8},{3,9},{4,14},{5,15},{6,12},{7,13},{8,2},{9,3},... | collective-permute-start | bytes 221192 | tf_op jit(solution)/shard_map/ppermute | solution.py:247
  4.2 1.2 %copy-start = (bf16[2,6,96,256]{3,2,1,0:T(8,128)(2,1)S(1)}, bf16[2,6,96,256]{3,2,1,0:T(8,128)(2,1)}, u32[]{:S(2)}) copy-start(bf16[2,6,96,256]{3,2,1,0:T(8,128)(2,1)} %own_hbm.3) | copy-start | bytes 1769476
  4.2 1.2 %copy-start.1 = (f32[2]{0:T(128)S(1)}, f32[2]{0:T(128)}, u32[]{:S(2)}) copy-start(f32[2]{0:T(128)} %tau_ref.5) | copy-start | bytes 28
  4.2 1.3 %copy-start.2 = (bf16[256,256]{1,0:T(8,128)(2,1)S(1)}, bf16[256,256]{1,0:T(8,128)(2,1)}, u32[]{:S(2)}) copy-start(bf16[256,256]{1,0:T(8,128)(2,1)} %constant.29.clone.split_ref) | copy-start | bytes 393220
  5.4 5.1 %copy-start.5 = (bf16[2,2,96,96]{3,2,1,0:T(8,128)(2,1)S(1)}, bf16[2,2,96,96]{3,2,1,0:T(8,128)(2,1)}, u32[]{:S(2)}) copy-start(bf16[2,2,96,96]{3,2,1,0:T(8,128)(2,1)} %param.8) | copy-start | bytes 221188
  7.3 26.4 %collective-permute-start.3 = (f32[1,6,96,256]{3,2,1,0:T(8,128)S(1)}, f32[1,6,96,256]{3,2,1,0:T(8,128)S(1)}, u32[]{:S(2)}, u32[]{:S(2)}) collective-permute-start(f32[1,6,96,256]{3,2,1,0:T(8,128)S(1)} %early.1.first_hbm), channel_id=1, source_target_pairs={{0,1},{1,0},{2,3},{3,2},{4,5},{5,4},{6,7},{7,6},{8,9},{9,8},{10,11... | collective-permute-start | bytes 1769480 | tf_op jit(solution)/shard_map/ppermute | solution.py:247
  10.5 19.4 %copy-start.4 = (bf16[64,256]{1,0:T(8,128)(2,1)S(1)}, bf16[64,256]{1,0:T(8,128)(2,1)}, u32[]{:S(2)}) copy-start(bf16[64,256]{1,0:T(8,128)(2,1)} %constant.30.clone.table_ref) | copy-start | bytes 98308
  10.6 13.8 %collective-permute-start.7 = (bf16[4,2,2,96,96]{4,3,2,1,0:T(8,128)(2,1)S(1)}, bf16[4,2,2,96,96]{4,3,2,1,0:T(8,128)(2,1)S(1)}, u32[]{:S(2)}, u32[]{:S(2)}) collective-permute-start(bf16[4,2,2,96,96]{4,3,2,1,0:T(8,128)(2,1)S(1)} %pad_maximum_fusion.refs_2_), channel_id=1, source_target_pairs={{0,4},{1,5},{2,6},{3,7},{4,0},{5,1},{6,2},{7,3},{8,12},{9,13},{10,... | collective-permute-start | bytes 884744 | tf_op jit(solution)/shard_map/ppermute | solution.py:247
  15.4 14.5 %collective-permute-start = (bf16[1,6,96,256]{3,2,1,0:T(8,128)(2,1)S(1)}, bf16[1,6,96,256]{3,2,1,0:T(8,128)(2,1)S(1)}, u32[]{:S(2)}, u32[]{:S(2)}) collective-permute-start(bf16[1,6,96,256]{3,2,1,0:T(8,128)(2,1)S(1)} %get-tuple-element.6), channel_id=1, source_target_pairs={{1,2},{3,4},{5,6},{7,8},{9,10},{11,12},{13,14},{2,1},{4,3},{6,5},{... | collective-permute-start | bytes 884744 | tf_op jit(solution)/shard_map/ppermute | solution.py:259
  19.2 14.5 %collective-permute-start.2 = (bf16[1,6,96,256]{3,2,1,0:T(8,128)(2,1)S(1)}, bf16[1,6,96,256]{3,2,1,0:T(8,128)(2,1)S(1)}, u32[]{:S(2)}, u32[]{:S(2)}) collective-permute-start(bf16[1,6,96,256]{3,2,1,0:T(8,128)(2,1)S(1)} %get-tuple-element.5), channel_id=1, source_target_pairs={{1,2},{3,4},{5,6},{7,8},{9,10},{11,12},{13,14},{2,1},{4,3},{6,5},{... | collective-permute-start | bytes 884744 | tf_op jit(solution)/shard_map/ppermute | solution.py:259
  21.1 16.4 %collective-permute-start.8 = (bf16[4,2,2,96,96]{4,3,2,1,0:T(8,128)(2,1)S(1)}, bf16[4,2,2,96,96]{4,3,2,1,0:T(8,128)(2,1)S(1)}, u32[]{:S(2)}, u32[]{:S(2)}) collective-permute-start(bf16[4,2,2,96,96]{4,3,2,1,0:T(8,128)(2,1)S(1)} %pad_maximum_fusion.refs_2_), channel_id=1, source_target_pairs={{0,1},{1,0},{2,3},{3,2},{4,5},{5,4},{6,7},{7,6},{8,9},{9,8},{10,11... | collective-permute-start | bytes 884744 | tf_op jit(solution)/shard_map/ppermute | solution.py:247
  24.4 13.1 %collective-permute-start.9 = (bf16[4,2,2,96,96]{4,3,2,1,0:T(8,128)(2,1)S(1)}, bf16[4,2,2,96,96]{4,3,2,1,0:T(8,128)(2,1)S(1)}, u32[]{:S(2)}, u32[]{:S(2)}) collective-permute-start(bf16[4,2,2,96,96]{4,3,2,1,0:T(8,128)(2,1)S(1)} %collective-permute-done.7.refs_3_), channel_id=1, source_target_pairs={{0,1},{1,0},{2,3},{3,2},{4,5},{5,4},{6,7},{7,6},{8,9},{9,8},{10,11... | collective-permute-start | bytes 884744 | tf_op jit(solution)/shard_map/ppermute | solution.py:247
  33.7 3.9 %copy-start.3 = (bf16[64,256]{1,0:T(8,128)(2,1)S(1)}, bf16[64,256]{1,0:T(8,128)(2,1)}, u32[]{:S(2)}) copy-start(bf16[64,256]{1,0:T(8,128)(2,1)} %constant.31.clone.refs_6_) | copy-start | bytes 98308

commit v4 on v3

--- a/solution.py
+++ b/solution.py
@@ -147,10 +147,10 @@
         strips(offsets, strip)
 
 
-def late_kernel(turn, tau_ref, halo_hbm, own_hbm, first_hbm, split_ref, table_ref, out_ref, halo_ref, own_ref, first_ref, field_ref, mid_ref, smooth_ref, sems):
-    lines, offsets, depth = own_ref.shape
+def late_kernel(turn, tau_ref, halo_ref, own_ref, first_ref, split_ref, table_ref, out_ref, field_ref, mid_ref, smooth_ref):
+    lines, offsets, depth = own_ref.shape[1:]
     half = depth // 2
-    share = first_hbm.shape[0]
+    share = first_ref.shape[0]
     me = lax.axis_index("xline")
     last = lax.axis_size("xline") - 1
     parity = me % 2
@@ -158,18 +158,8 @@
     mine = turn < share
     place = place_of(parity == 1, lines)
     places = {u: place(u) for u in range(-lines, lines)}
-    inline = inline_at(parity, turn, share)
-    halo_copy = pltpu.make_async_copy(halo_hbm.at[0], halo_ref, sems.at[0])
-    own_copy = pltpu.make_async_copy(own_hbm.at[inline], own_ref, sems.at[1])
-    first_copy = pltpu.make_async_copy(first_hbm.at[turn % share], first_ref, sems.at[2])
-    own_copy.start()
-    halo_copy.start()
-    first_copy.start()
-    own_copy.wait()
-    field_ref[1] = split_block(own_ref[...], split_ref[...])
-    halo_copy.wait()
-    field_ref[0] = split_block(halo_ref[...], split_ref[...])
-    first_copy.wait()
+    field_ref[0] = split_block(halo_ref[0], split_ref[...])
+    field_ref[1] = split_block(own_ref[inline_at(parity, turn, share)], split_ref[...])
 
     def strip(rows):
         before, after = shifts(half)
@@ -186,7 +176,7 @@
             if u < 3:
                 return mid_ref[u + 3, :, :half], mid_ref[u + 3, :, half:]
             spot = u - 3 if mine else lines + 2 - u
-            return first_ref[spot, rows, :half], first_ref[spot, rows, half:]
+            return first_ref[turn % share, spot, rows, :half], first_ref[turn % share, spot, rows, half:]
 
         def store(u, even, odd):
             spot = places[u][1]
@@ -203,36 +193,72 @@
         out_ref[x] = spectrum.astype(BF16)
 
 
-def radon_kernel(near, apart, *refs):
-    *spec_refs, mine_ref, theirs_ref, mine_mate_ref, theirs_mate_ref, inverse_ref, out_ref, bins_ref, done_ref = refs
-    lines, twice, _ = spec_refs[0].shape
-    bins = twice // 2
-    rows = bins_ref.shape[0] // twice
-    me = lax.axis_index("xline")
+def stage_bins(spec_refs, bins_ref):
+    lines, twice = spec_refs[0].shape[:2]
     for i, spec_ref in enumerate(spec_refs):
         for x in range(lines):
             at = (i * lines + x) * twice
             bins_ref[at : at + twice, :] = spec_ref[x].astype(F32)
-    held = mine_ref.shape[1]
-    for ref, extra in ((mine_ref, 0), (mine_mate_ref, 1), (theirs_ref, apart), (theirs_mate_ref, 1 ^ apart)):
-        for j, offset in enumerate(near):
-            owner = me ^ (offset ^ extra)
-            for b in range(held):
-                k = owner * held + b
-                real = bins_ref[pl.ds(k, rows, stride=twice), :]
-                imag = bins_ref[pl.ds(bins + k, rows, stride=twice), :]
-                both = jnp.concatenate([real, imag], axis=0).astype(BF16)
-                by_real = lax.dot_general(both, ref[j, b, 0], (((1,), (1,)), ((), ())), preferred_element_type=F32)
-                by_imag = lax.dot_general(both, ref[j, b, 1], (((1,), (1,)), ((), ())), preferred_element_type=F32)
-                done_ref[pl.ds(k, rows, stride=twice), :] = by_real[:rows] - by_imag[rows:]
-                done_ref[pl.ds(bins + k, rows, stride=twice), :] = by_imag[:rows] + by_real[rows:]
+
+
+def bins_of(near, apart, planes, extras, held):
+    me = lax.axis_index("xline") ^ (apart * (lax.axis_index("parts") % planes))
+    return [
+        (n, j, b, (me ^ (offset ^ extra)) * held + b)
+        for n, extra in enumerate(extras)
+        for j, offset in enumerate(near)
+        for b in range(held)
+    ]
+
+
+def filter_bin(bins_ref, twice, k, by_real_ref, by_imag_ref):
+    rows = bins_ref.shape[0] // twice
+    real = bins_ref[pl.ds(k, rows, stride=twice), :]
+    imag = bins_ref[pl.ds(twice // 2 + k, rows, stride=twice), :]
+    both = jnp.concatenate([real, imag], axis=0).astype(BF16)
+    by_real = lax.dot_general(both, by_real_ref[...], (((1,), (1,)), ((), ())), preferred_element_type=F32)
+    by_imag = lax.dot_general(both, by_imag_ref[...], (((1,), (1,)), ((), ())), preferred_element_type=F32)
+    return by_real[:rows] - by_imag[rows:], by_imag[:rows] + by_real[rows:]
+
+
+def some_bins_kernel(near, apart, planes, extras, *refs):
+    *spec_refs, out_ref, bins_ref = refs
+    spec_refs, set_refs = spec_refs[: -len(extras)], spec_refs[-len(extras) :]
+    twice = spec_refs[0].shape[1]
+    stage_bins(spec_refs, bins_ref)
+    for at, (n, j, b, k) in enumerate(bins_of(near, apart, planes, extras, set_refs[0].shape[1])):
+        ref = set_refs[n]
+        out_ref[at, 0], out_ref[at, 1] = filter_bin(bins_ref, twice, k, ref.at[j, b, 0], ref.at[j, b, 1])
+
+
+def radon_kernel(near, apart, planes, extras, last_extra, *refs):
+    *spec_refs, some_ref, last_ref, inverse_ref, out_hbm, bins_ref, done_ref, out_ref, sems = refs
+    lines, twice = spec_refs[0].shape[:2]
+    bins = twice // 2
+    rows = bins_ref.shape[0] // twice
+    held = last_ref.shape[1]
+    parity = lax.axis_index("xline") % 2
+    for at, (_, _, _, k) in enumerate(bins_of(near, apart, planes, extras, held)):
+        done_ref[pl.ds(k, rows, stride=twice), :] = some_ref[at, 0]
+        done_ref[pl.ds(bins + k, rows, stride=twice), :] = some_ref[at, 1]
+    stage_bins(spec_refs, bins_ref)
+    for _, j, b, k in bins_of(near, apart, planes, (last_extra,), held):
+        real, imag = filter_bin(bins_ref, twice, k, last_ref.at[j, b, 0], last_ref.at[j, b, 1])
+        done_ref[pl.ds(k, rows, stride=twice), :] = real
+        done_ref[pl.ds(bins + k, rows, stride=twice), :] = imag
+    copies = []
     for i in range(len(spec_refs)):
-        inline = inline_at(me % 2, i, len(spec_refs) // 2)
+        inline = inline_at(parity, i, len(spec_refs) // 2)
         for x in range(lines):
             at = (i * lines + x) * twice
             filtered = done_ref[at : at + twice, :].astype(BF16)
             result = lax.dot_general(filtered, inverse_ref[...], (((0,), (0,)), ((), ())), preferred_element_type=F32)
-            out_ref[inline, x] = result.astype(BF16)
+            out_ref[i, x] = result.astype(BF16)
+            copy = pltpu.make_async_copy(out_ref.at[i, x], out_hbm.at[inline, x], sems.at[i, x])
+            copy.start()
+            copies.append(copy)
+    for copy in copies:
+        copy.wait()
 
 
 def swapped(gathers, time_steps, radon_op):
@@ -240,6 +266,7 @@
     devices = lax.axis_size("xline")
     held = radon_op.shape[0]
     bins = held * devices
+    planes = 1
     apart = 4
     near = tuple(o for o in range(0, devices, 2) if not o & apart)
 
@@ -267,7 +294,7 @@
     table = forward_table(depth, bins)
     table = np.concatenate([table[0::2], table[1::2]], axis=0).T
     split = jnp.asarray(split_matrix(depth))
-    any_space = pl.BlockSpec(memory_space=pl.ANY)
+    any_space = pl.BlockSpec(memory_space=pltpu.HBM)
     share = inlines // 2
     first = pl.pallas_call(
         early_kernel,
@@ -286,35 +313,44 @@
             pl.pallas_call(
                 functools.partial(late_kernel, i),
                 out_shape=jax.ShapeDtypeStruct((lines, 2 * bins, offsets), BF16),
-                in_specs=[smem] + [any_space] * 3 + [vmem] * 2,
+                in_specs=[smem] + [vmem] * 5,
                 out_specs=vmem,
                 scratch_shapes=[
-                    pltpu.VMEM((lines, offsets, depth), BF16),
-                    pltpu.VMEM((lines, offsets, depth), BF16),
-                    pltpu.VMEM((lines, offsets, depth), F32),
                     pltpu.VMEM((2, lines, offsets, depth), F32),
                     pltpu.VMEM((6, ROWS, depth), F32),
                     pltpu.VMEM((lines, offsets, depth), F32),
-                    pltpu.SemaphoreType.DMA((3,)),
                 ],
                 cost_estimate=pl.CostEstimate(flops=3_000_000_000, bytes_accessed=0, transcendentals=0),
                 compiler_params=pltpu.CompilerParams(vmem_limit_bytes=16 << 20),
             )(time_steps, halos[i], gathers, first if i < share else other, split, jnp.asarray(table))
         )
     rows = -(-inlines * lines // 16) * 16
+    extras = (0, 1, apart)
+    some = pl.pallas_call(
+        functools.partial(some_bins_kernel, near, apart, planes, extras),
+        out_shape=jax.ShapeDtypeStruct((len(extras) * len(near) * held, 2, rows, offsets), F32),
+        in_specs=[vmem] * (len(spectra) + len(extras)),
+        out_specs=vmem,
+        scratch_shapes=[pltpu.VMEM((rows * 2 * bins, offsets), F32)],
+        cost_estimate=pl.CostEstimate(flops=1_000_000_000, bytes_accessed=0, transcendentals=0),
+        compiler_params=pltpu.CompilerParams(vmem_limit_bytes=16 << 20),
+        name="some",
+    )(*spectra, mine, mine_mate, theirs)
     return pl.pallas_call(
-        functools.partial(radon_kernel, near, apart),
+        functools.partial(radon_kernel, near, apart, planes, extras, 1 ^ apart),
         out_shape=jax.ShapeDtypeStruct((inlines, lines, offsets, depth), BF16),
-        in_specs=[vmem] * (len(spectra) + 5),
-        out_specs=vmem,
+        in_specs=[vmem] * (len(spectra) + 3),
+        out_specs=any_space,
         scratch_shapes=[
             pltpu.VMEM((rows * 2 * bins, offsets), F32),
             pltpu.VMEM((rows * 2 * bins, offsets), F32),
+            pltpu.VMEM((inlines, lines, offsets, depth), BF16),
+            pltpu.SemaphoreType.DMA((inlines, lines)),
         ],
-        cost_estimate=pl.CostEstimate(flops=int(4e-6 * 1.0e15), bytes_accessed=0, transcendentals=0),
+        cost_estimate=pl.CostEstimate(flops=2_000_000_000, bytes_accessed=0, transcendentals=0),
         compiler_params=pltpu.CompilerParams(vmem_limit_bytes=16 << 20),
         name="radon",
-    )(*spectra, mine, theirs, mine_mate, theirs_mate, jnp.asarray(inverse_table(depth, bins)))
+    )(*spectra, some, theirs_mate, jnp.asarray(inverse_table(depth, bins)))
 
 
 def solution(mesh):

time: 40.1 us -> 38.9 us (0.970)
  Pallas kernels: 11.7 us -> 10.8 us
    pallas_call x2, Pallas kernels: 7.6 us -> 6.48 us  [swapped(): pl.pallas_call(functools.partial(late_kernel, i), out_shape=jax.ShapeDtyp...]
    pallas_call x1 -> x2, Pallas kernels: 2.32 us -> 2.55 us  [the longest x1 1.82 us: swapped(): pl.pallas_call(functools.partial(radon_kernel, near, apart, planes, extra...]
  transfers between devices with their start and end apart: 10 -> 10, of which waited for: 3 -> 3; matrix products, arithmetic and copies ran while one was open for 3% -> 3% of each run, Pallas kernels for 24% -> 23%
where the time goes in v4:
time: 38.9 us; the launch traced here: 38.7 us
  starting transfers between devices  18 us (46%)
  Pallas kernels  10.8 us (28%)
  waiting for transfers between devices  8.34 us (21%)
  local copies, waits for them, and re-layouts  1.26 us (3%)
    ppermute x8, starting transfers between devices, swap(): return lax.ppermute(value, 'xline', [(i, i ^ mask) for i in range(devices)])  12.4 us
    pallas_call x2, Pallas kernels, swapped(): pl.pallas_call(functools.partial(late_kernel, i), out_shape=jax.ShapeDtyp...  6.48 us
    ppermute x2, starting transfers between devices, swapped(): halos.append(lax.ppermute(sent, 'xline', cross))  5.55 us
    ppermute x2, waiting for transfers between devices, swapped(): halos.append(lax.ppermute(sent, 'xline', cross))  4.28 us
    ppermute x8, waiting for transfers between devices, swap(): return lax.ppermute(value, 'xline', [(i, i ^ mask) for i in range(devices)])  4.06 us
    pallas_call x1, Pallas kernels, swapped(): pl.pallas_call(functools.partial(radon_kernel, near, apart, planes, extra...  1.82 us
    pallas_call x1, Pallas kernels, swapped(): pl.pallas_call(early_kernel, out_shape=jax.ShapeDtypeStruct((share, lines...  1.81 us
    dynamic_slice x1, local copies, waits for them, and re-layouts, swapped(): sent = lax.dynamic_slice_in_dim(gathers, at, 1, axis=0)  1.16 us
  transfers between devices with their start and end apart: 10, of which 3 were waited for; matrix products, arithmetic and copies ran while one was open for 3% of the time, Pallas kernels for 23%

profile of v4, /device:TPU:17, one launch (start us, length us, event | category | flops | bytes accessed | tf_op | source)
XLA Modules:
  0.0 38.7 jit_solution(17134940063911401001)
XLA Ops:
  0.0 0.7 %collective-permute-start.1 = (bf16[2,6,96,256]{3,2,1,0:T(8,128)(2,1)}, bf16[2,6,96,256]{3,2,1,0:T(8,128)(2,1)S(1)}, u32[]{:S(2)}, u32[]{:S(2)}) collective-permute-start(bf16[2,6,96,256]{3,2,1,0:T(8,128)(2,1)} %own_ref.5), channel_id=1, source_target_pairs={{0,1},{1,0},{2,3},{3,2},{4,5},{5,4},{6,7},{7,6},{8,9},{9,8},{10,11... | collective-permute-start | bytes 1769480 | tf_op jit(solution)/shard_map/ppermute | solution.py:274
  0.7 1.0 %collective-permute-start.6 = (bf16[2,2,96,96]{3,2,1,0:T(8,128)(2,1)}, bf16[2,2,96,96]{3,2,1,0:T(8,128)(2,1)S(1)}, u32[]{:S(2)}, u32[]{:S(2)}) collective-permute-start(bf16[2,2,96,96]{3,2,1,0:T(8,128)(2,1)} %param.8), channel_id=1, source_target_pairs={{0,10},{1,11},{2,8},{3,9},{4,14},{5,15},{6,12},{7,13},{8,2},{9,3},... | collective-permute-start | bytes 221192 | tf_op jit(solution)/shard_map/ppermute | solution.py:274
  1.7 2.3 %collective-permute-start.5 = (bf16[2,2,96,96]{3,2,1,0:T(8,128)(2,1)}, bf16[2,2,96,96]{3,2,1,0:T(8,128)(2,1)S(1)}, u32[]{:S(2)}, u32[]{:S(2)}) collective-permute-start(bf16[2,2,96,96]{3,2,1,0:T(8,128)(2,1)} %param.8), channel_id=1, source_target_pairs={{0,8},{1,9},{2,10},{3,11},{4,12},{5,13},{6,14},{7,15},{8,0},{9,1},... | collective-permute-start | bytes 221192 | tf_op jit(solution)/shard_map/ppermute | solution.py:274
  4.0 0.2 collective-permute-start.4
  4.2 1.2 %constant_dynamic-slice_fusion = (bf16[1,6,96,256]{3,2,1,0:T(8,128)(2,1)S(1)}, bf16[1,6,96,256]{3,2,1,0:T(8,128)(2,1)S(1)}) fusion(bf16[2,6,96,256]{3,2,1,0:T(8,128)(2,1)} %own_ref.5, s32[]{:T(128)S(6)} %select_n.20, s32[]{:T(128)S(6)} %select_n.19), kind=kLoop, calls=%fused_computation.1 | loop fusion | bytes 1179656 | tf_op jit(solution)/shard_map/dynamic_slice | solution.py:285
  5.4 0.0 copy-start.5
  5.4 0.1 copy-done
  5.5 0.0 copy-done.2
  5.5 1.8 %early.1.first_ref = f32[1,6,96,256]{3,2,1,0:T(8,128)S(1)} custom-call(f32[2]{0:T(128)S(1)} %copy-done.1, bf16[2,6,96,256]{3,2,1,0:T(8,128)(2,1)S(1)} %copy-done, bf16[2,6,96,256]{3,2,1,0:T(8,128)(2,1)S(1)} %collective-permute-done.1.mate_ref, bf16[256,256]{1,0:T(8,128)(2,1)S(1)} %copy-done.2), custom_call_target="tpu_custom_call" | custom-call | flops 3000000000 | tf_op jit(solution)/shard_map/early/pallas_call | solution.py:299
  7.3 0.9 %collective-permute-start.3 = (f32[1,6,96,256]{3,2,1,0:T(8,128)S(1)}, f32[1,6,96,256]{3,2,1,0:T(8,128)S(1)}, u32[]{:S(2)}, u32[]{:S(2)}) collective-permute-start(f32[1,6,96,256]{3,2,1,0:T(8,128)S(1)} %early.1.first_ref), channel_id=1, source_target_pairs={{0,1},{1,0},{2,3},{3,2},{4,5},{5,4},{6,7},{7,6},{8,9},{9,8},{10,11... | collective-permute-start | bytes 1769480 | tf_op jit(solution)/shard_map/ppermute | solution.py:274
  8.2 2.2 %collective-permute-done.5 = bf16[2,2,96,96]{3,2,1,0:T(8,128)(2,1)S(1)} collective-permute-done((bf16[2,2,96,96]{3,2,1,0:T(8,128)(2,1)}, bf16[2,2,96,96]{3,2,1,0:T(8,128)(2,1)S(1)}, u32[]{:S(2)}, u32[]{:S(2)}) %collective-permute-start.5) | collective-permute-done | bytes 73760 | tf_op jit(solution)/shard_map/ppermute | solution.py:274
  10.5 0.1 pad_maximum_fusion.refs_2_
  10.6 4.6 %collective-permute-start.8 = (bf16[4,2,2,96,96]{4,3,2,1,0:T(8,128)(2,1)S(1)}, bf16[4,2,2,96,96]{4,3,2,1,0:T(8,128)(2,1)S(1)}, u32[]{:S(2)}, u32[]{:S(2)}) collective-permute-start(bf16[4,2,2,96,96]{4,3,2,1,0:T(8,128)(2,1)S(1)} %pad_maximum_fusion.refs_2_), channel_id=1, source_target_pairs={{0,4},{1,5},{2,6},{3,7},{4,0},{5,1},{6,2},{7,3},{8,12},{9,13},{10,... | collective-permute-start | bytes 884744 | tf_op jit(solution)/shard_map/ppermute | solution.py:274
  15.2 2.7 %collective-permute-start = (bf16[1,6,96,256]{3,2,1,0:T(8,128)(2,1)S(1)}, bf16[1,6,96,256]{3,2,1,0:T(8,128)(2,1)S(1)}, u32[]{:S(2)}, u32[]{:S(2)}) collective-permute-start(bf16[1,6,96,256]{3,2,1,0:T(8,128)(2,1)S(1)} %get-tuple-element.6), channel_id=1, source_target_pairs={{1,2},{3,4},{5,6},{7,8},{9,10},{11,12},{13,14},{2,1},{4,3},{6,5},{... | collective-permute-start | bytes 884744 | tf_op jit(solution)/shard_map/ppermute | solution.py:286
  17.9 2.8 %collective-permute-start.2 = (bf16[1,6,96,256]{3,2,1,0:T(8,128)(2,1)S(1)}, bf16[1,6,96,256]{3,2,1,0:T(8,128)(2,1)S(1)}, u32[]{:S(2)}, u32[]{:S(2)}) collective-permute-start(bf16[1,6,96,256]{3,2,1,0:T(8,128)(2,1)S(1)} %get-tuple-element.5), channel_id=1, source_target_pairs={{1,2},{3,4},{5,6},{7,8},{9,10},{11,12},{13,14},{2,1},{4,3},{6,5},{... | collective-permute-start | bytes 884744 | tf_op jit(solution)/shard_map/ppermute | solution.py:286
  20.8 1.7 %collective-permute-start.7 = (bf16[4,2,2,96,96]{4,3,2,1,0:T(8,128)(2,1)S(1)}, bf16[4,2,2,96,96]{4,3,2,1,0:T(8,128)(2,1)S(1)}, u32[]{:S(2)}, u32[]{:S(2)}) collective-permute-start(bf16[4,2,2,96,96]{4,3,2,1,0:T(8,128)(2,1)S(1)} %pad_maximum_fusion.refs_2_), channel_id=1, source_target_pairs={{0,1},{1,0},{2,3},{3,2},{4,5},{5,4},{6,7},{7,6},{8,9},{9,8},{10,11... | collective-permute-start | bytes 884744 | tf_op jit(solution)/shard_map/ppermute | solution.py:274
  22.5 1.8 %collective-permute-done.8.refs_4_ = bf16[4,2,2,96,96]{4,3,2,1,0:T(8,128)(2,1)S(1)} collective-permute-done((bf16[4,2,2,96,96]{4,3,2,1,0:T(8,128)(2,1)S(1)}, bf16[4,2,2,96,96]{4,3,2,1,0:T(8,128)(2,1)S(1)}, u32[]{:S(2)}, u32[]{:S(2)}) %collective-permute-start.8) | collective-permute-done | bytes 294944 | tf_op jit(solution)/shard_map/ppermute | solution.py:274
  24.3 1.0 %collective-permute-start.9 = (bf16[4,2,2,96,96]{4,3,2,1,0:T(8,128)(2,1)S(1)}, bf16[4,2,2,96,96]{4,3,2,1,0:T(8,128)(2,1)S(1)}, u32[]{:S(2)}, u32[]{:S(2)}) collective-permute-start(bf16[4,2,2,96,96]{4,3,2,1,0:T(8,128)(2,1)S(1)} %collective-permute-done.8.refs_4_), channel_id=1, source_target_pairs={{0,1},{1,0},{2,3},{3,2},{4,5},{5,4},{6,7},{7,6},{8,9},{9,8},{10,11... | collective-permute-start | bytes 884744 | tf_op jit(solution)/shard_map/ppermute | solution.py:274
  25.3 4.3 %collective-permute-done.halo_ref = bf16[1,6,96,256]{3,2,1,0:T(8,128)(2,1)S(1)} collective-permute-done((bf16[1,6,96,256]{3,2,1,0:T(8,128)(2,1)S(1)}, bf16[1,6,96,256]{3,2,1,0:T(8,128)(2,1)S(1)}, u32[]{:S(2)}, u32[]{:S(2)}) %collective-permute-start) | collective-permute-done | bytes 294944 | tf_op jit(solution)/shard_map/ppermute | solution.py:286
  29.6 3.2 %shard_map.64.refs_0_ = bf16[6,64,96]{2,1,0:T(8,128)(2,1)S(1)} custom-call(f32[2]{0:T(128)S(1)} %copy-done.1, bf16[1,6,96,256]{3,2,1,0:T(8,128)(2,1)S(1)} %collective-permute-done.halo_ref, bf16[2,6,96,256]{3,2,1,0:T(8,128)(2,1)S(1)} %copy-done, f32[1,6,96,256]{3,2,1,0:T(8,128)S(1)} %early.1.first_ref, bf16[256,256]{1,0:T(8,128)(2,1)S(1)} %copy-done.2, ...), custom_call_target="tpu_custom_call" | custom-call | flops 3000000000 | tf_op jit(solution)/shard_map/pallas_call | solution.py:313
  32.8 3.2 %shard_map.65.refs_1_ = bf16[6,64,96]{2,1,0:T(8,128)(2,1)S(1)} custom-call(f32[2]{0:T(128)S(1)} %copy-done.1, bf16[1,6,96,256]{3,2,1,0:T(8,128)(2,1)S(1)} %collective-permute-done.2.halo_ref, bf16[2,6,96,256]{3,2,1,0:T(8,128)(2,1)S(1)} %copy-done, f32[1,6,96,256]{3,2,1,0:T(8,128)S(1)} %collective-permute-done.3.first_ref, bf16[256,256]{1,0:T(8,128)(2,1)S(1)} %copy-done.2, ...), custom_call_target="tpu_custom_call" | custom-call | flops 3000000000 | tf_op jit(solution)/shard_map/pallas_call | solution.py:313
  36.1 0.0 copy-start.3
  36.1 0.7 %some.1.refs_2_ = f32[24,2,16,96]{3,2,1,0:T(8,128)S(1)} custom-call(bf16[6,64,96]{2,1,0:T(8,128)(2,1)S(1)} %shard_map.64.refs_0_, bf16[6,64,96]{2,1,0:T(8,128)(2,1)S(1)} %shard_map.65.refs_1_, bf16[4,2,2,96,96]{4,3,2,1,0:T(8,128)(2,1)S(1)} %pad_maximum_fusion.refs_2_, bf16[4,2,2,96,96]{4,3,2,1,0:T(8,128)(2,1)S(1)} %collective-permute-done.7.refs_3_, ...), custom_call_target="tpu_custom_call" | custom-call | flops 1000000000 | tf_op jit(solution)/shard_map/some/pallas_call | solution.py:329
  36.9 1.8 %radon.1 = bf16[2,6,96,256]{3,2,1,0:T(8,128)(2,1)} custom-call(bf16[6,64,96]{2,1,0:T(8,128)(2,1)S(1)} %shard_map.64.refs_0_, bf16[6,64,96]{2,1,0:T(8,128)(2,1)S(1)} %shard_map.65.refs_1_, f32[24,2,16,96]{3,2,1,0:T(8,128)S(1)} %some.1.refs_2_, bf16[4,2,2,96,96]{4,3,2,1,0:T(8,128)(2,1)S(1)} %collective-permute-done.9.refs_3_, bf16[64,256]{1,0:T(8,128)(2,1)S(1)} %copy-done.3), custom_call_target="tpu_custom_call" | custom-call | flops 2000000000 | tf_op jit(solution)/shard_map/radon/pallas_call | solution.py:339
  (15 shorter events, 0.0 us)
Async XLA Ops:
  0.0 5.4 %collective-permute-start.1 = (bf16[2,6,96,256]{3,2,1,0:T(8,128)(2,1)}, bf16[2,6,96,256]{3,2,1,0:T(8,128)(2,1)S(1)}, u32[]{:S(2)}, u32[]{:S(2)}) collective-permute-start(bf16[2,6,96,256]{3,2,1,0:T(8,128)(2,1)} %own_ref.5), channel_id=1, source_target_pairs={{0,1},{1,0},{2,3},{3,2},{4,5},{5,4},{6,7},{7,6},{8,9},{9,8},{10,11... | collective-permute-start | bytes 1769480 | tf_op jit(solution)/shard_map/ppermute | solution.py:274
  0.7 7.6 %collective-permute-start.6 = (bf16[2,2,96,96]{3,2,1,0:T(8,128)(2,1)}, bf16[2,2,96,96]{3,2,1,0:T(8,128)(2,1)S(1)}, u32[]{:S(2)}, u32[]{:S(2)}) collective-permute-start(bf16[2,2,96,96]{3,2,1,0:T(8,128)(2,1)} %param.8), channel_id=1, source_target_pairs={{0,10},{1,11},{2,8},{3,9},{4,14},{5,15},{6,12},{7,13},{8,2},{9,3},... | collective-permute-start | bytes 221192 | tf_op jit(solution)/shard_map/ppermute | solution.py:274
  1.7 8.8 %collective-permute-start.5 = (bf16[2,2,96,96]{3,2,1,0:T(8,128)(2,1)}, bf16[2,2,96,96]{3,2,1,0:T(8,128)(2,1)S(1)}, u32[]{:S(2)}, u32[]{:S(2)}) collective-permute-start(bf16[2,2,96,96]{3,2,1,0:T(8,128)(2,1)} %param.8), channel_id=1, source_target_pairs={{0,8},{1,9},{2,10},{3,11},{4,12},{5,13},{6,14},{7,15},{8,0},{9,1},... | collective-permute-start | bytes 221192 | tf_op jit(solution)/shard_map/ppermute | solution.py:274
  4.0 6.5 %collective-permute-start.4 = (bf16[2,2,96,96]{3,2,1,0:T(8,128)(2,1)}, bf16[2,2,96,96]{3,2,1,0:T(8,128)(2,1)S(1)}, u32[]{:S(2)}, u32[]{:S(2)}) collective-permute-start(bf16[2,2,96,96]{3,2,1,0:T(8,128)(2,1)} %param.8), channel_id=1, source_target_pairs={{0,2},{1,3},{2,0},{3,1},{4,6},{5,7},{6,4},{7,5},{8,10},{9,11},{10,... | collective-permute-start | bytes 221192 | tf_op jit(solution)/shard_map/ppermute | solution.py:274
  4.2 1.2 %copy-start = (bf16[2,6,96,256]{3,2,1,0:T(8,128)(2,1)S(1)}, bf16[2,6,96,256]{3,2,1,0:T(8,128)(2,1)}, u32[]{:S(2)}) copy-start(bf16[2,6,96,256]{3,2,1,0:T(8,128)(2,1)} %own_ref.5) | copy-start | bytes 1769476
  4.2 1.2 %copy-start.1 = (f32[2]{0:T(128)S(1)}, f32[2]{0:T(128)}, u32[]{:S(2)}) copy-start(f32[2]{0:T(128)} %tau_ref.5) | copy-start | bytes 28
  4.2 1.3 %copy-start.2 = (bf16[256,256]{1,0:T(8,128)(2,1)S(1)}, bf16[256,256]{1,0:T(8,128)(2,1)}, u32[]{:S(2)}) copy-start(bf16[256,256]{1,0:T(8,128)(2,1)} %constant.29.clone.split_ref) | copy-start | bytes 393220
  5.4 5.1 %copy-start.5 = (bf16[2,2,96,96]{3,2,1,0:T(8,128)(2,1)S(1)}, bf16[2,2,96,96]{3,2,1,0:T(8,128)(2,1)}, u32[]{:S(2)}) copy-start(bf16[2,2,96,96]{3,2,1,0:T(8,128)(2,1)} %param.8) | copy-start | bytes 221188
  7.3 25.5 %collective-permute-start.3 = (f32[1,6,96,256]{3,2,1,0:T(8,128)S(1)}, f32[1,6,96,256]{3,2,1,0:T(8,128)S(1)}, u32[]{:S(2)}, u32[]{:S(2)}) collective-permute-start(f32[1,6,96,256]{3,2,1,0:T(8,128)S(1)} %early.1.first_ref), channel_id=1, source_target_pairs={{0,1},{1,0},{2,3},{3,2},{4,5},{5,4},{6,7},{7,6},{8,9},{9,8},{10,11... | collective-permute-start | bytes 1769480 | tf_op jit(solution)/shard_map/ppermute | solution.py:274
  10.5 19.1 %copy-start.4 = (bf16[64,256]{1,0:T(8,128)(2,1)S(1)}, bf16[64,256]{1,0:T(8,128)(2,1)}, u32[]{:S(2)}) copy-start(bf16[64,256]{1,0:T(8,128)(2,1)} %constant.30.clone.table_ref) | copy-start | bytes 98308
  10.6 13.7 %collective-permute-start.8 = (bf16[4,2,2,96,96]{4,3,2,1,0:T(8,128)(2,1)S(1)}, bf16[4,2,2,96,96]{4,3,2,1,0:T(8,128)(2,1)S(1)}, u32[]{:S(2)}, u32[]{:S(2)}) collective-permute-start(bf16[4,2,2,96,96]{4,3,2,1,0:T(8,128)(2,1)S(1)} %pad_maximum_fusion.refs_2_), channel_id=1, source_target_pairs={{0,4},{1,5},{2,6},{3,7},{4,0},{5,1},{6,2},{7,3},{8,12},{9,13},{10,... | collective-permute-start | bytes 884744 | tf_op jit(solution)/shard_map/ppermute | solution.py:274
  15.2 14.3 %collective-permute-start = (bf16[1,6,96,256]{3,2,1,0:T(8,128)(2,1)S(1)}, bf16[1,6,96,256]{3,2,1,0:T(8,128)(2,1)S(1)}, u32[]{:S(2)}, u32[]{:S(2)}) collective-permute-start(bf16[1,6,96,256]{3,2,1,0:T(8,128)(2,1)S(1)} %get-tuple-element.6), channel_id=1, source_target_pairs={{1,2},{3,4},{5,6},{7,8},{9,10},{11,12},{13,14},{2,1},{4,3},{6,5},{... | collective-permute-start | bytes 884744 | tf_op jit(solution)/shard_map/ppermute | solution.py:286
  17.9 14.9 %collective-permute-start.2 = (bf16[1,6,96,256]{3,2,1,0:T(8,128)(2,1)S(1)}, bf16[1,6,96,256]{3,2,1,0:T(8,128)(2,1)S(1)}, u32[]{:S(2)}, u32[]{:S(2)}) collective-permute-start(bf16[1,6,96,256]{3,2,1,0:T(8,128)(2,1)S(1)} %get-tuple-element.5), channel_id=1, source_target_pairs={{1,2},{3,4},{5,6},{7,8},{9,10},{11,12},{13,14},{2,1},{4,3},{6,5},{... | collective-permute-start | bytes 884744 | tf_op jit(solution)/shard_map/ppermute | solution.py:286
  20.8 15.3 %collective-permute-start.7 = (bf16[4,2,2,96,96]{4,3,2,1,0:T(8,128)(2,1)S(1)}, bf16[4,2,2,96,96]{4,3,2,1,0:T(8,128)(2,1)S(1)}, u32[]{:S(2)}, u32[]{:S(2)}) collective-permute-start(bf16[4,2,2,96,96]{4,3,2,1,0:T(8,128)(2,1)S(1)} %pad_maximum_fusion.refs_2_), channel_id=1, source_target_pairs={{0,1},{1,0},{2,3},{3,2},{4,5},{5,4},{6,7},{7,6},{8,9},{9,8},{10,11... | collective-permute-start | bytes 884744 | tf_op jit(solution)/shard_map/ppermute | solution.py:274
  24.3 12.6 %collective-permute-start.9 = (bf16[4,2,2,96,96]{4,3,2,1,0:T(8,128)(2,1)S(1)}, bf16[4,2,2,96,96]{4,3,2,1,0:T(8,128)(2,1)S(1)}, u32[]{:S(2)}, u32[]{:S(2)}) collective-permute-start(bf16[4,2,2,96,96]{4,3,2,1,0:T(8,128)(2,1)S(1)} %collective-permute-done.8.refs_4_), channel_id=1, source_target_pairs={{0,1},{1,0},{2,3},{3,2},{4,5},{5,4},{6,7},{7,6},{8,9},{9,8},{10,11... | collective-permute-start | bytes 884744 | tf_op jit(solution)/shard_map/ppermute | solution.py:274
  36.1 0.8 %copy-start.3 = (bf16[64,256]{1,0:T(8,128)(2,1)S(1)}, bf16[64,256]{1,0:T(8,128)(2,1)}, u32[]{:S(2)}) copy-start(bf16[64,256]{1,0:T(8,128)(2,1)} %constant.31.clone.refs_4_) | copy-start | bytes 98308

commit v5 on v3

--- a/solution.py
+++ b/solution.py
@@ -147,10 +147,10 @@
         strips(offsets, strip)
 
 
-def late_kernel(turn, tau_ref, halo_hbm, own_hbm, first_hbm, split_ref, table_ref, out_ref, halo_ref, own_ref, first_ref, field_ref, mid_ref, smooth_ref, sems):
-    lines, offsets, depth = own_ref.shape
+def late_kernel(turn, tau_ref, halo_ref, own_ref, first_ref, split_ref, table_ref, out_ref, field_ref, mid_ref, smooth_ref):
+    lines, offsets, depth = own_ref.shape[1:]
     half = depth // 2
-    share = first_hbm.shape[0]
+    share = first_ref.shape[0]
     me = lax.axis_index("xline")
     last = lax.axis_size("xline") - 1
     parity = me % 2
@@ -158,18 +158,8 @@
     mine = turn < share
     place = place_of(parity == 1, lines)
     places = {u: place(u) for u in range(-lines, lines)}
-    inline = inline_at(parity, turn, share)
-    halo_copy = pltpu.make_async_copy(halo_hbm.at[0], halo_ref, sems.at[0])
-    own_copy = pltpu.make_async_copy(own_hbm.at[inline], own_ref, sems.at[1])
-    first_copy = pltpu.make_async_copy(first_hbm.at[turn % share], first_ref, sems.at[2])
-    own_copy.start()
-    halo_copy.start()
-    first_copy.start()
-    own_copy.wait()
-    field_ref[1] = split_block(own_ref[...], split_ref[...])
-    halo_copy.wait()
-    field_ref[0] = split_block(halo_ref[...], split_ref[...])
-    first_copy.wait()
+    field_ref[0] = split_block(halo_ref[0], split_ref[...])
+    field_ref[1] = split_block(own_ref[inline_at(parity, turn, share)], split_ref[...])
 
     def strip(rows):
         before, after = shifts(half)
@@ -186,7 +176,7 @@
             if u < 3:
                 return mid_ref[u + 3, :, :half], mid_ref[u + 3, :, half:]
             spot = u - 3 if mine else lines + 2 - u
-            return first_ref[spot, rows, :half], first_ref[spot, rows, half:]
+            return first_ref[turn % share, spot, rows, :half], first_ref[turn % share, spot, rows, half:]
 
         def store(u, even, odd):
             spot = places[u][1]
@@ -203,17 +193,19 @@
         out_ref[x] = spectrum.astype(BF16)
 
 
-def radon_kernel(near, apart, *refs):
-    *spec_refs, mine_ref, theirs_ref, mine_mate_ref, theirs_mate_ref, inverse_ref, out_ref, bins_ref, done_ref = refs
+def radon_kernel(near, apart, planes, *refs):
+    *spec_refs, mine_ref, theirs_ref, mine_mate_ref, theirs_mate_ref, inverse_ref, out_hbm, bins_ref, done_ref, out_ref, sems = refs
     lines, twice, _ = spec_refs[0].shape
     bins = twice // 2
     rows = bins_ref.shape[0] // twice
     me = lax.axis_index("xline")
+    parity = me % 2
     for i, spec_ref in enumerate(spec_refs):
         for x in range(lines):
             at = (i * lines + x) * twice
             bins_ref[at : at + twice, :] = spec_ref[x].astype(F32)
     held = mine_ref.shape[1]
+    me = me ^ (apart * (lax.axis_index("parts") % planes))
     for ref, extra in ((mine_ref, 0), (mine_mate_ref, 1), (theirs_ref, apart), (theirs_mate_ref, 1 ^ apart)):
         for j, offset in enumerate(near):
             owner = me ^ (offset ^ extra)
@@ -226,13 +218,19 @@
                 by_imag = lax.dot_general(both, ref[j, b, 1], (((1,), (1,)), ((), ())), preferred_element_type=F32)
                 done_ref[pl.ds(k, rows, stride=twice), :] = by_real[:rows] - by_imag[rows:]
                 done_ref[pl.ds(bins + k, rows, stride=twice), :] = by_imag[:rows] + by_real[rows:]
+    copies = []
     for i in range(len(spec_refs)):
-        inline = inline_at(me % 2, i, len(spec_refs) // 2)
+        inline = inline_at(parity, i, len(spec_refs) // 2)
         for x in range(lines):
             at = (i * lines + x) * twice
             filtered = done_ref[at : at + twice, :].astype(BF16)
             result = lax.dot_general(filtered, inverse_ref[...], (((0,), (0,)), ((), ())), preferred_element_type=F32)
-            out_ref[inline, x] = result.astype(BF16)
+            out_ref[i, x] = result.astype(BF16)
+            copy = pltpu.make_async_copy(out_ref.at[i, x], out_hbm.at[inline, x], sems.at[i, x])
+            copy.start()
+            copies.append(copy)
+    for copy in copies:
+        copy.wait()
 
 
 def swapped(gathers, time_steps, radon_op):
@@ -240,6 +238,8 @@
     devices = lax.axis_size("xline")
     held = radon_op.shape[0]
     bins = held * devices
+    parts = lax.axis_size("parts")
+    planes = 2 if parts % 2 == 0 else 1
     apart = 4
     near = tuple(o for o in range(0, devices, 2) if not o & apart)
 
@@ -247,10 +247,17 @@
         return lax.ppermute(value, "xline", [(i, i ^ mask) for i in range(devices)])
 
     cross = [(i, i + 1) for i in range(1, devices - 1, 2)] + [(i + 1, i) for i in range(1, devices - 1, 2)]
-    pieces = [radon_op]
-    for o in reversed(near[1:]):
-        pieces.append(swap(radon_op, o))
-    pieces = [pieces[0]] + pieces[:0:-1]
+    plane = lax.axis_index("parts") % planes
+    pieces = []
+    for o in reversed(near):
+        pairs = [
+            (q * devices + i, q * devices + (i ^ o ^ (apart * (q % planes)) if o else i ^ apart))
+            for q in range(parts)
+            for i in range(devices)
+        ]
+        pieces.append(lax.ppermute(radon_op, ("parts", "xline"), pairs))
+    pieces = pieces[::-1]
+    pieces[0] = jnp.where(plane == 0, radon_op, pieces[0])
     mate = swap(gathers, 1)
     halos = []
     for i in range(inlines):
@@ -258,7 +265,11 @@
         sent = lax.dynamic_slice_in_dim(gathers, at, 1, axis=0)
         halos.append(lax.ppermute(sent, "xline", cross))
     mine = jnp.stack(pieces)
-    theirs = swap(mine, apart)
+    if planes == 2:
+        pairs = [(q * devices + i, (q ^ 1) * devices + i) for q in range(parts) for i in range(devices)]
+        theirs = lax.ppermute(mine, ("parts", "xline"), pairs)
+    else:
+        theirs = swap(mine, apart)
     mine_mate = swap(mine, 1)
     theirs_mate = swap(theirs, 1)
 
@@ -267,7 +278,7 @@
     table = forward_table(depth, bins)
     table = np.concatenate([table[0::2], table[1::2]], axis=0).T
     split = jnp.asarray(split_matrix(depth))
-    any_space = pl.BlockSpec(memory_space=pl.ANY)
+    any_space = pl.BlockSpec(memory_space=pltpu.HBM)
     share = inlines // 2
     first = pl.pallas_call(
         early_kernel,
@@ -286,16 +297,12 @@
             pl.pallas_call(
                 functools.partial(late_kernel, i),
                 out_shape=jax.ShapeDtypeStruct((lines, 2 * bins, offsets), BF16),
-                in_specs=[smem] + [any_space] * 3 + [vmem] * 2,
+                in_specs=[smem] + [vmem] * 5,
                 out_specs=vmem,
                 scratch_shapes=[
-                    pltpu.VMEM((lines, offsets, depth), BF16),
-                    pltpu.VMEM((lines, offsets, depth), BF16),
-                    pltpu.VMEM((lines, offsets, depth), F32),
                     pltpu.VMEM((2, lines, offsets, depth), F32),
                     pltpu.VMEM((6, ROWS, depth), F32),
                     pltpu.VMEM((lines, offsets, depth), F32),
-                    pltpu.SemaphoreType.DMA((3,)),
                 ],
                 cost_estimate=pl.CostEstimate(flops=3_000_000_000, bytes_accessed=0, transcendentals=0),
                 compiler_params=pltpu.CompilerParams(vmem_limit_bytes=16 << 20),
@@ -303,13 +310,15 @@
         )
     rows = -(-inlines * lines // 16) * 16
     return pl.pallas_call(
-        functools.partial(radon_kernel, near, apart),
+        functools.partial(radon_kernel, near, apart, planes),
         out_shape=jax.ShapeDtypeStruct((inlines, lines, offsets, depth), BF16),
         in_specs=[vmem] * (len(spectra) + 5),
-        out_specs=vmem,
+        out_specs=any_space,
         scratch_shapes=[
             pltpu.VMEM((rows * 2 * bins, offsets), F32),
             pltpu.VMEM((rows * 2 * bins, offsets), F32),
+            pltpu.VMEM((inlines, lines, offsets, depth), BF16),
+            pltpu.SemaphoreType.DMA((inlines, lines)),
         ],
         cost_estimate=pl.CostEstimate(flops=int(4e-6 * 1.0e15), bytes_accessed=0, transcendentals=0),
         compiler_params=pltpu.CompilerParams(vmem_limit_bytes=16 << 20),

time: 40.1 us -> 39.3 us (0.980)
  the two profiles are of different devices: /device:TPU:17 before, /device:TPU:6 now
where the time goes in v5:
time: 39.3 us; the launch traced here: 39.1 us
  starting transfers between devices  14.3 us (36%)
  waiting for transfers between devices  11.8 us (30%)
  Pallas kernels  10.6 us (27%)
  local copies, waits for them, and re-layouts  2.05 us (5%)
    ppermute x4, starting transfers between devices, swapped(): pieces.append(lax.ppermute(radon_op, ('parts', 'xline'), pairs))  6.75 us
    pallas_call x2, Pallas kernels, swapped(): pl.pallas_call(functools.partial(late_kernel, i), out_shape=jax.ShapeDtyp...  6.5 us
    ppermute x2, waiting for transfers between devices, swapped(): halos.append(lax.ppermute(sent, 'xline', cross))  5.57 us
    ppermute x2, starting transfers between devices, swapped(): halos.append(lax.ppermute(sent, 'xline', cross))  5.55 us
    ppermute x4, waiting for transfers between devices, swapped(): pieces.append(lax.ppermute(radon_op, ('parts', 'xline'), pairs))  3.19 us
    ppermute x1, waiting for transfers between devices, swapped(): theirs = lax.ppermute(mine, ('parts', 'xline'), pairs)  3.03 us
    pallas_call x1, Pallas kernels, swapped(): pl.pallas_call(functools.partial(radon_kernel, near, apart, planes), out_...  2.27 us
    pallas_call x1, Pallas kernels, swapped(): pl.pallas_call(early_kernel, out_shape=jax.ShapeDtypeStruct((share, lines...  1.81 us
  transfers between devices with their start and end apart: 11, of which 4 were waited for; matrix products, arithmetic and copies ran while one was open for 3% of the time, Pallas kernels for 21%

profile of v5, /device:TPU:6, one launch (start us, length us, event | category | flops | bytes accessed | tf_op | source)
XLA Modules:
  0.0 39.1 jit_solution(9176484210668486264)
XLA Ops:
  0.0 1.6 %collective-permute-start.4 = (bf16[2,2,96,96]{3,2,1,0:T(8,128)(2,1)}, bf16[2,2,96,96]{3,2,1,0:T(8,128)(2,1)S(1)}, u32[]{:S(2)}, u32[]{:S(2)}) collective-permute-start(bf16[2,2,96,96]{3,2,1,0:T(8,128)(2,1)} %param.8), channel_id=1, source_target_pairs={{0,4},{1,5},{2,6},{3,7},{4,0},{5,1},{6,2},{7,3},{8,12},{9,13},{10,... | collective-permute-start | bytes 221192 | tf_op jit(solution)/shard_map/ppermute | solution.py:258
  1.6 0.4 %collective-permute-start.5 = (bf16[2,2,96,96]{3,2,1,0:T(8,128)(2,1)}, bf16[2,2,96,96]{3,2,1,0:T(8,128)(2,1)S(1)}, u32[]{:S(2)}, u32[]{:S(2)}) collective-permute-start(bf16[2,2,96,96]{3,2,1,0:T(8,128)(2,1)} %param.8), channel_id=1, source_target_pairs={{0,2},{1,3},{2,0},{3,1},{4,6},{5,7},{6,4},{7,5},{8,10},{9,11},{10,... | collective-permute-start | bytes 221192 | tf_op jit(solution)/shard_map/ppermute | solution.py:258
  2.0 3.6 %collective-permute-start.6 = (bf16[2,2,96,96]{3,2,1,0:T(8,128)(2,1)}, bf16[2,2,96,96]{3,2,1,0:T(8,128)(2,1)S(1)}, u32[]{:S(2)}, u32[]{:S(2)}) collective-permute-start(bf16[2,2,96,96]{3,2,1,0:T(8,128)(2,1)} %param.8), channel_id=1, source_target_pairs={{0,8},{1,9},{2,10},{3,11},{4,12},{5,13},{6,14},{7,15},{8,0},{9,1},... | collective-permute-start | bytes 221192 | tf_op jit(solution)/shard_map/ppermute | solution.py:258
  5.6 1.2 %collective-permute-start.7 = (bf16[2,2,96,96]{3,2,1,0:T(8,128)(2,1)}, bf16[2,2,96,96]{3,2,1,0:T(8,128)(2,1)S(1)}, u32[]{:S(2)}, u32[]{:S(2)}) collective-permute-start(bf16[2,2,96,96]{3,2,1,0:T(8,128)(2,1)} %param.8), channel_id=1, source_target_pairs={{0,10},{1,11},{2,8},{3,9},{4,14},{5,15},{6,12},{7,13},{8,2},{9,3},... | collective-permute-start | bytes 221192 | tf_op jit(solution)/shard_map/ppermute | solution.py:258
  6.8 1.2 %constant_dynamic-slice_fusion = (bf16[1,6,96,256]{3,2,1,0:T(8,128)(2,1)S(1)}, bf16[1,6,96,256]{3,2,1,0:T(8,128)(2,1)S(1)}) fusion(bf16[2,6,96,256]{3,2,1,0:T(8,128)(2,1)} %own_ref.5, s32[]{:T(128)S(6)} %select_n.32, s32[]{:T(128)S(6)} %select_n.31), kind=kLoop, calls=%fused_computation.2 | loop fusion | bytes 1179656 | tf_op jit(solution)/shard_map/dynamic_slice | solution.py:265
  7.9 0.0 copy-start.2
  8.0 0.0 copy-done
  8.0 0.6 %copy-done.1 = f32[2]{0:T(128)S(1)} copy-done((f32[2]{0:T(128)S(1)}, f32[2]{0:T(128)}, u32[]{:S(2)}) %copy-start.1) | copy-done | bytes 32
  8.6 0.3 copy-done.2
  8.9 1.8 %early.1.first_ref = f32[1,6,96,256]{3,2,1,0:T(8,128)S(1)} custom-call(f32[2]{0:T(128)S(1)} %copy-done.1, bf16[2,6,96,256]{3,2,1,0:T(8,128)(2,1)S(1)} %copy-done, bf16[2,6,96,256]{3,2,1,0:T(8,128)(2,1)S(1)} %collective-permute-done.1.mate_ref, bf16[256,256]{1,0:T(8,128)(2,1)S(1)} %copy-done.2), custom_call_target="tpu_custom_call" | custom-call | flops 3000000000 | tf_op jit(solution)/shard_map/early/pallas_call | solution.py:283
  10.7 0.1 collective-permute-start.3
  10.8 1.5 %collective-permute-done.6 = bf16[2,2,96,96]{3,2,1,0:T(8,128)(2,1)S(1)} collective-permute-done((bf16[2,2,96,96]{3,2,1,0:T(8,128)(2,1)}, bf16[2,2,96,96]{3,2,1,0:T(8,128)(2,1)S(1)}, u32[]{:S(2)}, u32[]{:S(2)}) %collective-permute-start.6) | collective-permute-done | bytes 73760 | tf_op jit(solution)/shard_map/ppermute | solution.py:258
  12.3 1.7 %collective-permute-done.7 = bf16[2,2,96,96]{3,2,1,0:T(8,128)(2,1)S(1)} collective-permute-done((bf16[2,2,96,96]{3,2,1,0:T(8,128)(2,1)}, bf16[2,2,96,96]{3,2,1,0:T(8,128)(2,1)S(1)}, u32[]{:S(2)}, u32[]{:S(2)}) %collective-permute-start.7) | collective-permute-done | bytes 73760 | tf_op jit(solution)/shard_map/ppermute | solution.py:258
  14.0 0.1 pad_maximum_fusion.refs_2_
  14.1 1.8 %collective-permute-start.8 = (bf16[4,2,2,96,96]{4,3,2,1,0:T(8,128)(2,1)S(1)}, bf16[4,2,2,96,96]{4,3,2,1,0:T(8,128)(2,1)S(1)}, u32[]{:S(2)}, u32[]{:S(2)}) collective-permute-start(bf16[4,2,2,96,96]{4,3,2,1,0:T(8,128)(2,1)S(1)} %pad_maximum_fusion.refs_2_), channel_id=1, source_target_pairs={{0,16},{1,17},{2,18},{3,19},{4,20},{5,21},{6,22},{7,23},{8,24},{9,... | collective-permute-start | bytes 884744 | tf_op jit(solution)/shard_map/ppermute | solution.py:270
  15.9 1.9 %collective-permute-start = (bf16[1,6,96,256]{3,2,1,0:T(8,128)(2,1)S(1)}, bf16[1,6,96,256]{3,2,1,0:T(8,128)(2,1)S(1)}, u32[]{:S(2)}, u32[]{:S(2)}) collective-permute-start(bf16[1,6,96,256]{3,2,1,0:T(8,128)(2,1)S(1)} %get-tuple-element.6), channel_id=1, source_target_pairs={{1,2},{3,4},{5,6},{7,8},{9,10},{11,12},{13,14},{2,1},{4,3},{6,5},{... | collective-permute-start | bytes 884744 | tf_op jit(solution)/shard_map/ppermute | solution.py:266
  17.8 3.6 %collective-permute-start.2 = (bf16[1,6,96,256]{3,2,1,0:T(8,128)(2,1)S(1)}, bf16[1,6,96,256]{3,2,1,0:T(8,128)(2,1)S(1)}, u32[]{:S(2)}, u32[]{:S(2)}) collective-permute-start(bf16[1,6,96,256]{3,2,1,0:T(8,128)(2,1)S(1)} %get-tuple-element.5), channel_id=1, source_target_pairs={{1,2},{3,4},{5,6},{7,8},{9,10},{11,12},{13,14},{2,1},{4,3},{6,5},{... | collective-permute-start | bytes 884744 | tf_op jit(solution)/shard_map/ppermute | solution.py:266
  21.4 0.2 collective-permute-start.9
  21.6 3.0 %collective-permute-done.8.refs_3_ = bf16[4,2,2,96,96]{4,3,2,1,0:T(8,128)(2,1)S(1)} collective-permute-done((bf16[4,2,2,96,96]{4,3,2,1,0:T(8,128)(2,1)S(1)}, bf16[4,2,2,96,96]{4,3,2,1,0:T(8,128)(2,1)S(1)}, u32[]{:S(2)}, u32[]{:S(2)}) %collective-permute-start.8) | collective-permute-done | bytes 294944 | tf_op jit(solution)/shard_map/ppermute | solution.py:270
  24.6 5.6 %collective-permute-done.halo_ref = bf16[1,6,96,256]{3,2,1,0:T(8,128)(2,1)S(1)} collective-permute-done((bf16[1,6,96,256]{3,2,1,0:T(8,128)(2,1)S(1)}, bf16[1,6,96,256]{3,2,1,0:T(8,128)(2,1)S(1)}, u32[]{:S(2)}, u32[]{:S(2)}) %collective-permute-start) | collective-permute-done | bytes 294944 | tf_op jit(solution)/shard_map/ppermute | solution.py:266
  30.2 3.2 %shard_map.64.refs_0_ = bf16[6,64,96]{2,1,0:T(8,128)(2,1)S(1)} custom-call(f32[2]{0:T(128)S(1)} %copy-done.1, bf16[1,6,96,256]{3,2,1,0:T(8,128)(2,1)S(1)} %collective-permute-done.halo_ref, bf16[2,6,96,256]{3,2,1,0:T(8,128)(2,1)S(1)} %copy-done, f32[1,6,96,256]{3,2,1,0:T(8,128)S(1)} %early.1.first_ref, bf16[256,256]{1,0:T(8,128)(2,1)S(1)} %copy-done.2, ...), custom_call_target="tpu_custom_call" | custom-call | flops 3000000000 | tf_op jit(solution)/shard_map/pallas_call | solution.py:297
  33.5 0.0 copy-start.3
  33.5 3.3 %shard_map.65.refs_1_ = bf16[6,64,96]{2,1,0:T(8,128)(2,1)S(1)} custom-call(f32[2]{0:T(128)S(1)} %copy-done.1, bf16[1,6,96,256]{3,2,1,0:T(8,128)(2,1)S(1)} %collective-permute-done.2.halo_ref, bf16[2,6,96,256]{3,2,1,0:T(8,128)(2,1)S(1)} %copy-done, f32[1,6,96,256]{3,2,1,0:T(8,128)S(1)} %collective-permute-done.3.first_ref, bf16[256,256]{1,0:T(8,128)(2,1)S(1)} %copy-done.2, ...), custom_call_target="tpu_custom_call" | custom-call | flops 3000000000 | tf_op jit(solution)/shard_map/pallas_call | solution.py:297
  36.8 2.3 %radon.1 = bf16[2,6,96,256]{3,2,1,0:T(8,128)(2,1)} custom-call(bf16[6,64,96]{2,1,0:T(8,128)(2,1)S(1)} %shard_map.64.refs_0_, bf16[6,64,96]{2,1,0:T(8,128)(2,1)S(1)} %shard_map.65.refs_1_, bf16[4,2,2,96,96]{4,3,2,1,0:T(8,128)(2,1)S(1)} %pad_maximum_fusion.refs_2_, bf16[4,2,2,96,96]{4,3,2,1,0:T(8,128)(2,1)S(1)} %collective-permute-done.8.refs_3_, ...), custom_call_target="tpu_custom_call" | custom-call | flops 4000000000 | tf_op jit(solution)/shard_map/radon/pallas_call | solution.py:312
  (17 shorter events, 0.1 us)
Async XLA Ops:
  0.0 8.0 %collective-permute-start.1 = (bf16[2,6,96,256]{3,2,1,0:T(8,128)(2,1)}, bf16[2,6,96,256]{3,2,1,0:T(8,128)(2,1)S(1)}, u32[]{:S(2)}, u32[]{:S(2)}) collective-permute-start(bf16[2,6,96,256]{3,2,1,0:T(8,128)(2,1)} %own_ref.5), channel_id=1, source_target_pairs={{0,1},{1,0},{2,3},{3,2},{4,5},{5,4},{6,7},{7,6},{8,9},{9,8},{10,11... | collective-permute-start | bytes 1769480 | tf_op jit(solution)/shard_map/ppermute | solution.py:247
  0.0 7.9 %collective-permute-start.4 = (bf16[2,2,96,96]{3,2,1,0:T(8,128)(2,1)}, bf16[2,2,96,96]{3,2,1,0:T(8,128)(2,1)S(1)}, u32[]{:S(2)}, u32[]{:S(2)}) collective-permute-start(bf16[2,2,96,96]{3,2,1,0:T(8,128)(2,1)} %param.8), channel_id=1, source_target_pairs={{0,4},{1,5},{2,6},{3,7},{4,0},{5,1},{6,2},{7,3},{8,12},{9,13},{10,... | collective-permute-start | bytes 221192 | tf_op jit(solution)/shard_map/ppermute | solution.py:258
  1.6 9.2 %collective-permute-start.5 = (bf16[2,2,96,96]{3,2,1,0:T(8,128)(2,1)}, bf16[2,2,96,96]{3,2,1,0:T(8,128)(2,1)S(1)}, u32[]{:S(2)}, u32[]{:S(2)}) collective-permute-start(bf16[2,2,96,96]{3,2,1,0:T(8,128)(2,1)} %param.8), channel_id=1, source_target_pairs={{0,2},{1,3},{2,0},{3,1},{4,6},{5,7},{6,4},{7,5},{8,10},{9,11},{10,... | collective-permute-start | bytes 221192 | tf_op jit(solution)/shard_map/ppermute | solution.py:258
  2.0 10.3 %collective-permute-start.6 = (bf16[2,2,96,96]{3,2,1,0:T(8,128)(2,1)}, bf16[2,2,96,96]{3,2,1,0:T(8,128)(2,1)S(1)}, u32[]{:S(2)}, u32[]{:S(2)}) collective-permute-start(bf16[2,2,96,96]{3,2,1,0:T(8,128)(2,1)} %param.8), channel_id=1, source_target_pairs={{0,8},{1,9},{2,10},{3,11},{4,12},{5,13},{6,14},{7,15},{8,0},{9,1},... | collective-permute-start | bytes 221192 | tf_op jit(solution)/shard_map/ppermute | solution.py:258
  5.6 8.4 %collective-permute-start.7 = (bf16[2,2,96,96]{3,2,1,0:T(8,128)(2,1)}, bf16[2,2,96,96]{3,2,1,0:T(8,128)(2,1)S(1)}, u32[]{:S(2)}, u32[]{:S(2)}) collective-permute-start(bf16[2,2,96,96]{3,2,1,0:T(8,128)(2,1)} %param.8), channel_id=1, source_target_pairs={{0,10},{1,11},{2,8},{3,9},{4,14},{5,15},{6,12},{7,13},{8,2},{9,3},... | collective-permute-start | bytes 221192 | tf_op jit(solution)/shard_map/ppermute | solution.py:258
  6.8 1.2 %copy-start.5 = (bf16[2,2,96,96]{3,2,1,0:T(8,128)(2,1)S(1)}, bf16[2,2,96,96]{3,2,1,0:T(8,128)(2,1)}, u32[]{:S(2)}) copy-start(bf16[2,2,96,96]{3,2,1,0:T(8,128)(2,1)} %param.8) | copy-start | bytes 221188
  6.8 1.3 %copy-start = (bf16[2,6,96,256]{3,2,1,0:T(8,128)(2,1)S(1)}, bf16[2,6,96,256]{3,2,1,0:T(8,128)(2,1)}, u32[]{:S(2)}) copy-start(bf16[2,6,96,256]{3,2,1,0:T(8,128)(2,1)} %own_ref.5) | copy-start | bytes 1769476
  7.9 0.7 %copy-start.1 = (f32[2]{0:T(128)S(1)}, f32[2]{0:T(128)}, u32[]{:S(2)}) copy-start(f32[2]{0:T(128)} %tau_ref.5) | copy-start | bytes 28
  7.9 0.9 %copy-start.2 = (bf16[256,256]{1,0:T(8,128)(2,1)S(1)}, bf16[256,256]{1,0:T(8,128)(2,1)}, u32[]{:S(2)}) copy-start(bf16[256,256]{1,0:T(8,128)(2,1)} %constant.38.clone.split_ref) | copy-start | bytes 393220
  10.7 22.8 %collective-permute-start.3 = (f32[1,6,96,256]{3,2,1,0:T(8,128)S(1)}, f32[1,6,96,256]{3,2,1,0:T(8,128)S(1)}, u32[]{:S(2)}, u32[]{:S(2)}) collective-permute-start(f32[1,6,96,256]{3,2,1,0:T(8,128)S(1)} %early.1.first_ref), channel_id=1, source_target_pairs={{0,1},{1,0},{2,3},{3,2},{4,5},{5,4},{6,7},{7,6},{8,9},{9,8},{10,11... | collective-permute-start | bytes 1769480 | tf_op jit(solution)/shard_map/ppermute | solution.py:247
  14.0 16.2 %copy-start.4 = (bf16[64,256]{1,0:T(8,128)(2,1)S(1)}, bf16[64,256]{1,0:T(8,128)(2,1)}, u32[]{:S(2)}) copy-start(bf16[64,256]{1,0:T(8,128)(2,1)} %constant.39.clone.table_ref) | copy-start | bytes 98308
  14.1 10.6 %collective-permute-start.8 = (bf16[4,2,2,96,96]{4,3,2,1,0:T(8,128)(2,1)S(1)}, bf16[4,2,2,96,96]{4,3,2,1,0:T(8,128)(2,1)S(1)}, u32[]{:S(2)}, u32[]{:S(2)}) collective-permute-start(bf16[4,2,2,96,96]{4,3,2,1,0:T(8,128)(2,1)S(1)} %pad_maximum_fusion.refs_2_), channel_id=1, source_target_pairs={{0,16},{1,17},{2,18},{3,19},{4,20},{5,21},{6,22},{7,23},{8,24},{9,... | collective-permute-start | bytes 884744 | tf_op jit(solution)/shard_map/ppermute | solution.py:270
  15.9 14.3 %collective-permute-start = (bf16[1,6,96,256]{3,2,1,0:T(8,128)(2,1)S(1)}, bf16[1,6,96,256]{3,2,1,0:T(8,128)(2,1)S(1)}, u32[]{:S(2)}, u32[]{:S(2)}) collective-permute-start(bf16[1,6,96,256]{3,2,1,0:T(8,128)(2,1)S(1)} %get-tuple-element.6), channel_id=1, source_target_pairs={{1,2},{3,4},{5,6},{7,8},{9,10},{11,12},{13,14},{2,1},{4,3},{6,5},{... | collective-permute-start | bytes 884744 | tf_op jit(solution)/shard_map/ppermute | solution.py:266
  17.8 15.7 %collective-permute-start.2 = (bf16[1,6,96,256]{3,2,1,0:T(8,128)(2,1)S(1)}, bf16[1,6,96,256]{3,2,1,0:T(8,128)(2,1)S(1)}, u32[]{:S(2)}, u32[]{:S(2)}) collective-permute-start(bf16[1,6,96,256]{3,2,1,0:T(8,128)(2,1)S(1)} %get-tuple-element.5), channel_id=1, source_target_pairs={{1,2},{3,4},{5,6},{7,8},{9,10},{11,12},{13,14},{2,1},{4,3},{6,5},{... | collective-permute-start | bytes 884744 | tf_op jit(solution)/shard_map/ppermute | solution.py:266
  21.4 15.3 %collective-permute-start.9 = (bf16[4,2,2,96,96]{4,3,2,1,0:T(8,128)(2,1)S(1)}, bf16[4,2,2,96,96]{4,3,2,1,0:T(8,128)(2,1)S(1)}, u32[]{:S(2)}, u32[]{:S(2)}) collective-permute-start(bf16[4,2,2,96,96]{4,3,2,1,0:T(8,128)(2,1)S(1)} %pad_maximum_fusion.refs_2_), channel_id=1, source_target_pairs={{0,1},{1,0},{2,3},{3,2},{4,5},{5,4},{6,7},{7,6},{8,9},{9,8},{10,11... | collective-permute-start | bytes 884744 | tf_op jit(solution)/shard_map/ppermute | solution.py:247
  24.6 12.1 %collective-permute-start.10 = (bf16[4,2,2,96,96]{4,3,2,1,0:T(8,128)(2,1)S(1)}, bf16[4,2,2,96,96]{4,3,2,1,0:T(8,128)(2,1)S(1)}, u32[]{:S(2)}, u32[]{:S(2)}) collective-permute-start(bf16[4,2,2,96,96]{4,3,2,1,0:T(8,128)(2,1)S(1)} %collective-permute-done.8.refs_3_), channel_id=1, source_target_pairs={{0,1},{1,0},{2,3},{3,2},{4,5},{5,4},{6,7},{7,6},{8,9},{9,8},{10,11... | collective-permute-start | bytes 884744 | tf_op jit(solution)/shard_map/ppermute | solution.py:247
  33.5 3.3 %copy-start.3 = (bf16[64,256]{1,0:T(8,128)(2,1)S(1)}, bf16[64,256]{1,0:T(8,128)(2,1)}, u32[]{:S(2)}) copy-start(bf16[64,256]{1,0:T(8,128)(2,1)} %constant.40.clone.refs_6_) | copy-start | bytes 98308

commit v6 on v5

--- a/solution.py
+++ b/solution.py
@@ -55,7 +55,7 @@
             narrow[u] = tuple(part.astype(BF16) for part in load(u))
         return narrow[u]
 
-    grads, prods, fluxes, slopes = {}, {}, {}, {}
+    grads, prods, pairs, fluxes, slopes = {}, {}, {}, {}, {}
     for u in range(low - 2, high + 2):
         (ae, ao), (be, bo), (ce, co) = line(u - 1), line(u), line(u + 1)
         gxe, gxo = ce - ae, co - ao
@@ -66,7 +66,10 @@
         prods[u] = (gxe * gxe, gxo * gxo, gxe * gze, gxo * gzo, gze * gze, gzo * gzo)
         v = u - 1
         if v - 1 in prods:
-            sums = [a + b + c for a, b, c in zip(prods[v - 1], prods[v], prods[v + 1])]
+            first = v - v % 2
+            if first not in pairs:
+                pairs[first] = [a + b for a, b in zip(prods[first], prods[first + 1])]
+            sums = [a + b for a, b in zip(pairs[first], prods[v - 1 if v == first else v + 1])]
             boxes = []
             for even, odd in zip(sums[0::2], sums[1::2]):
                 both = even + odd

time: 39.3 us -> 39 us (level)
  no operation moved by 1% of the time
where the time goes in v6:
time: 39 us; the launch traced here: 38.8 us
  starting transfers between devices  14.3 us (37%)
  waiting for transfers between devices  11.8 us (30%)
  Pallas kernels  10.4 us (27%)
  local copies, waits for them, and re-layouts  2.05 us (5%)
    ppermute x4, starting transfers between devices, swapped(): pieces.append(lax.ppermute(radon_op, ('parts', 'xline'), pairs))  6.75 us
    pallas_call x2, Pallas kernels, swapped(): pl.pallas_call(functools.partial(late_kernel, i), out_shape=jax.ShapeDtyp...  6.27 us
    ppermute x2, waiting for transfers between devices, swapped(): halos.append(lax.ppermute(sent, 'xline', cross))  5.57 us
    ppermute x2, starting transfers between devices, swapped(): halos.append(lax.ppermute(sent, 'xline', cross))  5.55 us
    ppermute x4, waiting for transfers between devices, swapped(): pieces.append(lax.ppermute(radon_op, ('parts', 'xline'), pairs))  3.19 us
    ppermute x1, waiting for transfers between devices, swapped(): theirs = lax.ppermute(mine, ('parts', 'xline'), pairs)  3.03 us
    pallas_call x1, Pallas kernels, swapped(): pl.pallas_call(functools.partial(radon_kernel, near, apart, planes), out_...  2.27 us
    pallas_call x1, Pallas kernels, swapped(): pl.pallas_call(early_kernel, out_shape=jax.ShapeDtypeStruct((share, lines...  1.81 us
  transfers between devices with their start and end apart: 11, of which 4 were waited for; matrix products, arithmetic and copies ran while one was open for 3% of the time, Pallas kernels for 21%

profile of v6, /device:TPU:6, one launch (start us, length us, event | category | flops | bytes accessed | tf_op | source)
XLA Modules:
  0.0 38.8 jit_solution(13961244898017890298)
XLA Ops:
  0.0 1.6 %collective-permute-start.4 = (bf16[2,2,96,96]{3,2,1,0:T(8,128)(2,1)}, bf16[2,2,96,96]{3,2,1,0:T(8,128)(2,1)S(1)}, u32[]{:S(2)}, u32[]{:S(2)}) collective-permute-start(bf16[2,2,96,96]{3,2,1,0:T(8,128)(2,1)} %param.8), channel_id=1, source_target_pairs={{0,4},{1,5},{2,6},{3,7},{4,0},{5,1},{6,2},{7,3},{8,12},{9,13},{10,... | collective-permute-start | bytes 221192 | tf_op jit(solution)/shard_map/ppermute | solution.py:261
  1.6 0.4 %collective-permute-start.5 = (bf16[2,2,96,96]{3,2,1,0:T(8,128)(2,1)}, bf16[2,2,96,96]{3,2,1,0:T(8,128)(2,1)S(1)}, u32[]{:S(2)}, u32[]{:S(2)}) collective-permute-start(bf16[2,2,96,96]{3,2,1,0:T(8,128)(2,1)} %param.8), channel_id=1, source_target_pairs={{0,2},{1,3},{2,0},{3,1},{4,6},{5,7},{6,4},{7,5},{8,10},{9,11},{10,... | collective-permute-start | bytes 221192 | tf_op jit(solution)/shard_map/ppermute | solution.py:261
  2.0 3.6 %collective-permute-start.6 = (bf16[2,2,96,96]{3,2,1,0:T(8,128)(2,1)}, bf16[2,2,96,96]{3,2,1,0:T(8,128)(2,1)S(1)}, u32[]{:S(2)}, u32[]{:S(2)}) collective-permute-start(bf16[2,2,96,96]{3,2,1,0:T(8,128)(2,1)} %param.8), channel_id=1, source_target_pairs={{0,8},{1,9},{2,10},{3,11},{4,12},{5,13},{6,14},{7,15},{8,0},{9,1},... | collective-permute-start | bytes 221192 | tf_op jit(solution)/shard_map/ppermute | solution.py:261
  5.6 1.2 %collective-permute-start.7 = (bf16[2,2,96,96]{3,2,1,0:T(8,128)(2,1)}, bf16[2,2,96,96]{3,2,1,0:T(8,128)(2,1)S(1)}, u32[]{:S(2)}, u32[]{:S(2)}) collective-permute-start(bf16[2,2,96,96]{3,2,1,0:T(8,128)(2,1)} %param.8), channel_id=1, source_target_pairs={{0,10},{1,11},{2,8},{3,9},{4,14},{5,15},{6,12},{7,13},{8,2},{9,3},... | collective-permute-start | bytes 221192 | tf_op jit(solution)/shard_map/ppermute | solution.py:261
  6.8 1.2 %constant_dynamic-slice_fusion = (bf16[1,6,96,256]{3,2,1,0:T(8,128)(2,1)S(1)}, bf16[1,6,96,256]{3,2,1,0:T(8,128)(2,1)S(1)}) fusion(bf16[2,6,96,256]{3,2,1,0:T(8,128)(2,1)} %own_ref.5, s32[]{:T(128)S(6)} %select_n.32, s32[]{:T(128)S(6)} %select_n.31), kind=kLoop, calls=%fused_computation.2 | loop fusion | bytes 1179656 | tf_op jit(solution)/shard_map/dynamic_slice | solution.py:268
  7.9 0.0 copy-start.2
  8.0 0.0 copy-done
  8.0 0.6 %copy-done.1 = f32[2]{0:T(128)S(1)} copy-done((f32[2]{0:T(128)S(1)}, f32[2]{0:T(128)}, u32[]{:S(2)}) %copy-start.1) | copy-done | bytes 32
  8.6 0.3 copy-done.2
  8.9 1.8 %early.1.first_ref = f32[1,6,96,256]{3,2,1,0:T(8,128)S(1)} custom-call(f32[2]{0:T(128)S(1)} %copy-done.1, bf16[2,6,96,256]{3,2,1,0:T(8,128)(2,1)S(1)} %copy-done, bf16[2,6,96,256]{3,2,1,0:T(8,128)(2,1)S(1)} %collective-permute-done.1.mate_ref, bf16[256,256]{1,0:T(8,128)(2,1)S(1)} %copy-done.2), custom_call_target="tpu_custom_call" | custom-call | flops 3000000000 | tf_op jit(solution)/shard_map/early/pallas_call | solution.py:286
  10.7 0.1 collective-permute-start.3
  10.8 1.5 %collective-permute-done.6 = bf16[2,2,96,96]{3,2,1,0:T(8,128)(2,1)S(1)} collective-permute-done((bf16[2,2,96,96]{3,2,1,0:T(8,128)(2,1)}, bf16[2,2,96,96]{3,2,1,0:T(8,128)(2,1)S(1)}, u32[]{:S(2)}, u32[]{:S(2)}) %collective-permute-start.6) | collective-permute-done | bytes 73760 | tf_op jit(solution)/shard_map/ppermute | solution.py:261
  12.3 1.7 %collective-permute-done.7 = bf16[2,2,96,96]{3,2,1,0:T(8,128)(2,1)S(1)} collective-permute-done((bf16[2,2,96,96]{3,2,1,0:T(8,128)(2,1)}, bf16[2,2,96,96]{3,2,1,0:T(8,128)(2,1)S(1)}, u32[]{:S(2)}, u32[]{:S(2)}) %collective-permute-start.7) | collective-permute-done | bytes 73760 | tf_op jit(solution)/shard_map/ppermute | solution.py:261
  14.0 0.1 pad_maximum_fusion.refs_2_
  14.1 1.8 %collective-permute-start.8 = (bf16[4,2,2,96,96]{4,3,2,1,0:T(8,128)(2,1)S(1)}, bf16[4,2,2,96,96]{4,3,2,1,0:T(8,128)(2,1)S(1)}, u32[]{:S(2)}, u32[]{:S(2)}) collective-permute-start(bf16[4,2,2,96,96]{4,3,2,1,0:T(8,128)(2,1)S(1)} %pad_maximum_fusion.refs_2_), channel_id=1, source_target_pairs={{0,16},{1,17},{2,18},{3,19},{4,20},{5,21},{6,22},{7,23},{8,24},{9,... | collective-permute-start | bytes 884744 | tf_op jit(solution)/shard_map/ppermute | solution.py:273
  15.9 1.9 %collective-permute-start = (bf16[1,6,96,256]{3,2,1,0:T(8,128)(2,1)S(1)}, bf16[1,6,96,256]{3,2,1,0:T(8,128)(2,1)S(1)}, u32[]{:S(2)}, u32[]{:S(2)}) collective-permute-start(bf16[1,6,96,256]{3,2,1,0:T(8,128)(2,1)S(1)} %get-tuple-element.6), channel_id=1, source_target_pairs={{1,2},{3,4},{5,6},{7,8},{9,10},{11,12},{13,14},{2,1},{4,3},{6,5},{... | collective-permute-start | bytes 884744 | tf_op jit(solution)/shard_map/ppermute | solution.py:269
  17.8 3.6 %collective-permute-start.2 = (bf16[1,6,96,256]{3,2,1,0:T(8,128)(2,1)S(1)}, bf16[1,6,96,256]{3,2,1,0:T(8,128)(2,1)S(1)}, u32[]{:S(2)}, u32[]{:S(2)}) collective-permute-start(bf16[1,6,96,256]{3,2,1,0:T(8,128)(2,1)S(1)} %get-tuple-element.5), channel_id=1, source_target_pairs={{1,2},{3,4},{5,6},{7,8},{9,10},{11,12},{13,14},{2,1},{4,3},{6,5},{... | collective-permute-start | bytes 884744 | tf_op jit(solution)/shard_map/ppermute | solution.py:269
  21.4 0.2 collective-permute-start.9
  21.6 3.0 %collective-permute-done.8.refs_3_ = bf16[4,2,2,96,96]{4,3,2,1,0:T(8,128)(2,1)S(1)} collective-permute-done((bf16[4,2,2,96,96]{4,3,2,1,0:T(8,128)(2,1)S(1)}, bf16[4,2,2,96,96]{4,3,2,1,0:T(8,128)(2,1)S(1)}, u32[]{:S(2)}, u32[]{:S(2)}) %collective-permute-start.8) | collective-permute-done | bytes 294944 | tf_op jit(solution)/shard_map/ppermute | solution.py:273
  24.6 5.6 %collective-permute-done.halo_ref = bf16[1,6,96,256]{3,2,1,0:T(8,128)(2,1)S(1)} collective-permute-done((bf16[1,6,96,256]{3,2,1,0:T(8,128)(2,1)S(1)}, bf16[1,6,96,256]{3,2,1,0:T(8,128)(2,1)S(1)}, u32[]{:S(2)}, u32[]{:S(2)}) %collective-permute-start) | collective-permute-done | bytes 294944 | tf_op jit(solution)/shard_map/ppermute | solution.py:269
  30.2 3.1 %shard_map.64.refs_0_ = bf16[6,64,96]{2,1,0:T(8,128)(2,1)S(1)} custom-call(f32[2]{0:T(128)S(1)} %copy-done.1, bf16[1,6,96,256]{3,2,1,0:T(8,128)(2,1)S(1)} %collective-permute-done.halo_ref, bf16[2,6,96,256]{3,2,1,0:T(8,128)(2,1)S(1)} %copy-done, f32[1,6,96,256]{3,2,1,0:T(8,128)S(1)} %early.1.first_ref, bf16[256,256]{1,0:T(8,128)(2,1)S(1)} %copy-done.2, ...), custom_call_target="tpu_custom_call" | custom-call | flops 3000000000 | tf_op jit(solution)/shard_map/pallas_call | solution.py:300
  33.4 0.0 copy-start.3
  33.4 3.1 %shard_map.65.refs_1_ = bf16[6,64,96]{2,1,0:T(8,128)(2,1)S(1)} custom-call(f32[2]{0:T(128)S(1)} %copy-done.1, bf16[1,6,96,256]{3,2,1,0:T(8,128)(2,1)S(1)} %collective-permute-done.2.halo_ref, bf16[2,6,96,256]{3,2,1,0:T(8,128)(2,1)S(1)} %copy-done, f32[1,6,96,256]{3,2,1,0:T(8,128)S(1)} %collective-permute-done.3.first_ref, bf16[256,256]{1,0:T(8,128)(2,1)S(1)} %copy-done.2, ...), custom_call_target="tpu_custom_call" | custom-call | flops 3000000000 | tf_op jit(solution)/shard_map/pallas_call | solution.py:300
  36.6 2.3 %radon.1 = bf16[2,6,96,256]{3,2,1,0:T(8,128)(2,1)} custom-call(bf16[6,64,96]{2,1,0:T(8,128)(2,1)S(1)} %shard_map.64.refs_0_, bf16[6,64,96]{2,1,0:T(8,128)(2,1)S(1)} %shard_map.65.refs_1_, bf16[4,2,2,96,96]{4,3,2,1,0:T(8,128)(2,1)S(1)} %pad_maximum_fusion.refs_2_, bf16[4,2,2,96,96]{4,3,2,1,0:T(8,128)(2,1)S(1)} %collective-permute-done.8.refs_3_, ...), custom_call_target="tpu_custom_call" | custom-call | flops 4000000000 | tf_op jit(solution)/shard_map/radon/pallas_call | solution.py:315
  (17 shorter events, 0.1 us)
Async XLA Ops:
  0.0 8.0 %collective-permute-start.1 = (bf16[2,6,96,256]{3,2,1,0:T(8,128)(2,1)}, bf16[2,6,96,256]{3,2,1,0:T(8,128)(2,1)S(1)}, u32[]{:S(2)}, u32[]{:S(2)}) collective-permute-start(bf16[2,6,96,256]{3,2,1,0:T(8,128)(2,1)} %own_ref.5), channel_id=1, source_target_pairs={{0,1},{1,0},{2,3},{3,2},{4,5},{5,4},{6,7},{7,6},{8,9},{9,8},{10,11... | collective-permute-start | bytes 1769480 | tf_op jit(solution)/shard_map/ppermute | solution.py:250
  0.0 7.9 %collective-permute-start.4 = (bf16[2,2,96,96]{3,2,1,0:T(8,128)(2,1)}, bf16[2,2,96,96]{3,2,1,0:T(8,128)(2,1)S(1)}, u32[]{:S(2)}, u32[]{:S(2)}) collective-permute-start(bf16[2,2,96,96]{3,2,1,0:T(8,128)(2,1)} %param.8), channel_id=1, source_target_pairs={{0,4},{1,5},{2,6},{3,7},{4,0},{5,1},{6,2},{7,3},{8,12},{9,13},{10,... | collective-permute-start | bytes 221192 | tf_op jit(solution)/shard_map/ppermute | solution.py:261
  1.6 9.2 %collective-permute-start.5 = (bf16[2,2,96,96]{3,2,1,0:T(8,128)(2,1)}, bf16[2,2,96,96]{3,2,1,0:T(8,128)(2,1)S(1)}, u32[]{:S(2)}, u32[]{:S(2)}) collective-permute-start(bf16[2,2,96,96]{3,2,1,0:T(8,128)(2,1)} %param.8), channel_id=1, source_target_pairs={{0,2},{1,3},{2,0},{3,1},{4,6},{5,7},{6,4},{7,5},{8,10},{9,11},{10,... | collective-permute-start | bytes 221192 | tf_op jit(solution)/shard_map/ppermute | solution.py:261
  2.0 10.3 %collective-permute-start.6 = (bf16[2,2,96,96]{3,2,1,0:T(8,128)(2,1)}, bf16[2,2,96,96]{3,2,1,0:T(8,128)(2,1)S(1)}, u32[]{:S(2)}, u32[]{:S(2)}) collective-permute-start(bf16[2,2,96,96]{3,2,1,0:T(8,128)(2,1)} %param.8), channel_id=1, source_target_pairs={{0,8},{1,9},{2,10},{3,11},{4,12},{5,13},{6,14},{7,15},{8,0},{9,1},... | collective-permute-start | bytes 221192 | tf_op jit(solution)/shard_map/ppermute | solution.py:261
  5.6 8.4 %collective-permute-start.7 = (bf16[2,2,96,96]{3,2,1,0:T(8,128)(2,1)}, bf16[2,2,96,96]{3,2,1,0:T(8,128)(2,1)S(1)}, u32[]{:S(2)}, u32[]{:S(2)}) collective-permute-start(bf16[2,2,96,96]{3,2,1,0:T(8,128)(2,1)} %param.8), channel_id=1, source_target_pairs={{0,10},{1,11},{2,8},{3,9},{4,14},{5,15},{6,12},{7,13},{8,2},{9,3},... | collective-permute-start | bytes 221192 | tf_op jit(solution)/shard_map/ppermute | solution.py:261
  6.8 1.2 %copy-start.5 = (bf16[2,2,96,96]{3,2,1,0:T(8,128)(2,1)S(1)}, bf16[2,2,96,96]{3,2,1,0:T(8,128)(2,1)}, u32[]{:S(2)}) copy-start(bf16[2,2,96,96]{3,2,1,0:T(8,128)(2,1)} %param.8) | copy-start | bytes 221188
  6.8 1.3 %copy-start = (bf16[2,6,96,256]{3,2,1,0:T(8,128)(2,1)S(1)}, bf16[2,6,96,256]{3,2,1,0:T(8,128)(2,1)}, u32[]{:S(2)}) copy-start(bf16[2,6,96,256]{3,2,1,0:T(8,128)(2,1)} %own_ref.5) | copy-start | bytes 1769476
  7.9 0.7 %copy-start.1 = (f32[2]{0:T(128)S(1)}, f32[2]{0:T(128)}, u32[]{:S(2)}) copy-start(f32[2]{0:T(128)} %tau_ref.5) | copy-start | bytes 28
  7.9 0.9 %copy-start.2 = (bf16[256,256]{1,0:T(8,128)(2,1)S(1)}, bf16[256,256]{1,0:T(8,128)(2,1)}, u32[]{:S(2)}) copy-start(bf16[256,256]{1,0:T(8,128)(2,1)} %constant.38.clone.split_ref) | copy-start | bytes 393220
  10.7 22.7 %collective-permute-start.3 = (f32[1,6,96,256]{3,2,1,0:T(8,128)S(1)}, f32[1,6,96,256]{3,2,1,0:T(8,128)S(1)}, u32[]{:S(2)}, u32[]{:S(2)}) collective-permute-start(f32[1,6,96,256]{3,2,1,0:T(8,128)S(1)} %early.1.first_ref), channel_id=1, source_target_pairs={{0,1},{1,0},{2,3},{3,2},{4,5},{5,4},{6,7},{7,6},{8,9},{9,8},{10,11... | collective-permute-start | bytes 1769480 | tf_op jit(solution)/shard_map/ppermute | solution.py:250
  14.0 16.2 %copy-start.4 = (bf16[64,256]{1,0:T(8,128)(2,1)S(1)}, bf16[64,256]{1,0:T(8,128)(2,1)}, u32[]{:S(2)}) copy-start(bf16[64,256]{1,0:T(8,128)(2,1)} %constant.39.clone.table_ref) | copy-start | bytes 98308
  14.1 10.6 %collective-permute-start.8 = (bf16[4,2,2,96,96]{4,3,2,1,0:T(8,128)(2,1)S(1)}, bf16[4,2,2,96,96]{4,3,2,1,0:T(8,128)(2,1)S(1)}, u32[]{:S(2)}, u32[]{:S(2)}) collective-permute-start(bf16[4,2,2,96,96]{4,3,2,1,0:T(8,128)(2,1)S(1)} %pad_maximum_fusion.refs_2_), channel_id=1, source_target_pairs={{0,16},{1,17},{2,18},{3,19},{4,20},{5,21},{6,22},{7,23},{8,24},{9,... | collective-permute-start | bytes 884744 | tf_op jit(solution)/shard_map/ppermute | solution.py:273
  15.9 14.3 %collective-permute-start = (bf16[1,6,96,256]{3,2,1,0:T(8,128)(2,1)S(1)}, bf16[1,6,96,256]{3,2,1,0:T(8,128)(2,1)S(1)}, u32[]{:S(2)}, u32[]{:S(2)}) collective-permute-start(bf16[1,6,96,256]{3,2,1,0:T(8,128)(2,1)S(1)} %get-tuple-element.6), channel_id=1, source_target_pairs={{1,2},{3,4},{5,6},{7,8},{9,10},{11,12},{13,14},{2,1},{4,3},{6,5},{... | collective-permute-start | bytes 884744 | tf_op jit(solution)/shard_map/ppermute | solution.py:269
  17.8 15.6 %collective-permute-start.2 = (bf16[1,6,96,256]{3,2,1,0:T(8,128)(2,1)S(1)}, bf16[1,6,96,256]{3,2,1,0:T(8,128)(2,1)S(1)}, u32[]{:S(2)}, u32[]{:S(2)}) collective-permute-start(bf16[1,6,96,256]{3,2,1,0:T(8,128)(2,1)S(1)} %get-tuple-element.5), channel_id=1, source_target_pairs={{1,2},{3,4},{5,6},{7,8},{9,10},{11,12},{13,14},{2,1},{4,3},{6,5},{... | collective-permute-start | bytes 884744 | tf_op jit(solution)/shard_map/ppermute | solution.py:269
  21.4 15.1 %collective-permute-start.9 = (bf16[4,2,2,96,96]{4,3,2,1,0:T(8,128)(2,1)S(1)}, bf16[4,2,2,96,96]{4,3,2,1,0:T(8,128)(2,1)S(1)}, u32[]{:S(2)}, u32[]{:S(2)}) collective-permute-start(bf16[4,2,2,96,96]{4,3,2,1,0:T(8,128)(2,1)S(1)} %pad_maximum_fusion.refs_2_), channel_id=1, source_target_pairs={{0,1},{1,0},{2,3},{3,2},{4,5},{5,4},{6,7},{7,6},{8,9},{9,8},{10,11... | collective-permute-start | bytes 884744 | tf_op jit(solution)/shard_map/ppermute | solution.py:250
  24.6 11.9 %collective-permute-start.10 = (bf16[4,2,2,96,96]{4,3,2,1,0:T(8,128)(2,1)S(1)}, bf16[4,2,2,96,96]{4,3,2,1,0:T(8,128)(2,1)S(1)}, u32[]{:S(2)}, u32[]{:S(2)}) collective-permute-start(bf16[4,2,2,96,96]{4,3,2,1,0:T(8,128)(2,1)S(1)} %collective-permute-done.8.refs_3_), channel_id=1, source_target_pairs={{0,1},{1,0},{2,3},{3,2},{4,5},{5,4},{6,7},{7,6},{8,9},{9,8},{10,11... | collective-permute-start | bytes 884744 | tf_op jit(solution)/shard_map/ppermute | solution.py:250
  33.4 3.2 %copy-start.3 = (bf16[64,256]{1,0:T(8,128)(2,1)S(1)}, bf16[64,256]{1,0:T(8,128)(2,1)}, u32[]{:S(2)}) copy-start(bf16[64,256]{1,0:T(8,128)(2,1)} %constant.40.clone.refs_6_) | copy-start | bytes 98308
